TPU v7x, 32 devices: a whole 2x2x4 slice. The times are simulated.
32 devices in a mesh: groups: 2 (over y), tm: 16 (over z, x, core).
Axes of the slice: x: 2, y: 2, z: 4, core: 2. Of those that a mesh axis runs over, the one named last changes fastest.
Arguments:
- voltages: bfloat16 [256, 256, 2, 188], P(None, ('groups', 'tm')), parts along dimension 1, as said below
- off_starts: int32 [16], P('groups'), parts along dimension 0, may hold values from 0 to 124, as said below
- pointing: int32 [36], replicated, may hold values from 0 to 2047, as said below
- patterns: bfloat16 [2, 188, 2048], P(None, None, 'tm'), may hold values from -0.3125 to 0.3125
Outputs:
- beam_weights: bfloat16 [512, 2, 6768], P(('groups', 'tm')), parts along dimension 0
- beam_maps: float32 [512, 36, 2048], P('groups', None, 'tm'), parts along dimension 0
There are 2 independent parts, one for each index of `groups`. A program takes and returns all parts, laid end to end along the dimension named above; an argument that names none is the same for every part. Nothing has to cross between parts.
Inputs may be any that keep to these rules, and one draw needn't show every extreme that they name: Complex port voltages: thermal noise whose power differs between ports and grows along time, plus sky signals common to the ports. `off_starts`: each of the 8 off-source ranges covers 4 samples from this start; ranges may intersect. `pointing`: several beams may point at the same pixel.
All inputs are finite; a program needn't handle non-finite values.
Results may differ from a plain program's by a relative error of at most 0.0034.
Values may be sent and summed in bfloat16 or wider, within the bound.
No kernel may reach another device: no remote copies, remote signals or barrier semaphores. Data moves between devices by JAX's collectives and lax.ppermute only.
A program may use at most 64 MiB of HBM per device.

v0:
```python
import jax
import jax.numpy as jnp
from jax import lax
from jax.sharding import PartitionSpec as P

ITERS = 20


highest = lax.Precision.HIGHEST


def off_flags(moments, starts, range_len):
    shape_now = moments.shape
    flat_moments = moments.reshape(-1)
    inside = (flat_moments[None, :] >= starts[:, None]) & (
        flat_moments[None, :] < starts[:, None] + range_len
    )
    return jnp.any(inside, axis=0).reshape(shape_now)


def split_gram(products, port_count):
    corr_real = products[..., :port_count, :port_count] + products[..., port_count:, port_count:]
    corr_imag = products[..., port_count:, :port_count] - products[..., :port_count, port_count:]
    return jnp.stack([corr_real, corr_imag], axis=-3)


def beam_power(weights, patterns):
    port_count = weights.shape[3]
    real_rows = jnp.concatenate([weights[:, 0], weights[:, 1]], axis=-1)
    imag_rows = jnp.concatenate([-weights[:, 1], weights[:, 0]], axis=-1)
    rows_all = jnp.stack([real_rows, imag_rows], axis=2).reshape(-1, 2 * port_count)
    response = jnp.dot(
        rows_all, patterns.reshape(2 * port_count, -1), preferred_element_type=jnp.float32
    )
    response = response.reshape(weights.shape[0], weights.shape[2], 2, -1)
    return response[:, :, 0] * response[:, :, 0] + response[:, :, 1] * response[:, :, 1]


def on_device(voltages, off_starts, pointing, patterns):
    devices = lax.axis_size("tm")
    position = lax.axis_index("tm")
    channels = voltages.shape[0]
    samples_dev = voltages.shape[1]
    ports = voltages.shape[3]
    beams = pointing.shape[0]
    per_dev = channels // devices
    double_width = 2 * ports
    total_time = samples_dev * devices
    off_span = max(4, total_time // 32)
    every_moment = jnp.arange(total_time, dtype=jnp.int32)
    off_count = jnp.sum(off_flags(every_moment, off_starts, off_span).astype(jnp.float32))
    pixels = patterns.shape[2]
    pixel_ids = position * pixels + jnp.arange(pixels, dtype=jnp.int32)
    selector = (pixel_ids[:, None] == pointing[None, :]).astype(jnp.bfloat16)
    steer_local = jnp.einsum("rpx,xb->rpb", patterns, selector, preferred_element_type=jnp.float32)
    steering = lax.psum(steer_local, "tm")
    blocks = voltages.reshape(devices, per_dev, samples_dev, double_width)
    arrived = lax.all_to_all(blocks, "tm", split_axis=0, concat_axis=0, tiled=True)
    moments = (
        jnp.arange(devices, dtype=jnp.int32)[:, None] * samples_dev
        + jnp.arange(samples_dev, dtype=jnp.int32)[None, :]
    )
    is_off = off_flags(moments, off_starts, off_span)
    on_source = jnp.where(is_off[:, None, :, None], jnp.zeros_like(arrived), arrived)
    products = jnp.einsum("nksi,nksj->kij", on_source, arrived, preferred_element_type=jnp.float32)
    corr_mine = split_gram(products, ports)
    squared = jnp.square(arrived.astype(jnp.float32))
    powers = jnp.sum(jnp.where(is_off[:, None, :, None], squared, jnp.float32(0.0)), axis=(0, 2))
    noise_total = powers[:, :ports] + powers[:, ports:]
    noise_power = noise_total / off_count + 1e-06
    scales = 1.0 / jnp.sqrt(noise_power)
    white_real = corr_mine[:, 0] * scales[:, :, None] * scales[:, None, :]
    white_imag = corr_mine[:, 1] * scales[:, :, None] * scales[:, None, :]
    steer_real = steering[0][None]
    steer_imag = steering[1][None]

    def apply_white(matrix, vector):
        return jnp.einsum("kij,kjb->kib", matrix, vector, precision=highest)

    def power_turn(counter, state_pair):
        beam_real, beam_imag = state_pair
        conj_real = steer_real * beam_real + steer_imag * beam_imag
        conj_imag = steer_real * beam_imag - steer_imag * beam_real
        mixed_real = apply_white(white_real, conj_real) - apply_white(white_imag, conj_imag)
        mixed_imag = apply_white(white_real, conj_imag) + apply_white(white_imag, conj_real)
        image_real = steer_real * mixed_real - steer_imag * mixed_imag
        image_imag = steer_real * mixed_imag + steer_imag * mixed_real
        mean_square = (
            jnp.sum(image_real * image_real, axis=1) + jnp.sum(image_imag * image_imag, axis=1)
        ) / (2 * ports)
        factor = 1.0 / jnp.sqrt(mean_square + 1e-06)
        return (image_real * factor[:, None, :], image_imag * factor[:, None, :])

    initial = (
        jnp.broadcast_to(steer_real, (per_dev, ports, beams)),
        jnp.broadcast_to(steer_imag, (per_dev, ports, beams)),
    )
    beam_real, beam_imag = lax.fori_loop(0, ITERS, power_turn, initial)
    weight_real = beam_real * scales[:, :, None]
    weight_imag = beam_imag * scales[:, :, None]
    weight_pair = (
        jnp.stack([weight_real, weight_imag], axis=1).transpose(0, 1, 3, 2).astype(jnp.bfloat16)
    )
    flat_pair = weight_pair.reshape(per_dev, 2, beams * ports)
    collected = lax.all_gather(flat_pair, "tm", axis=0, tiled=True)
    all_weights = collected.reshape(channels, 2, beams, ports)
    maps_out = beam_power(all_weights, patterns)
    return (flat_pair, maps_out)


def solution(mesh):
    in_specs = (P(None, ("groups", "tm"), None, None), P("groups"), P(), P(None, None, "tm"))
    out_specs = (P(("groups", "tm"), None, None), P("groups", None, "tm"))
    return jax.shard_map(
        on_device, mesh=mesh, in_specs=in_specs, out_specs=out_specs, check_vma=False
    )
```

profile of v0, /device:TPU:0, one launch (start us, length us, event | category | flops | bytes accessed | tf_op | source)
XLA Modules:
  0.0 552.6 jit_solution(12295495400840213857)
XLA Ops:
  7.2 7.9 %copy.28 = bf16[256,8,2,188]{3,2,1,0:T(2,128)(2,1)S(1)} copy(bf16[256,8,2,188]{0,2,3,1:T(2,128)(2,1)} %param.6) | data formatting | bytes 3080192 | tf_op args[0]
  17.1 7.4 %all-to-all-start = ((bf16[16,16,8,376]{3,2,1,0:T(8,128)(2,1)}), bf16[16,16,8,376]{3,2,1,0:T(8,128)(2,1)S(1)}, u32[]{:S(2)}, u32[]{:S(2)}) async-start(bf16[16,16,8,376]{3,2,1,0:T(8,128)(2,1)} %reshape.61), calls=%async_computation | async-start | bytes 3145728 | tf_op jit(solution)/shard_map/all_to_all | solution.py:58
  25.1 81.9 %psum.7 = f32[2,188,36]{1,2,0:T(8,128)S(1)} all-reduce(f32[2,188,36]{1,2,0:T(8,128)S(1)} %convolution_bitcast_fusion.1), channel_id=1, replica_groups=mesh['groups'=2,'tm'=16] {'tm'}, use_global_device_ids=true, to_apply=%region_0.0 | all-reduce | flops 13536 | bytes 108288 | tf_op jit(solution)/shard_map/psum | solution.py:56
  110.7 3.6 fusion.11
  116.0 321.7 %while.12 = (s32[]{:T(128)}, f32[16,188,36]{1,2,0:T(8,128)}, f32[16,188,36]{1,2,0:T(8,128)}, f32[1,188,36]{1,2,0:T(8,128)S(1)}, f32[1,188,36]{1,2,0:T(8,128)S(1)...) while((s32[]{:T(128)}, f32[16,188,36]{1,2,0:T(8,128)}, f32[16,188,36]{1,2,0:T(8,128)}, ...), condition=%wide.region_8.9_spmd, body=%wide.region_5.8_spmd.sunk | while | flops 980656704 | bytes 30075944 | solution.py:98
  116.0 5.4 fusion.50
  127.6 3.2 multiply_reduce_fusion.3
  132.1 5.4 fusion.50
  148.2 5.4 fusion.50
  164.3 5.4 fusion.50
  180.4 5.4 fusion.50
  196.4 5.4 fusion.50
  212.5 5.4 fusion.50
  228.6 5.4 fusion.50
  244.7 5.4 fusion.50
  260.8 5.4 fusion.50
  276.9 5.4 fusion.50
  292.9 5.4 fusion.50
  309.0 5.4 fusion.50
  325.1 5.4 fusion.50
  341.2 5.4 fusion.50
  357.3 5.4 fusion.50
  373.4 5.4 fusion.50
  389.5 5.4 fusion.50
  405.5 5.4 fusion.50
  421.6 5.4 fusion.50
  442.7 60.5 %all-gather.2.cloned.1.call-done = bf16[256,2,6768]{2,0,1:T(8,128)(2,1)} async-done(((bf16[16,2,6768]{2,0,1:T(8,128)(2,1)}), bf16[256,2,6768]{2,0,1:T(8,128)(2,1)}) %all-gather.2.cloned.1.call-update) | async-done | bytes 6930448 | tf_op jit(solution)/shard_map/all_gather | solution.py:105
  503.3 10.1 %copy.29 = bf16[256,2,6768]{0,2,1:T(8,128)(2,1)} copy(bf16[256,2,6768]{2,0,1:T(8,128)(2,1)} %all-gather.2.cloned.1.call-done) | data formatting | bytes 13860864 | tf_op jit(solution)/shard_map/all_gather | solution.py:105
  513.4 9.9 %reshape.63 = bf16[256,2,36,188]{0,3,2,1:T(8,128)(2,1)} reshape(bf16[256,2,6768]{0,2,1:T(8,128)(2,1)} %copy.29) | data formatting | bytes 13860864 | tf_op jit(solution)/shard_map/reshape | solution.py:106
  523.3 3.7 slice_bitcast_fusion
  528.6 7.0 %maximum_bitcast_fusion = (bf16[256,36,1,376]{0,3,2,1:T(8,128)(2,1)}, bf16[256,36,1,376]{0,3,2,1:T(8,128)(2,1)}) fusion(bf16[256,36,188]{0,2,1:T(8,128)(2,1)S(1)} %get-tuple-element.71, bf16[256,36,188]{0,2,1:T(8,128)(2,1)S(1)} %get-tuple-element.72, bf16[256,36,188]{0,2,1:T(8,128)(2,1)S(1)} %fusion.32), kind=kLoop, calls=%fused_computation.19 | loop fusion | flops 27721728 | bytes 24256512 | tf_op jit(solution)/shard_map/stack | solution.py:31
  535.6 7.2 %fusion.4 = f32[256,36,2,128]{3,0,2,1:T(8,128)S(1)} fusion(bf16[256,36,1,376]{0,3,2,1:T(8,128)(2,1)} %get-tuple-element.74, bf16[256,36,1,376]{0,3,2,1:T(8,128)(2,1)} %get-tuple-element.73, bf16[376,128,1,1]{1,0,2,3:T(8,128)(2,1)S(1)} %reshape.67), kind=kOutput, calls=%fused_computation.15 | convolution fusion | flops 1781121024 | bytes 23394304 | tf_op jit(solution)/shard_map/dot_general | solution.py:32
  (254 shorter events, 226.4 us)
Async XLA Ops:
  15.1 9.6 %copy-start.6 = (s32[8]{0:T(128)S(1)}, s32[8]{0:T(128)}, u32[]{:S(2)}) copy-start(s32[8]{0:T(128)} %param.7) | copy-start | bytes 100
  15.1 9.8 %copy-start.4 = (bf16[2,188,128]{2,0,1:T(2,128)(2,1)S(1)}, bf16[2,188,128]{2,0,1:T(2,128)(2,1)}, u32[]{:S(2)}) copy-start(bf16[2,188,128]{2,0,1:T(2,128)(2,1)} %param.9) | copy-start | bytes 288772
  15.1 9.8 %copy-start.5 = (s32[36]{0:T(128)S(1)}, s32[36]{0:T(128)}, u32[]{:S(2)}) copy-start(s32[36]{0:T(128)} %param.8) | copy-start | bytes 436
  17.1 90.5 %all-to-all-start = ((bf16[16,16,8,376]{3,2,1,0:T(8,128)(2,1)}), bf16[16,16,8,376]{3,2,1,0:T(8,128)(2,1)S(1)}, u32[]{:S(2)}, u32[]{:S(2)}) async-start(bf16[16,16,8,376]{3,2,1,0:T(8,128)(2,1)} %reshape.61), calls=%async_computation | async-start | bytes 3145728 | tf_op jit(solution)/shard_map/all_to_all | solution.py:58
  24.5 478.8 %all-gather.2.cloned.1.call-start = ((), (), s32[]{:S(2)}) async-start(), calls=%async_computation.1 | async-start | bytes 7380992 | tf_op jit(solution)/shard_map/all_gather | solution.py:105
  116.0 5.4 copy-start.2
  132.1 5.4 copy-start.1
  132.1 5.4 copy-start.2
  148.2 5.4 copy-start.1
  148.2 5.4 copy-start.2
  164.3 5.4 copy-start.1
  164.3 5.4 copy-start.2
  180.4 5.4 copy-start.1
  180.4 5.4 copy-start.2
  196.4 5.4 copy-start.1
  196.4 5.4 copy-start.2
  212.5 5.4 copy-start.1
  212.5 5.4 copy-start.2
  228.6 5.4 copy-start.1
  228.6 5.4 copy-start.2
  244.7 5.4 copy-start.2
  260.8 5.4 copy-start.2
  276.9 5.4 copy-start.2
  292.9 5.4 copy-start.2
  309.0 5.4 copy-start.2
  325.1 5.4 copy-start.2
  341.2 5.4 copy-start.2
  357.3 5.4 copy-start.2
  373.4 5.4 copy-start.2
  389.5 5.4 copy-start.2
  405.5 5.4 copy-start.2
  421.6 5.4 copy-start.2
  (34 other events, 137.7 us)
Sparse Core Ops, SparseCore 0:
  440.7 62.5 all-gather.1
where the time goes:
time: 553 us
  matrix products  303 us (55%)
  blocking collectives  81.9 us (15%)
  waiting for transfers between devices  60.6 us (11%)
  other arithmetic  43.2 us (8%)
  local copies, waits for them, and re-layouts  40.7 us (7%)
  between operations  14.2 us (3%)
  starting transfers between devices  7.43 us (1%)
    dot_general x80, matrix products, apply_white(): return jnp.einsum('kij,kjb->kib', matrix, vector, precision=highest)  294 us
    psum x1, blocking collectives, on_device(): steering = lax.psum(steer_local, 'tm')  81.9 us
    all_gather x1, waiting for transfers between devices, on_device(): collected = lax.all_gather(flat_pair, 'tm', axis=0, tiled=True)  60.5 us
    mul x20, other arithmetic, power_turn(): return (image_real * factor[:, None, :], image_imag * factor[:, None, :])  25.8 us
    unnamed x11, local copies, waits for them, and re-layouts  11.5 us
  transfers between devices with their start and end apart: 2, of which 1 were waited for; matrix products, arithmetic and copies ran while one was open for 1% of the time, Pallas kernels for 0%

commit v1 on v0

v1 whole, which is shorter than its diff:
```python
import functools

import jax
import jax.numpy as jnp
from jax import lax
from jax.experimental import pallas as pl
from jax.experimental.pallas import tpu as pltpu
from jax.sharding import PartitionSpec as P

ITERS = 20
LANES = 128
SUB = 8
PAIR = 4


def lane_order(real, imag, axis):
    ports = real.shape[axis]
    full = ports // LANES * LANES
    tail = ports - full
    half = LANES // 2
    assert 0 < tail <= half
    blank = list(real.shape)
    blank[axis] = half - tail
    blank = jnp.zeros(blank, real.dtype)
    cut = functools.partial(lax.slice_in_dim, axis=axis)
    return jnp.concatenate(
        [cut(real, 0, full), cut(imag, 0, full), cut(real, full, ports), blank, cut(imag, full, ports), blank],
        axis=axis,
    )


def split_lanes(block, full):
    tails = block[:, 2 * full :]
    real = jnp.concatenate([block[:, :full], tails], axis=1)
    imag = jnp.concatenate([block[:, full : 2 * full], pltpu.roll(tails, LANES // 2, 1)], axis=1)
    return real, imag


def power_kernel(
    arr_ref, on_ref, count_ref, steer_ref, pay_ref, flat_ref, volt_ref, voltt_ref, scale_ref, lhs_ref, pay_sc, *, ports, group
):
    sources, channels, samples, wide = arr_ref.shape
    beams = steer_ref.shape[0]
    rows = volt_ref.shape[1] // 2
    full = ports // LANES * LANES
    width = full + LANES
    pad = lhs_ref.shape[1] // 4
    valid = lax.broadcasted_iota(jnp.int32, (beams, width), 1) < ports

    def padded(block):
        return jnp.concatenate([block, jnp.zeros((pad - beams, width), jnp.float32)], axis=0)

    steer_real, steer_imag = split_lanes(steer_ref[...].astype(jnp.float32), full)
    steer_real = padded(jnp.where(valid, steer_real, 0.0))
    steer_imag = padded(jnp.where(valid, steer_imag, 0.0))
    energy = steer_real * steer_real + steer_imag * steer_imag
    on = on_ref[...]

    def store_pair(k, both):
        high = both.astype(jnp.bfloat16)
        low = (both - high.astype(jnp.float32)).astype(jnp.bfloat16)
        lhs_ref[k, : 2 * pad] = high
        lhs_ref[k, 2 * pad :] = low

    def halves_dot(k_lhs, rhs):
        out = jnp.dot(k_lhs, rhs, preferred_element_type=jnp.float32)
        return out[: 2 * pad] + out[2 * pad :]

    def prepare(k, carry):
        block = arr_ref[:, pl.ds(k, 1)].astype(jnp.float32).reshape(rows, wide)
        kept = block * on
        gone = block - kept
        power = jnp.sum(gone * gone, axis=0, keepdims=True)
        power_real, power_imag = split_lanes(power, full)
        noise = (power_real + power_imag) / count_ref[0, 0] + 1e-06
        real, imag = split_lanes(kept, full)
        both = jnp.concatenate([real, imag], axis=0)
        volt_ref[k] = both.astype(jnp.bfloat16)
        voltt_ref[k] = both.T.astype(jnp.bfloat16)
        scale_ref[pl.ds(k, 1)] = (1.0 / noise)[None]
        first = energy * (1.0 / jnp.sqrt(noise))
        store_pair(k, jnp.concatenate([first, jnp.zeros_like(first)], axis=0))
        return carry

    lax.fori_loop(0, channels, prepare, 0)

    def apply_corr(k):
        part = halves_dot(lhs_ref[k], voltt_ref[k])
        real, imag = part[:pad], part[pad:]
        amp_real = real[:, :rows] + imag[:, rows:]
        amp_imag = imag[:, :rows] - real[:, rows:]
        both = jnp.concatenate(
            [jnp.concatenate([amp_real, -amp_imag], axis=1), jnp.concatenate([amp_imag, amp_real], axis=1)], axis=0
        )
        high = both.astype(jnp.bfloat16)
        low = (both - high.astype(jnp.float32)).astype(jnp.bfloat16)
        out = halves_dot(jnp.concatenate([high, low], axis=0), volt_ref[k])
        real, imag = out[:pad], out[pad:]
        weight = energy * scale_ref[k]
        scaled_real = weight * real
        scaled_imag = weight * imag
        mean = jnp.sum(scaled_real * real + scaled_imag * imag, axis=1, keepdims=True) / (2 * ports)
        factor = lax.rsqrt(mean + 1e-06)
        return real, imag, scaled_real, scaled_imag, factor

    def group_body(g, carry):
        def turn(step, inner):
            for j in range(group):
                k = g * group + j
                _, _, scaled_real, scaled_imag, factor = apply_corr(k)
                store_pair(k, jnp.concatenate([scaled_real * factor, scaled_imag * factor], axis=0))
            return inner

        lax.fori_loop(0, ITERS - 1, turn, 0)
        for j in range(group):
            k = g * group + j
            real, imag, _, _, factor = apply_corr(k)
            gain = scale_ref[k] * factor
            weight_real = ((steer_real * real - steer_imag * imag) * gain)[:beams]
            weight_imag = ((steer_real * imag + steer_imag * real) * gain)[:beams]
            flat_ref[k, 0] = weight_real[:, :ports].astype(jnp.bfloat16)
            flat_ref[k, 1] = weight_imag[:, :ports].astype(jnp.bfloat16)
            tails = weight_real[:, full:] + pltpu.roll(weight_imag[:, full:], LANES // 2, 1)
            tiles = [weight_real[:, i : i + LANES] for i in range(0, full, LANES)]
            tiles += [weight_imag[:, i : i + LANES] for i in range(0, full, LANES)]
            for i, tile in enumerate(tiles + [tails]):
                pay_sc[i, pl.ds(k, beams, stride=channels)] = tile
        return carry

    lax.fori_loop(0, channels // group, group_body, 0)
    for i in range(pay_sc.shape[0]):
        pay_ref[:, i * LANES : (i + 1) * LANES] = pay_sc[i].astype(jnp.bfloat16)


def power_weights(arrived, on, count, steer, ports):
    sources, channels, samples, wide = arrived.shape
    beams = steer.shape[0]
    rows = sources * samples
    width = ports // LANES * LANES + LANES
    pad = -(-beams // SUB) * SUB
    group = PAIR
    while channels % group:
        group //= 2
    return pl.pallas_call(
        functools.partial(power_kernel, ports=ports, group=group),
        out_shape=(
            jax.ShapeDtypeStruct((beams * channels, wide), jnp.bfloat16),
            jax.ShapeDtypeStruct((channels, 2, beams, ports), jnp.bfloat16),
        ),
        in_specs=[
            pl.BlockSpec(memory_space=pltpu.VMEM),
            pl.BlockSpec(memory_space=pltpu.VMEM),
            pl.BlockSpec(memory_space=pltpu.SMEM),
            pl.BlockSpec(memory_space=pltpu.VMEM),
        ],
        out_specs=(pl.BlockSpec(memory_space=pltpu.VMEM), pl.BlockSpec(memory_space=pltpu.VMEM)),
        scratch_shapes=[
            pltpu.VMEM((channels, 2 * rows, width), jnp.bfloat16),
            pltpu.VMEM((channels, width, 2 * rows), jnp.bfloat16),
            pltpu.VMEM((channels, 1, width), jnp.float32),
            pltpu.VMEM((channels, 4 * pad, width), jnp.bfloat16),
            pltpu.VMEM((wide // LANES, beams * channels, LANES), jnp.float32),
        ],
        name="power",
    )(arrived, on, count, steer)


def maps_kernel(w_ref, p_ref, o_ref):
    devices, block, channels, wide = w_ref.shape
    pixels = o_ref.shape[2]
    taps = p_ref[...]
    for b in range(block):
        rows = w_ref[:, b].reshape(devices * channels, wide)
        response = jnp.dot(rows, taps, preferred_element_type=jnp.float32)
        real, imag = response[:, :pixels], response[:, pixels:]
        o_ref[b] = real * real + imag * imag


def beam_power(gathered, taps):
    devices, beams, channels, wide = gathered.shape
    pixels = taps.shape[1] // 2
    block = 4
    while beams % block:
        block //= 2
    return pl.pallas_call(
        maps_kernel,
        grid=(beams // block,),
        out_shape=jax.ShapeDtypeStruct((beams, devices * channels, pixels), jnp.float32),
        in_specs=[
            pl.BlockSpec((devices, block, channels, wide), lambda i: (0, i, 0, 0)),
            pl.BlockSpec(taps.shape, lambda i: (0, 0)),
        ],
        out_specs=pl.BlockSpec((block, devices * channels, pixels), lambda i: (i, 0, 0)),
        name="maps",
    )(gathered, taps)


def off_flags(moments, starts, range_len):
    inside = (moments[None, :] >= starts[:, None]) & (moments[None, :] < starts[:, None] + range_len)
    return jnp.any(inside, axis=0)


def sum_over(value, axis, devices):
    if devices & (devices - 1):
        return lax.psum(value, axis)
    step = 1
    while step < devices:
        value = value + lax.ppermute(value, axis, [(i, i ^ step) for i in range(devices)])
        step *= 2
    return value


def on_device(voltages, off_starts, pointing, patterns):
    devices = lax.axis_size("tm")
    position = lax.axis_index("tm")
    channels, samples_dev, _, ports = voltages.shape
    beams = pointing.shape[0]
    per_dev = channels // devices
    total_time = samples_dev * devices
    off_span = max(4, total_time // 32)
    is_off = off_flags(jnp.arange(total_time, dtype=jnp.int32), off_starts, off_span)
    off_count = jnp.sum(is_off.astype(jnp.float32)).reshape(1, 1)
    on = 1.0 - is_off.astype(jnp.float32)[:, None]

    pixels = patterns.shape[2]
    real, imag = patterns[0], patterns[1]
    ordered = lane_order(real, imag, 0)
    taps = jnp.concatenate([ordered, lane_order(imag, -real, 0)], axis=1)
    pixel_ids = position * pixels + jnp.arange(pixels, dtype=jnp.int32)
    selector = (pointing[:, None] == pixel_ids[None, :]).astype(jnp.bfloat16)
    steer_local = jnp.einsum("bx,lx->bl", selector, ordered, preferred_element_type=jnp.float32)
    steering = sum_over(steer_local.astype(jnp.bfloat16), "tm", devices)

    packed = lane_order(voltages[:, :, 0], voltages[:, :, 1], 2)
    blocks = packed.reshape(devices, per_dev, samples_dev, packed.shape[-1])
    arrived = lax.all_to_all(blocks, "tm", split_axis=0, concat_axis=0, tiled=True)
    payload, weights = power_weights(arrived, on, off_count, steering, ports)
    flat_pair = weights.reshape(per_dev, 2, beams * ports)
    collected = lax.all_gather(payload, "tm", axis=0, tiled=False)
    maps = beam_power(collected.reshape(devices, beams, per_dev, -1), taps)
    return (flat_pair, maps.transpose(1, 0, 2))


def solution(mesh):
    in_specs = (P(None, ("groups", "tm"), None, None), P("groups"), P(), P(None, None, "tm"))
    out_specs = (P(("groups", "tm"), None, None), P("groups", None, "tm"))
    return jax.shard_map(on_device, mesh=mesh, in_specs=in_specs, out_specs=out_specs, check_vma=False)
```

time: 553 us -> 199 us (0.36)
  matrix products: 303 us -> 0.19 us
  blocking collectives: 81.9 us -> 0 us
  Pallas kernels: 0 us -> 63.5 us
  other arithmetic: 43.2 us -> 2.13 us
  waiting for transfers between devices: 60.6 us -> 92.3 us
  local copies, waits for them, and re-layouts: 40.7 us -> 11.7 us
  starting transfers between devices: 7.43 us -> 14.6 us
    dot_general x83 -> x1, matrix products: 303 us -> 0.19 us  [on_device(): jnp.einsum('bx,lx->bl', selector, ordered, preferred_element_type=jnp.flo...]
    psum x1 -> x0, blocking collectives: 81.9 us -> none  [on_device(): steering = lax.psum(steer_local, 'tm')]
    pallas_call x0 -> x2, Pallas kernels: none -> 63.5 us  [the longest x1 53.9 us: power_weights(): pl.pallas_call(functools.partial(power_kernel, ports=ports, group=group),...]
    ppermute x0 -> x4, waiting for transfers between devices: none -> 29.9 us  [sum_over(): lax.ppermute(value, axis, [(i, i ^ step) for i in range(devices)])]
    mul x22 -> x0, other arithmetic: 29.4 us -> none  [the longest x20 25.8 us: power_turn(): return (image_real * factor[:, None, :], image_imag * factor[:, None, :])]
    reshape x4 -> x1, local copies, waits for them, and re-layouts: 13.2 us -> 1.79 us  [on_device(): flat_pair = weights.reshape(per_dev, 2, beams * ports)]
    all_gather x1 -> x0, local copies, waits for them, and re-layouts: 10.1 us -> none  [on_device(): collected = lax.all_gather(flat_pair, 'tm', axis=0, tiled=True)]
    unnamed x11 -> x15, local copies, waits for them, and re-layouts: 11.5 us -> 1.48 us
  transfers between devices with their start and end apart: 2 -> 6, of which waited for: 1 -> 5; matrix products, arithmetic and copies ran while one was open for 1% -> 3% of each run, Pallas kernels for 0% -> 0%
where the time goes in v1:
time: 199 us
  waiting for transfers between devices  92.3 us (46%)
  Pallas kernels  63.5 us (32%)
  starting transfers between devices  14.6 us (7%)
  between operations  14.2 us (7%)
  local copies, waits for them, and re-layouts  11.7 us (6%)
  other arithmetic  2.13 us (1%)
    all_gather x1, waiting for transfers between devices, on_device(): collected = lax.all_gather(payload, 'tm', axis=0, tiled=False)  62.4 us
    pallas_call x1, Pallas kernels, power_weights(): pl.pallas_call(functools.partial(power_kernel, ports=ports, group=group),...  53.9 us
    ppermute x4, waiting for transfers between devices, sum_over(): lax.ppermute(value, axis, [(i, i ^ step) for i in range(devices)])  29.9 us
    pallas_call x1, Pallas kernels, beam_power(): pl.pallas_call(maps_kernel, grid=(beams // block,), out_shape=jax.ShapeDt...  9.64 us
    all_to_all x1, starting transfers between devices, on_device(): lax.all_to_all(blocks, 'tm', split_axis=0, concat_axis=0, tiled=True)  7.52 us
    ppermute x4, starting transfers between devices, sum_over(): lax.ppermute(value, axis, [(i, i ^ step) for i in range(devices)])  7.04 us
    slice x1, local copies, waits for them, and re-layouts, on_device(): packed = lane_order(voltages[:, :, 0], voltages[:, :, 1], 2)  4.37 us
  transfers between devices with their start and end apart: 6, of which 5 were waited for; matrix products, arithmetic and copies ran while one was open for 3% of the time, Pallas kernels for 0%

profile of v1, /device:TPU:0, one launch (start us, length us, event | category | flops | bytes accessed | tf_op | source)
XLA Modules:
  0.0 198.6 jit_solution(7228689542363241928)
XLA Ops:
  7.2 4.4 %fusion.5 = (bf16[256,8,1,188]{0,2,3,1:T(2,128)(2,1)S(1)}, bf16[256,8,1,188]{0,2,3,1:T(2,128)(2,1)S(1)}) fusion(bf16[256,8,2,188]{0,2,3,1:T(2,128)(2,1)} %param.4), kind=kLoop, calls=%fused_computation.28 | loop fusion | bytes 3080192 | tf_op jit(solution)/shard_map/slice | solution.py:234
  11.5 0.5 copy_bitcast_fusion
  12.2 2.4 %copy.27 = bf16[256,8,384]{2,1,0:T(8,128)(2,1)} copy(bf16[256,8,384]{0,1,2:T(8,128)(2,1)S(1)} %constant_dynamic-update-slice_fusion) | data formatting | bytes 3145728 | tf_op jit(solution)/shard_map/concatenate | solution.py:26
  14.6 7.5 %all-to-all-start = ((bf16[16,16,8,384]{3,2,1,0:T(8,128)(2,1)}), bf16[16,16,8,384]{3,2,1,0:T(8,128)(2,1)S(1)}, u32[]{:S(2)}, u32[]{:S(2)}) async-start(bf16[16,16,8,384]{3,2,1,0:T(8,128)(2,1)} %bitcast.2), calls=%async_computation | async-start | bytes 3145728 | tf_op jit(solution)/shard_map/all_to_all | solution.py:236
  22.1 0.0 all-gather.3.cloned.1.call-start
  22.2 0.0 copy-done.1
  22.3 0.1 fusion.7
  22.4 0.1 concatenate.13
  22.5 0.0 copy-done.3
  22.5 0.2 convolution_convert_fusion
  22.7 0.5 collective-permute-start
  23.2 0.9 collective-permute-done
  24.1 1.9 collective-permute-start.1
  26.0 7.5 %collective-permute-done.1 = bf16[36,384]{1,0:T(8,128)(2,1)S(1)} collective-permute-done((bf16[36,384]{1,0:T(8,128)(2,1)S(1)}, bf16[36,384]{1,0:T(8,128)(2,1)S(1)}, u32[]{:S(2)}, u32[]{:S(2)}) %collective-permute-start.1) | collective-permute-done | bytes 27680 | tf_op jit(solution)/shard_map/ppermute | solution.py:208
  33.6 0.2 collective-permute-start.2
  33.8 0.1 fusion.4
  33.8 15.5 %collective-permute-done.2 = bf16[36,384]{1,0:T(8,128)(2,1)S(1)} collective-permute-done((bf16[36,384]{1,0:T(8,128)(2,1)S(1)}, bf16[36,384]{1,0:T(8,128)(2,1)S(1)}, u32[]{:S(2)}, u32[]{:S(2)}) %collective-permute-start.2) | collective-permute-done | bytes 27680 | tf_op jit(solution)/shard_map/ppermute | solution.py:208
  49.3 4.4 %collective-permute-start.3 = (bf16[36,384]{1,0:T(8,128)(2,1)S(1)}, bf16[36,384]{1,0:T(8,128)(2,1)S(1)}, u32[]{:S(2)}, u32[]{:S(2)}) collective-permute-start(bf16[36,384]{1,0:T(8,128)(2,1)S(1)} %add.31), channel_id=1, source_target_pairs={{0,8},{1,9},{2,10},{3,11},{4,12},{5,13},{6,14},{7,15},{8,0},{9,1},... | collective-permute-start | bytes 82952 | tf_op jit(solution)/shard_map/ppermute | solution.py:208
  53.8 0.7 convert_reduce_fusion
  54.4 0.7 copy.32.on_ref
  55.2 6.1 %collective-permute-done.3 = bf16[36,384]{1,0:T(8,128)(2,1)S(1)} collective-permute-done((bf16[36,384]{1,0:T(8,128)(2,1)S(1)}, bf16[36,384]{1,0:T(8,128)(2,1)S(1)}, u32[]{:S(2)}, u32[]{:S(2)}) %collective-permute-start.3) | collective-permute-done | bytes 27680 | tf_op jit(solution)/shard_map/ppermute | solution.py:208
  61.2 0.6 add.32.steer_ref
  61.9 0.0 all-to-all-done.arr_ref
  61.9 1.1 copy-done
  63.0 53.9 %power.1 = (bf16[576,384]{1,0:T(8,128)(2,1)}, bf16[16,2,36,188]{3,2,1,0:T(8,128)(2,1)}) custom-call(bf16[16,16,8,384]{3,2,1,0:T(8,128)(2,1)} %copy-done, f32[128,1]{1,0:T(8,128)} %copy.32.on_ref, f32[1,1]{1,0:T(1,128)} %bitcast.4.count_ref, bf16[36,384]{1,0:T(8,128)(2,1)} %add.32.steer_ref), custom_call_target="tpu_custom_call" | custom-call | tf_op jit(solution)/shard_map/power/pallas_call | solution.py:144
  116.9 0.0 all-gather.3.cloned.1.call-update
  117.0 0.1 concatenate.14
  117.1 0.7 pad_maximum_fusion.p_ref
  117.8 0.2 copy-done.2
  118.0 1.8 reshape.51
  119.8 62.4 %all-gather.3.cloned.1.call-done = bf16[9216,384]{1,0:T(8,128)(2,1)} async-done(((bf16[576,384]{1,0:T(8,128)(2,1)}), bf16[9216,384]{1,0:T(8,128)(2,1)}) %all-gather.3.cloned.1.call-update) | async-done | bytes 7077904 | tf_op jit(solution)/shard_map/all_gather | solution.py:239
  182.1 9.6 %maps.1 = f32[36,256,128]{2,1,0:T(8,128)} custom-call(bf16[16,36,16,384]{3,2,1,0:T(8,128)(2,1)} %bitcast.24, bf16[384,256]{1,0:T(8,128)(2,1)} %pad_maximum_fusion.p_ref), custom_call_target="tpu_custom_call" | custom-call | tf_op jit(solution)/shard_map/maps/pallas_call | solution.py:185
  (24 shorter events, 0.3 us)
Async XLA Ops:
  14.6 7.6 %copy-start.1 = (bf16[2,188,128]{2,0,1:T(2,128)(2,1)S(1)}, bf16[2,188,128]{2,0,1:T(2,128)(2,1)}, u32[]{:S(2)}) copy-start(bf16[2,188,128]{2,0,1:T(2,128)(2,1)} %param.7) | copy-start | bytes 288772
  14.6 7.9 %copy-start.3 = (s32[36]{0:T(128)S(1)}, s32[36]{0:T(128)}, u32[]{:S(2)}) copy-start(s32[36]{0:T(128)} %param.6) | copy-start | bytes 436
  14.6 11.4 %copy-start.4 = (s32[8]{0:T(128)S(1)}, s32[8]{0:T(128)}, u32[]{:S(2)}) copy-start(s32[8]{0:T(128)} %param.5) | copy-start | bytes 100
  14.6 47.3 %all-to-all-start = ((bf16[16,16,8,384]{3,2,1,0:T(8,128)(2,1)}), bf16[16,16,8,384]{3,2,1,0:T(8,128)(2,1)S(1)}, u32[]{:S(2)}, u32[]{:S(2)}) async-start(bf16[16,16,8,384]{3,2,1,0:T(8,128)(2,1)} %bitcast.2), calls=%async_computation | async-start | bytes 3145728 | tf_op jit(solution)/shard_map/all_to_all | solution.py:236
  22.1 160.0 %all-gather.3.cloned.1.call-start = ((), (), s32[]{:S(2)}) async-start(), calls=%async_computation.1 | async-start | bytes 7520256 | tf_op jit(solution)/shard_map/all_gather | solution.py:239
  22.7 1.3 collective-permute-start
  24.1 9.5 %collective-permute-start.1 = (bf16[36,384]{1,0:T(8,128)(2,1)S(1)}, bf16[36,384]{1,0:T(8,128)(2,1)S(1)}, u32[]{:S(2)}, u32[]{:S(2)}) collective-permute-start(bf16[36,384]{1,0:T(8,128)(2,1)S(1)} %add.29), channel_id=1, source_target_pairs={{0,2},{1,3},{2,0},{3,1},{4,6},{5,7},{6,4},{7,5},{8,10},{9,11},{10,... | collective-permute-start | bytes 82952 | tf_op jit(solution)/shard_map/ppermute | solution.py:208
  33.6 15.8 %collective-permute-start.2 = (bf16[36,384]{1,0:T(8,128)(2,1)S(1)}, bf16[36,384]{1,0:T(8,128)(2,1)S(1)}, u32[]{:S(2)}, u32[]{:S(2)}) collective-permute-start(bf16[36,384]{1,0:T(8,128)(2,1)S(1)} %add.30), channel_id=1, source_target_pairs={{0,4},{1,5},{2,6},{3,7},{4,0},{5,1},{6,2},{7,3},{8,12},{9,13},{10,... | collective-permute-start | bytes 82952 | tf_op jit(solution)/shard_map/ppermute | solution.py:208
  49.3 11.9 %collective-permute-start.3 = (bf16[36,384]{1,0:T(8,128)(2,1)S(1)}, bf16[36,384]{1,0:T(8,128)(2,1)S(1)}, u32[]{:S(2)}, u32[]{:S(2)}) collective-permute-start(bf16[36,384]{1,0:T(8,128)(2,1)S(1)} %add.31), channel_id=1, source_target_pairs={{0,8},{1,9},{2,10},{3,11},{4,12},{5,13},{6,14},{7,15},{8,0},{9,1},... | collective-permute-start | bytes 82952 | tf_op jit(solution)/shard_map/ppermute | solution.py:208
  61.9 1.1 copy-start
  116.9 1.1 copy-start.2
Sparse Core Ops, SparseCore 0:
  117.1 65.0 all-gather.2

commit v2 on v1

--- a/solution.py
+++ b/solution.py
@@ -7,10 +7,13 @@
 from jax.experimental.pallas import tpu as pltpu
 from jax.sharding import PartitionSpec as P
 
+
 ITERS = 20
 LANES = 128
 SUB = 8
-PAIR = 4
+PAIR = 16
+TURNS = 3
+CHUNKS = 2
 
 
 def lane_order(real, imag, axis):
@@ -39,7 +42,7 @@
 def power_kernel(
     arr_ref, on_ref, count_ref, steer_ref, pay_ref, flat_ref, volt_ref, voltt_ref, scale_ref, lhs_ref, pay_sc, *, ports, group
 ):
-    sources, channels, samples, wide = arr_ref.shape
+    _, channels, _, wide = arr_ref.shape
     beams = steer_ref.shape[0]
     rows = volt_ref.shape[1] // 2
     full = ports // LANES * LANES
@@ -48,6 +51,8 @@
     valid = lax.broadcasted_iota(jnp.int32, (beams, width), 1) < ports
 
     def padded(block):
+        if pad == beams:
+            return block
         return jnp.concatenate([block, jnp.zeros((pad - beams, width), jnp.float32)], axis=0)
 
     steer_real, steer_imag = split_lanes(steer_ref[...].astype(jnp.float32), full)
@@ -82,7 +87,7 @@
         store_pair(k, jnp.concatenate([first, jnp.zeros_like(first)], axis=0))
         return carry
 
-    lax.fori_loop(0, channels, prepare, 0)
+    lax.fori_loop(0, channels, prepare, 0, unroll=min(4, channels))
 
     def apply_corr(k):
         part = halves_dot(lhs_ref[k], voltt_ref[k])
@@ -104,14 +109,20 @@
         return real, imag, scaled_real, scaled_imag, factor
 
     def group_body(g, carry):
-        def turn(step, inner):
+        def turn():
             for j in range(group):
                 k = g * group + j
                 _, _, scaled_real, scaled_imag, factor = apply_corr(k)
                 store_pair(k, jnp.concatenate([scaled_real * factor, scaled_imag * factor], axis=0))
+
+        def trip(step, inner):
+            for _ in range(TURNS):
+                turn()
             return inner
 
-        lax.fori_loop(0, ITERS - 1, turn, 0)
+        lax.fori_loop(0, (ITERS - 1) // TURNS, trip, 0)
+        for _ in range((ITERS - 1) % TURNS):
+            turn()
         for j in range(group):
             k = g * group + j
             real, imag, _, _, factor = apply_corr(k)
@@ -165,34 +176,118 @@
     )(arrived, on, count, steer)
 
 
-def maps_kernel(w_ref, p_ref, o_ref):
-    devices, block, channels, wide = w_ref.shape
-    pixels = o_ref.shape[2]
-    taps = p_ref[...]
-    for b in range(block):
-        rows = w_ref[:, b].reshape(devices * channels, wide)
+def maps_kernel(ids_ref, taps_ref, *refs, shards, views, channels, first, per_dev, begun):
+    shard_refs = refs[:shards]
+    out_ref, *sent_refs = refs[shards + begun : shards + begun + views]
+    in_buf, out_buf, in_sem, out_sem = refs[-4:]
+    pixels = out_buf.shape[3]
+    each = shard_refs[0].shape[0]
+
+    def fetch(op, i, slot):
+        return pltpu.make_async_copy(shard_refs[op].at[i], in_buf.at[slot], in_sem.at[slot])
+
+    def emit(step, slot):
+        row = pl.multiple_of(ids_ref[step] * per_dev + first, channels)
+        return pltpu.make_async_copy(out_buf.at[slot], out_ref.at[:, pl.ds(row, channels)], out_sem.at[slot])
+
+    def view(rows, j):
+        taps = taps_ref[:, 2 * j * pixels : 2 * (j + 1) * pixels]
         response = jnp.dot(rows, taps, preferred_element_type=jnp.float32)
         real, imag = response[:, :pixels], response[:, pixels:]
-        o_ref[b] = real * real + imag * imag
-
-
-def beam_power(gathered, taps):
-    devices, beams, channels, wide = gathered.shape
-    pixels = taps.shape[1] // 2
-    block = 4
-    while beams % block:
-        block //= 2
+        return real * real + imag * imag
+
+    if each == 1:
+        for step in range(shards):
+            fetch(step, 0, step).start()
+        for step in range(shards):
+            fetch(step, 0, step).wait()
+            rows = in_buf[step]
+            out_buf[step] = view(rows, 0).reshape(out_buf.shape[1:])
+            emit(step, step).start()
+            for j, sent in enumerate(sent_refs):
+                sent[step] = view(rows, j + 1).astype(jnp.bfloat16)
+        for step in range(shards):
+            emit(step, step).wait()
+    else:
+
+        def body(step, carry):
+            copy = fetch(0, step, 0)
+            copy.start()
+            copy.wait()
+            out_buf[0] = view(in_buf[0], 0).reshape(out_buf.shape[1:])
+            out = emit(step, 0)
+            out.start()
+            out.wait()
+            return carry
+
+        lax.fori_loop(0, each, body, 0)
+
+
+def beam_power(ids, taps, shards, into, shape, channels, first, per_dev):
+    beams, _, pixels = shape
+    each, depth, wide = shards[0].shape
+    assert each == 1 or len(shards) == 1
+    views = taps.shape[1] // (2 * pixels)
+    begun = into is not None
+    any_space = pl.BlockSpec(memory_space=pl.ANY)
+    vmem = pl.BlockSpec(memory_space=pltpu.VMEM)
+    operands = [ids, taps, *shards] + ([into] if begun else [])
+    sent = jax.ShapeDtypeStruct((len(shards), depth, pixels), jnp.bfloat16)
+    slots = len(shards)
     return pl.pallas_call(
-        maps_kernel,
-        grid=(beams // block,),
-        out_shape=jax.ShapeDtypeStruct((beams, devices * channels, pixels), jnp.float32),
-        in_specs=[
-            pl.BlockSpec((devices, block, channels, wide), lambda i: (0, i, 0, 0)),
-            pl.BlockSpec(taps.shape, lambda i: (0, 0)),
+        functools.partial(
+            maps_kernel, shards=slots, views=views, channels=channels, first=first, per_dev=per_dev, begun=begun
+        ),
+        out_shape=(jax.ShapeDtypeStruct(shape, jnp.float32),) + (sent,) * (views - 1),
+        in_specs=[pl.BlockSpec(memory_space=pltpu.SMEM), vmem] + [any_space] * (len(operands) - 2),
+        out_specs=(any_space,) + (vmem,) * (views - 1),
+        scratch_shapes=[
+            pltpu.VMEM((slots, depth, wide), jnp.bfloat16),
+            pltpu.VMEM((slots, beams, channels, pixels), jnp.float32),
+            pltpu.SemaphoreType.DMA((slots,)),
+            pltpu.SemaphoreType.DMA((slots,)),
         ],
-        out_specs=pl.BlockSpec((block, devices * channels, pixels), lambda i: (i, 0, 0)),
+        input_output_aliases={2 + slots: 0} if begun else {},
         name="maps",
-    )(gathered, taps)
+    )(*operands)
+
+
+def place_kernel(ids_ref, *refs, parts, channels, first, per_dev):
+    part_refs = refs[:parts]
+    out_ref, buf, sem = refs[parts + 1], refs[-2], refs[-1]
+    each = part_refs[0].shape[0]
+
+    def emit(slot):
+        row = pl.multiple_of(ids_ref[slot] * per_dev + first, channels)
+        return pltpu.make_async_copy(buf.at[slot], out_ref.at[:, pl.ds(row, channels)], sem.at[slot])
+
+    for op, part in enumerate(part_refs):
+        for i in range(each):
+            slot = op * each + i
+            buf[slot] = part[i].astype(jnp.float32).reshape(buf.shape[1:])
+            emit(slot).start()
+    for slot in range(parts * each):
+        emit(slot).wait()
+
+
+def place_maps(ids, parts, into, channels, first, per_dev):
+    beams, _, pixels = into.shape
+    slots = len(parts) * parts[0].shape[0]
+    any_space = pl.BlockSpec(memory_space=pl.ANY)
+    return pl.pallas_call(
+        functools.partial(place_kernel, parts=len(parts), channels=channels, first=first, per_dev=per_dev),
+        out_shape=jax.ShapeDtypeStruct(into.shape, jnp.float32),
+        in_specs=[pl.BlockSpec(memory_space=pltpu.SMEM)]
+        + [pl.BlockSpec(memory_space=pltpu.VMEM)] * len(parts)
+        + [any_space],
+        out_specs=any_space,
+        scratch_shapes=[
+            pltpu.VMEM((slots, beams, channels, pixels), jnp.float32),
+            pltpu.SemaphoreType.DMA((slots,)),
+        ],
+        input_output_aliases={1 + len(parts): 0},
+        name="place",
+    )(ids, *parts, into)
 
 
 def off_flags(moments, starts, range_len):
@@ -205,9 +300,24 @@
         return lax.psum(value, axis)
     step = 1
     while step < devices:
-        value = value + lax.ppermute(value, axis, [(i, i ^ step) for i in range(devices)])
+        moved = lax.ppermute(value, axis, [(i, i ^ step) for i in range(devices)])
+        value = value + moved
         step *= 2
     return value
+
+
+def turned(value, shift, count):
+    return lax.ppermute(value, "tm", [(i, (i + shift) % count) for i in range(count)])
+
+
+def crossed(value, bits, count):
+    return lax.ppermute(value, "tm", [(i, i ^ bits) for i in range(count)])
+
+
+def other_parts(ordered, full):
+    half = LANES // 2
+    real, imag, tails = ordered[:full], ordered[full : 2 * full], ordered[2 * full :]
+    return jnp.concatenate([imag, -real, tails[half:], -tails[:half]], axis=0)
 
 
 def on_device(voltages, off_starts, pointing, patterns):
@@ -216,6 +326,7 @@
     channels, samples_dev, _, ports = voltages.shape
     beams = pointing.shape[0]
     per_dev = channels // devices
+    full = ports // LANES * LANES
     total_time = samples_dev * devices
     off_span = max(4, total_time // 32)
     is_off = off_flags(jnp.arange(total_time, dtype=jnp.int32), off_starts, off_span)
@@ -223,9 +334,7 @@
     on = 1.0 - is_off.astype(jnp.float32)[:, None]
 
     pixels = patterns.shape[2]
-    real, imag = patterns[0], patterns[1]
-    ordered = lane_order(real, imag, 0)
-    taps = jnp.concatenate([ordered, lane_order(imag, -real, 0)], axis=1)
+    ordered = lane_order(patterns[0], patterns[1], 0)
     pixel_ids = position * pixels + jnp.arange(pixels, dtype=jnp.int32)
     selector = (pointing[:, None] == pixel_ids[None, :]).astype(jnp.bfloat16)
     steer_local = jnp.einsum("bx,lx->bl", selector, ordered, preferred_element_type=jnp.float32)
@@ -233,11 +342,42 @@
 
     packed = lane_order(voltages[:, :, 0], voltages[:, :, 1], 2)
     blocks = packed.reshape(devices, per_dev, samples_dev, packed.shape[-1])
-    arrived = lax.all_to_all(blocks, "tm", split_axis=0, concat_axis=0, tiled=True)
-    payload, weights = power_weights(arrived, on, off_count, steering, ports)
+    lines = devices == 16 and per_dev % (8 * CHUNKS) == 0
+    chunks = CHUNKS if lines else 1
+    part = per_dev // chunks
+    shape = (beams, channels, pixels)
+
+    arrived = []
+    for i in range(chunks):
+        block = blocks[:, i * part : (i + 1) * part]
+        arrived.append(lax.all_to_all(block, "tm", split_axis=0, concat_axis=0, tiled=True))
+    taps = [ordered]
+    if lines:
+        taps += [crossed(ordered, bits, devices) for bits in (1, 2, 3)]
+    taps = jnp.concatenate([t for o in taps for t in (o, other_parts(o, full))], axis=1)
+
+    outs = []
+    for block in arrived:
+        outs.append(power_weights(block, on, off_count, steering, ports))
+    weights = jnp.concatenate([w for _, w in outs], axis=0)
     flat_pair = weights.reshape(per_dev, 2, beams * ports)
-    collected = lax.all_gather(payload, "tm", axis=0, tiled=False)
-    maps = beam_power(collected.reshape(devices, beams, per_dev, -1), taps)
+    if lines:
+        shifts = (0, 4, 12, 8)
+        sources = jnp.stack([(position - shift) % devices for shift in shifts]).astype(jnp.int32)
+        maps = None
+        sent = []
+        for i, (payload, _) in enumerate(outs):
+            shards = [payload] + [turned(payload, shift, devices) for shift in shifts[1:]]
+            maps, *away = beam_power(
+                sources, taps, [shard[None] for shard in shards], maps, shape, part, i * part, per_dev
+            )
+            sent.append([crossed(away[bits - 1], bits, devices) for bits in (2, 3, 1)])
+        places = jnp.concatenate([sources ^ bits for bits in (2, 3, 1)])
+        for i, parts in enumerate(sent):
+            maps = place_maps(places, parts, maps, part, i * part, per_dev)
+    else:
+        collected = lax.all_gather(outs[0][0], "tm", axis=0, tiled=False)
+        (maps,) = beam_power(jnp.arange(devices, dtype=jnp.int32), taps, [collected], None, shape, part, 0, per_dev)
     return (flat_pair, maps.transpose(1, 0, 2))
 
 

time: 199 us -> 165 us (0.83)
  the two profiles are of different devices: /device:TPU:0 before, /device:TPU:13 now
where the time goes in v2:
time: 165 us; the launch traced here: 164 us
  waiting for transfers between devices  65 us (39%)
  Pallas kernels  45.1 us (27%)
  starting transfers between devices  28.6 us (17%)
  local copies, waits for them, and re-layouts  18.1 us (11%)
  other arithmetic  4.32 us (3%)
    ppermute x6, waiting for transfers between devices, turned(): lax.ppermute(value, 'tm', [(i, (i + shift) % count) for i in range(count)])  37.2 us
    pallas_call x2, Pallas kernels, power_weights(): pl.pallas_call(functools.partial(power_kernel, ports=ports, group=group),...  29.1 us
    ppermute x9, waiting for transfers between devices, crossed(): return lax.ppermute(value, 'tm', [(i, i ^ bits) for i in range(count)])  15.3 us
    pallas_call x2, Pallas kernels, beam_power(): pl.pallas_call(functools.partial(maps_kernel, shards=slots, views=views,...  11.1 us
    all_to_all x2, starting transfers between devices, on_device(): lax.all_to_all(block, 'tm', split_axis=0, concat_axis=0, tiled=True)  10.5 us
    ppermute x4, waiting for transfers between devices, sum_over(): moved = lax.ppermute(value, axis, [(i, i ^ step) for i in range(devices)])  8.31 us
    ppermute x9, starting transfers between devices, crossed(): return lax.ppermute(value, 'tm', [(i, i ^ bits) for i in range(count)])  7.31 us
    ppermute x6, starting transfers between devices, turned(): lax.ppermute(value, 'tm', [(i, (i + shift) % count) for i in range(count)])  6.05 us
  transfers between devices with their start and end apart: 21, of which 8 were waited for; matrix products, arithmetic and copies ran while one was open for 10% of the time, Pallas kernels for 26%

profile of v2, /device:TPU:13, one launch (start us, length us, event | category | flops | bytes accessed | tf_op | source)
XLA Modules:
  0.0 163.9 jit_solution(4691150629898257407)
XLA Ops:
  1.5 1.0 fusion.20
  3.9 1.8 %collective-permute-start.6 = (bf16[384,128]{1,0:T(8,128)(2,1)S(1)}, bf16[384,128]{1,0:T(8,128)(2,1)S(1)}, u32[]{:S(2)}, u32[]{:S(2)}) collective-permute-start(bf16[384,128]{1,0:T(8,128)(2,1)S(1)} %concatenate.35), channel_id=1, source_target_pairs={{0,3},{1,2},{2,1},{3,0},{4,7},{5,6},{6,5},{7,4},{8,11},{9,10},{10,... | collective-permute-start | bytes 294920 | tf_op jit(solution)/shard_map/ppermute | solution.py:314
  6.2 1.5 convolution_convert_fusion
  8.0 4.4 %fusion.12 = (bf16[256,8,1,188]{0,2,3,1:T(2,128)(2,1)S(1)}, bf16[256,8,1,188]{0,2,3,1:T(2,128)(2,1)S(1)}) fusion(bf16[256,8,2,188]{0,2,3,1:T(2,128)(2,1)} %param.4), kind=kLoop, calls=%fused_computation.53 | loop fusion | bytes 3080192 | tf_op jit(solution)/shard_map/slice | solution.py:343
  13.0 1.6 copy.30
  14.7 1.4 fusion.11
  16.1 6.1 %all-to-all-start = ((bf16[16,8,8,384]{3,2,1,0:T(8,128)(2,1)}), bf16[16,8,8,384]{3,2,1,0:T(8,128)(2,1)S(1)}, u32[]{:S(2)}, u32[]{:S(2)}) async-start(bf16[16,8,8,384]{3,2,1,0:T(8,128)(2,1)} %get-tuple-element.34), calls=%async_computation | async-start | bytes 1572864 | tf_op jit(solution)/shard_map/all_to_all | solution.py:353
  23.2 1.2 collective-permute-start.1
  25.1 1.6 collective-permute-done.1
  26.7 2.2 %collective-permute-start.2 = (bf16[36,384]{1,0:T(8,128)(2,1)S(1)}, bf16[36,384]{1,0:T(8,128)(2,1)S(1)}, u32[]{:S(2)}, u32[]{:S(2)}) collective-permute-start(bf16[36,384]{1,0:T(8,128)(2,1)S(1)} %add.50), channel_id=1, source_target_pairs={{0,4},{1,5},{2,6},{3,7},{4,0},{5,1},{6,2},{7,3},{8,12},{9,13},{10,... | collective-permute-start | bytes 82952 | tf_op jit(solution)/shard_map/ppermute | solution.py:303
  30.3 6.7 %collective-permute-done.2 = bf16[36,384]{1,0:T(8,128)(2,1)S(1)} collective-permute-done((bf16[36,384]{1,0:T(8,128)(2,1)S(1)}, bf16[36,384]{1,0:T(8,128)(2,1)S(1)}, u32[]{:S(2)}, u32[]{:S(2)}) %collective-permute-start.2) | collective-permute-done | bytes 27680 | tf_op jit(solution)/shard_map/ppermute | solution.py:303
  37.0 1.0 collective-permute-start.3
  38.0 4.2 %all-to-all-done.arr_ref = bf16[16,8,8,384]{3,2,1,0:T(8,128)(2,1)S(1)} async-done(((bf16[16,8,8,384]{3,2,1,0:T(8,128)(2,1)}), bf16[16,8,8,384]{3,2,1,0:T(8,128)(2,1)S(1)}, u32[]{:S(2)}, u32[]{:S(2)}) %all-to-all-start) | async-done | bytes 786464 | tf_op jit(solution)/shard_map/all_to_all | solution.py:353
  42.2 4.4 %all-to-all-start.1 = ((bf16[16,8,8,384]{3,2,1,0:T(8,128)(2,1)}), bf16[16,8,8,384]{3,2,1,0:T(8,128)(2,1)S(1)}, u32[]{:S(2)}, u32[]{:S(2)}) async-start(bf16[16,8,8,384]{3,2,1,0:T(8,128)(2,1)} %get-tuple-element.35), calls=%async_computation.1 | async-start | bytes 1572864 | tf_op jit(solution)/shard_map/all_to_all | solution.py:353
  47.4 14.6 %power.2 = (bf16[288,384]{1,0:T(8,128)(2,1)}, bf16[8,2,36,188]{3,2,1,0:T(8,128)(2,1)}) custom-call(bf16[16,8,8,384]{3,2,1,0:T(8,128)(2,1)} %copy-done.1, f32[128,1]{1,0:T(8,128)} %copy.35.on_ref, f32[1,1]{1,0:T(1,128)} %bitcast.4.count_ref, bf16[36,384]{1,0:T(8,128)(2,1)} %add.52.steer_ref), custom_call_target="tpu_custom_call" | custom-call | tf_op jit(solution)/shard_map/power/pallas_call | solution.py:155
  62.0 2.1 %collective-permute-start.12 = (bf16[288,384]{1,0:T(8,128)(2,1)}, bf16[288,384]{1,0:T(8,128)(2,1)S(1)}, u32[]{:S(2)}, u32[]{:S(2)}) collective-permute-start(bf16[288,384]{1,0:T(8,128)(2,1)} %get-tuple-element.17), channel_id=1, source_target_pairs={{0,8},{1,9},{2,10},{3,11},{4,12},{5,13},{6,14},{7,15},{8,0},{9,1},... | collective-permute-start | bytes 663560 | tf_op jit(solution)/shard_map/ppermute | solution.py:310
  64.3 1.2 collective-permute-start.10
  65.6 13.5 %collective-permute-done.12 = bf16[288,384]{1,0:T(8,128)(2,1)S(1)} collective-permute-done((bf16[288,384]{1,0:T(8,128)(2,1)}, bf16[288,384]{1,0:T(8,128)(2,1)S(1)}, u32[]{:S(2)}, u32[]{:S(2)}) %collective-permute-start.12) | collective-permute-done | bytes 221216 | tf_op jit(solution)/shard_map/ppermute | solution.py:310
  79.1 5.4 %collective-permute-done.11 = bf16[288,384]{1,0:T(8,128)(2,1)S(1)} collective-permute-done((bf16[288,384]{1,0:T(8,128)(2,1)}, bf16[288,384]{1,0:T(8,128)(2,1)S(1)}, u32[]{:S(2)}, u32[]{:S(2)}) %collective-permute-start.11) | collective-permute-done | bytes 221216 | tf_op jit(solution)/shard_map/ppermute | solution.py:310
  85.3 5.5 %maps.2 = (f32[36,256,128]{2,1,0:T(8,128)}, bf16[4,288,128]{2,1,0:T(8,128)(2,1)}, bf16[4,288,128]{2,1,0:T(8,128)(2,1)}, bf16[4,288,128]{2,1,0:T(8,128)(2,1)}) custom-call(s32[4]{0:T(128)} %get-tuple-element.33.ids_ref, bf16[384,1024]{1,0:T(8,128)(2,1)} %copy-done, bf16[1,288,384]{2,1,0:T(8,128)(2,1)} %bitcast.36, bf16[1,288,384]{2,1,0:T(8,128)(2,1)} %bitcast.39, ...), custom_call_target="tpu_custom_call" | custom-call | tf_op jit(solution)/shard_map/maps/pallas_call | solution.py:237
  90.8 1.2 collective-permute-start.16
  92.0 0.9 copy-done.2
  93.0 14.6 %power.3 = (bf16[288,384]{1,0:T(8,128)(2,1)}, bf16[8,2,36,188]{3,2,1,0:T(8,128)(2,1)}) custom-call(bf16[16,8,8,384]{3,2,1,0:T(8,128)(2,1)} %copy-done.2, f32[128,1]{1,0:T(8,128)} %copy.35.on_ref, f32[1,1]{1,0:T(1,128)} %bitcast.4.count_ref, bf16[36,384]{1,0:T(8,128)(2,1)} %add.52.steer_ref), custom_call_target="tpu_custom_call" | custom-call | tf_op jit(solution)/shard_map/power/pallas_call | solution.py:155
  107.5 2.5 %collective-permute-start.8 = (bf16[288,384]{1,0:T(8,128)(2,1)}, bf16[288,384]{1,0:T(8,128)(2,1)S(1)}, u32[]{:S(2)}, u32[]{:S(2)}) collective-permute-start(bf16[288,384]{1,0:T(8,128)(2,1)} %get-tuple-element.16), channel_id=1, source_target_pairs={{0,12},{1,13},{2,14},{3,15},{4,0},{5,1},{6,2},{7,3},{8,4},{9,5},{1... | collective-permute-start | bytes 663560 | tf_op jit(solution)/shard_map/ppermute | solution.py:310
  110.0 10.5 %collective-permute-done.9 = bf16[288,384]{1,0:T(8,128)(2,1)S(1)} collective-permute-done((bf16[288,384]{1,0:T(8,128)(2,1)}, bf16[288,384]{1,0:T(8,128)(2,1)S(1)}, u32[]{:S(2)}, u32[]{:S(2)}) %collective-permute-start.9) | collective-permute-done | bytes 221216 | tf_op jit(solution)/shard_map/ppermute | solution.py:310
  120.5 7.8 %collective-permute-done.8 = bf16[288,384]{1,0:T(8,128)(2,1)S(1)} collective-permute-done((bf16[288,384]{1,0:T(8,128)(2,1)}, bf16[288,384]{1,0:T(8,128)(2,1)S(1)}, u32[]{:S(2)}, u32[]{:S(2)}) %collective-permute-start.8) | collective-permute-done | bytes 221216 | tf_op jit(solution)/shard_map/ppermute | solution.py:310
  129.2 5.6 %maps.3 = (f32[36,256,128]{2,1,0:T(8,128)}, bf16[4,288,128]{2,1,0:T(8,128)(2,1)}, bf16[4,288,128]{2,1,0:T(8,128)(2,1)}, bf16[4,288,128]{2,1,0:T(8,128)(2,1)}) custom-call(s32[4]{0:T(128)} %get-tuple-element.33.ids_ref, bf16[384,1024]{1,0:T(8,128)(2,1)} %copy-done, bf16[1,288,384]{2,1,0:T(8,128)(2,1)} %bitcast.40, ...), custom_call_target="tpu_custom_call", output_to_operand_aliasing={{0}: (6, {})} | custom-call | tf_op jit(solution)/shard_map/maps/pallas_call | solution.py:237
  135.1 2.7 %collective-permute-start.14 = (bf16[4,288,128]{2,1,0:T(8,128)(2,1)}, bf16[4,288,128]{2,1,0:T(8,128)(2,1)S(1)}, u32[]{:S(2)}, u32[]{:S(2)}) collective-permute-start(bf16[4,288,128]{2,1,0:T(8,128)(2,1)} %get-tuple-element.20), channel_id=1, source_target_pairs={{0,3},{1,2},{2,1},{3,0},{4,7},{5,6},{6,5},{7,4},{8,11},{9,10},{10,... | collective-permute-start | bytes 884744 | tf_op jit(solution)/shard_map/ppermute | solution.py:314
  139.3 1.8 %reshape.42 = bf16[16,2,6768]{2,1,0:T(2,128)(2,1)} reshape(bf16[16,2,36,188]{3,2,1,0:T(8,128)(2,1)S(1)} %pad_maximum_fusion) | data formatting | bytes 866304 | tf_op jit(solution)/shard_map/reshape | solution.py:363
  141.1 15.3 %collective-permute-done.17.refs_1_ = bf16[4,288,128]{2,1,0:T(8,128)(2,1)S(1)} collective-permute-done((bf16[4,288,128]{2,1,0:T(8,128)(2,1)}, bf16[4,288,128]{2,1,0:T(8,128)(2,1)S(1)}, u32[]{:S(2)}, u32[]{:S(2)}) %collective-permute-start.17) | collective-permute-done | bytes 294944 | tf_op jit(solution)/shard_map/ppermute | solution.py:314
  157.2 2.5 %place.2.refs_3_ = f32[36,256,128]{2,1,0:T(8,128)} custom-call(s32[12]{0:T(128)} %pad_add_fusion.1.ids_ref, bf16[4,288,128]{2,1,0:T(8,128)(2,1)} %copy-done.7, bf16[4,288,128]{2,1,0:T(8,128)(2,1)} %copy-done.11, bf16[4,288,128]{2,1,0:T(8,128)(2,1)} %copy-done.12, f32[36,256,128]{2,1,0:T(8,128)} %get-tuple-element.25.refs_3_), custom_call_target="tpu_custom_call", output_to_operand_aliasing={{}: (4, {})} | custom-call | tf_op jit(solution)/shard_map/place/pallas_call | solution.py:277
  161.3 2.5 %place.3 = f32[36,256,128]{2,1,0:T(8,128)} custom-call(s32[12]{0:T(128)} %pad_add_fusion.1.ids_ref, bf16[4,288,128]{2,1,0:T(8,128)(2,1)} %copy-done.8, bf16[4,288,128]{2,1,0:T(8,128)(2,1)} %copy-done.9, bf16[4,288,128]{2,1,0:T(8,128)(2,1)} %copy-done.10, f32[36,256,128]{2,1,0:T(8,128)} %place.2.refs_3_), custom_call_target="tpu_custom_call", output_to_operand_aliasing={{}: (4, {})} | custom-call | tf_op jit(solution)/shard_map/place/pallas_call | solution.py:277
  (113 shorter events, 13.5 us)
Async XLA Ops:
  2.6 9.8 %copy-start.5 = (bf16[1,128,128]{2,1,0:T(8,128)(2,1)}, bf16[1,128,128]{2,1,0:T(8,128)(2,1)S(1)}, u32[]{:S(2)}) copy-start(bf16[1,128,128]{2,1,0:T(8,128)(2,1)S(1)} %copy.53) | copy-start | bytes 98308
  3.9 42.8 %collective-permute-start.6 = (bf16[384,128]{1,0:T(8,128)(2,1)S(1)}, bf16[384,128]{1,0:T(8,128)(2,1)S(1)}, u32[]{:S(2)}, u32[]{:S(2)}) collective-permute-start(bf16[384,128]{1,0:T(8,128)(2,1)S(1)} %concatenate.35), channel_id=1, source_target_pairs={{0,3},{1,2},{2,1},{3,0},{4,7},{5,6},{6,5},{7,4},{8,11},{9,10},{10,... | collective-permute-start | bytes 294920 | tf_op jit(solution)/shard_map/ppermute | solution.py:314
  5.7 40.9 %collective-permute-start.5 = (bf16[384,128]{1,0:T(8,128)(2,1)S(1)}, bf16[384,128]{1,0:T(8,128)(2,1)S(1)}, u32[]{:S(2)}, u32[]{:S(2)}) collective-permute-start(bf16[384,128]{1,0:T(8,128)(2,1)S(1)} %concatenate.35), channel_id=1, source_target_pairs={{0,2},{1,3},{2,0},{3,1},{4,6},{5,7},{6,4},{7,5},{8,10},{9,11},{10,... | collective-permute-start | bytes 294920 | tf_op jit(solution)/shard_map/ppermute | solution.py:314
  6.0 31.9 %collective-permute-start.4 = (bf16[384,128]{1,0:T(8,128)(2,1)S(1)}, bf16[384,128]{1,0:T(8,128)(2,1)S(1)}, u32[]{:S(2)}, u32[]{:S(2)}) collective-permute-start(bf16[384,128]{1,0:T(8,128)(2,1)S(1)} %concatenate.35), channel_id=1, source_target_pairs={{0,1},{1,0},{2,3},{3,2},{4,5},{5,4},{6,7},{7,6},{8,9},{9,8},{10,11... | collective-permute-start | bytes 294920 | tf_op jit(solution)/shard_map/ppermute | solution.py:314
  7.7 14.7 %collective-permute-start = (bf16[36,384]{1,0:T(8,128)(2,1)}, bf16[36,384]{1,0:T(8,128)(2,1)}, u32[]{:S(2)}, u32[]{:S(2)}) collective-permute-start(bf16[36,384]{1,0:T(8,128)(2,1)} %convolution_convert_fusion), channel_id=1, source_target_pairs={{0,1},{1,0},{2,3},{3,2},{4,5},{5,4},{6,7},{7,6},{8,9},{9,8},{10,11... | collective-permute-start | bytes 82952 | tf_op jit(solution)/shard_map/ppermute | solution.py:303
  16.0 6.2 %copy-start.24 = (s32[8]{0:T(128)S(1)}, s32[8]{0:T(128)}, u32[]{:S(2)}) copy-start(s32[8]{0:T(128)} %param.5) | copy-start | bytes 100
  16.0 6.3 %copy-start.6 = (bf16[1,128,128]{2,1,0:T(8,128)(2,1)S(1)}, bf16[1,128,128]{2,1,0:T(8,128)(2,1)}, u32[]{:S(2)}) copy-start(bf16[1,128,128]{2,1,0:T(8,128)(2,1)} %copy-done.5) | copy-start | bytes 98308
  16.1 6.3 %copy-start.21 = (bf16[128,128]{1,0:T(8,128)(2,1)S(1)}, bf16[128,128]{1,0:T(8,128)(2,1)}, u32[]{:S(2)}) copy-start(bf16[128,128]{1,0:T(8,128)(2,1)} %get-tuple-element.30) | copy-start | bytes 98308
  16.1 26.1 %all-to-all-start = ((bf16[16,8,8,384]{3,2,1,0:T(8,128)(2,1)}), bf16[16,8,8,384]{3,2,1,0:T(8,128)(2,1)S(1)}, u32[]{:S(2)}, u32[]{:S(2)}) async-start(bf16[16,8,8,384]{3,2,1,0:T(8,128)(2,1)} %get-tuple-element.34), calls=%async_computation | async-start | bytes 1572864 | tf_op jit(solution)/shard_map/all_to_all | solution.py:353
  23.2 3.5 %collective-permute-start.1 = (bf16[36,384]{1,0:T(8,128)(2,1)S(1)}, bf16[36,384]{1,0:T(8,128)(2,1)S(1)}, u32[]{:S(2)}, u32[]{:S(2)}) collective-permute-start(bf16[36,384]{1,0:T(8,128)(2,1)S(1)} %add.49), channel_id=1, source_target_pairs={{0,2},{1,3},{2,0},{3,1},{4,6},{5,7},{6,4},{7,5},{8,10},{9,11},{10,... | collective-permute-start | bytes 82952 | tf_op jit(solution)/shard_map/ppermute | solution.py:303
  26.7 10.2 %collective-permute-start.2 = (bf16[36,384]{1,0:T(8,128)(2,1)S(1)}, bf16[36,384]{1,0:T(8,128)(2,1)S(1)}, u32[]{:S(2)}, u32[]{:S(2)}) collective-permute-start(bf16[36,384]{1,0:T(8,128)(2,1)S(1)} %add.50), channel_id=1, source_target_pairs={{0,4},{1,5},{2,6},{3,7},{4,0},{5,1},{6,2},{7,3},{8,12},{9,13},{10,... | collective-permute-start | bytes 82952 | tf_op jit(solution)/shard_map/ppermute | solution.py:303
  37.0 9.8 %collective-permute-start.3 = (bf16[36,384]{1,0:T(8,128)(2,1)S(1)}, bf16[36,384]{1,0:T(8,128)(2,1)S(1)}, u32[]{:S(2)}, u32[]{:S(2)}) collective-permute-start(bf16[36,384]{1,0:T(8,128)(2,1)S(1)} %add.51), channel_id=1, source_target_pairs={{0,8},{1,9},{2,10},{3,11},{4,12},{5,13},{6,14},{7,15},{8,0},{9,1},... | collective-permute-start | bytes 82952 | tf_op jit(solution)/shard_map/ppermute | solution.py:303
  42.2 49.8 %all-to-all-start.1 = ((bf16[16,8,8,384]{3,2,1,0:T(8,128)(2,1)}), bf16[16,8,8,384]{3,2,1,0:T(8,128)(2,1)S(1)}, u32[]{:S(2)}, u32[]{:S(2)}) async-start(bf16[16,8,8,384]{3,2,1,0:T(8,128)(2,1)} %get-tuple-element.35), calls=%async_computation.1 | async-start | bytes 1572864 | tf_op jit(solution)/shard_map/all_to_all | solution.py:353
  62.0 17.1 %collective-permute-start.12 = (bf16[288,384]{1,0:T(8,128)(2,1)}, bf16[288,384]{1,0:T(8,128)(2,1)S(1)}, u32[]{:S(2)}, u32[]{:S(2)}) collective-permute-start(bf16[288,384]{1,0:T(8,128)(2,1)} %get-tuple-element.17), channel_id=1, source_target_pairs={{0,8},{1,9},{2,10},{3,11},{4,12},{5,13},{6,14},{7,15},{8,0},{9,1},... | collective-permute-start | bytes 663560 | tf_op jit(solution)/shard_map/ppermute | solution.py:310
  64.1 20.4 %collective-permute-start.11 = (bf16[288,384]{1,0:T(8,128)(2,1)}, bf16[288,384]{1,0:T(8,128)(2,1)S(1)}, u32[]{:S(2)}, u32[]{:S(2)}) collective-permute-start(bf16[288,384]{1,0:T(8,128)(2,1)} %get-tuple-element.17), channel_id=1, source_target_pairs={{0,12},{1,13},{2,14},{3,15},{4,0},{5,1},{6,2},{7,3},{8,4},{9,5},{1... | collective-permute-start | bytes 663560 | tf_op jit(solution)/shard_map/ppermute | solution.py:310
  64.3 20.2 %collective-permute-start.10 = (bf16[288,384]{1,0:T(8,128)(2,1)}, bf16[288,384]{1,0:T(8,128)(2,1)S(1)}, u32[]{:S(2)}, u32[]{:S(2)}) collective-permute-start(bf16[288,384]{1,0:T(8,128)(2,1)} %get-tuple-element.17), channel_id=1, source_target_pairs={{0,4},{1,5},{2,6},{3,7},{4,8},{5,9},{6,10},{7,11},{8,12},{9,13},{1... | collective-permute-start | bytes 663560 | tf_op jit(solution)/shard_map/ppermute | solution.py:310
  65.6 18.9 %copy-start = (bf16[384,1024]{1,0:T(8,128)(2,1)}, bf16[384,1024]{1,0:T(8,128)(2,1)S(1)}, u32[]{:S(2)}) copy-start(bf16[384,1024]{1,0:T(8,128)(2,1)S(1)} %maximum_dynamic-update-slice_fusion.taps_ref) | copy-start | bytes 2359300
  90.8 47.7 %collective-permute-start.16 = (bf16[4,288,128]{2,1,0:T(8,128)(2,1)}, bf16[4,288,128]{2,1,0:T(8,128)(2,1)S(1)}, u32[]{:S(2)}, u32[]{:S(2)}) collective-permute-start(bf16[4,288,128]{2,1,0:T(8,128)(2,1)} %get-tuple-element.22), channel_id=1, source_target_pairs={{0,2},{1,3},{2,0},{3,1},{4,6},{5,7},{6,4},{7,5},{8,10},{9,11},{10,... | collective-permute-start | bytes 884744 | tf_op jit(solution)/shard_map/ppermute | solution.py:314
  107.5 13.0 %collective-permute-start.9 = (bf16[288,384]{1,0:T(8,128)(2,1)}, bf16[288,384]{1,0:T(8,128)(2,1)S(1)}, u32[]{:S(2)}, u32[]{:S(2)}) collective-permute-start(bf16[288,384]{1,0:T(8,128)(2,1)} %get-tuple-element.16), channel_id=1, source_target_pairs={{0,8},{1,9},{2,10},{3,11},{4,12},{5,13},{6,14},{7,15},{8,0},{9,1},... | collective-permute-start | bytes 663560 | tf_op jit(solution)/shard_map/ppermute | solution.py:310
  107.5 20.8 %collective-permute-start.8 = (bf16[288,384]{1,0:T(8,128)(2,1)}, bf16[288,384]{1,0:T(8,128)(2,1)S(1)}, u32[]{:S(2)}, u32[]{:S(2)}) collective-permute-start(bf16[288,384]{1,0:T(8,128)(2,1)} %get-tuple-element.16), channel_id=1, source_target_pairs={{0,12},{1,13},{2,14},{3,15},{4,0},{5,1},{6,2},{7,3},{8,4},{9,5},{1... | collective-permute-start | bytes 663560 | tf_op jit(solution)/shard_map/ppermute | solution.py:310
  110.0 18.4 %collective-permute-start.7 = (bf16[288,384]{1,0:T(8,128)(2,1)}, bf16[288,384]{1,0:T(8,128)(2,1)S(1)}, u32[]{:S(2)}, u32[]{:S(2)}) collective-permute-start(bf16[288,384]{1,0:T(8,128)(2,1)} %get-tuple-element.16), channel_id=1, source_target_pairs={{0,4},{1,5},{2,6},{3,7},{4,8},{5,9},{6,10},{7,11},{8,12},{9,13},{1... | collective-permute-start | bytes 663560 | tf_op jit(solution)/shard_map/ppermute | solution.py:310
  120.5 7.9 %copy-start.16 = (bf16[288,384]{1,0:T(8,128)(2,1)}, bf16[288,384]{1,0:T(8,128)(2,1)S(1)}, u32[]{:S(2)}) copy-start(bf16[288,384]{1,0:T(8,128)(2,1)S(1)} %collective-permute-done.9) | copy-start | bytes 663556
  129.2 9.3 %copy-start.23 = (bf16[4,288,128]{2,1,0:T(8,128)(2,1)S(1)}, bf16[4,288,128]{2,1,0:T(8,128)(2,1)}, u32[]{:S(2)}) copy-start(bf16[4,288,128]{2,1,0:T(8,128)(2,1)} %get-tuple-element.24) | copy-start | bytes 884740
  129.2 9.4 %copy-start.22 = (s32[4]{0:T(128)S(1)}, s32[4]{0:T(128)}, u32[]{:S(2)}) copy-start(s32[4]{0:T(128)} %get-tuple-element.33.ids_ref) | copy-start | bytes 52
  129.2 10.0 %copy-start.3 = (bf16[8,2,36,188]{3,2,1,0:T(8,128)(2,1)S(1)}, bf16[8,2,36,188]{3,2,1,0:T(8,128)(2,1)}, u32[]{:S(2)}) copy-start(bf16[8,2,36,188]{3,2,1,0:T(8,128)(2,1)} %get-tuple-element.14) | copy-start | bytes 649732
  129.2 10.0 %copy-start.4 = (bf16[8,2,36,188]{3,2,1,0:T(8,128)(2,1)S(1)}, bf16[8,2,36,188]{3,2,1,0:T(8,128)(2,1)}, u32[]{:S(2)}) copy-start(bf16[8,2,36,188]{3,2,1,0:T(8,128)(2,1)} %get-tuple-element.15) | copy-start | bytes 649732
  134.7 25.0 %collective-permute-start.13 = (bf16[4,288,128]{2,1,0:T(8,128)(2,1)}, bf16[4,288,128]{2,1,0:T(8,128)(2,1)S(1)}, u32[]{:S(2)}, u32[]{:S(2)}) collective-permute-start(bf16[4,288,128]{2,1,0:T(8,128)(2,1)} %get-tuple-element.19), channel_id=1, source_target_pairs={{0,2},{1,3},{2,0},{3,1},{4,6},{5,7},{6,4},{7,5},{8,10},{9,11},{10,... | collective-permute-start | bytes 884744 | tf_op jit(solution)/shard_map/ppermute | solution.py:314
  135.1 24.6 %collective-permute-start.14 = (bf16[4,288,128]{2,1,0:T(8,128)(2,1)}, bf16[4,288,128]{2,1,0:T(8,128)(2,1)S(1)}, u32[]{:S(2)}, u32[]{:S(2)}) collective-permute-start(bf16[4,288,128]{2,1,0:T(8,128)(2,1)} %get-tuple-element.20), channel_id=1, source_target_pairs={{0,3},{1,2},{2,1},{3,0},{4,7},{5,6},{6,5},{7,4},{8,11},{9,10},{10,... | collective-permute-start | bytes 884744 | tf_op jit(solution)/shard_map/ppermute | solution.py:314
  137.8 22.0 %collective-permute-start.15 = (bf16[4,288,128]{2,1,0:T(8,128)(2,1)}, bf16[4,288,128]{2,1,0:T(8,128)(2,1)S(1)}, u32[]{:S(2)}, u32[]{:S(2)}) collective-permute-start(bf16[4,288,128]{2,1,0:T(8,128)(2,1)} %get-tuple-element.21), channel_id=1, source_target_pairs={{0,1},{1,0},{2,3},{3,2},{4,5},{5,4},{6,7},{7,6},{8,9},{9,8},{10,11... | collective-permute-start | bytes 884744 | tf_op jit(solution)/shard_map/ppermute | solution.py:314
  137.8 18.6 %collective-permute-start.17 = (bf16[4,288,128]{2,1,0:T(8,128)(2,1)}, bf16[4,288,128]{2,1,0:T(8,128)(2,1)S(1)}, u32[]{:S(2)}, u32[]{:S(2)}) collective-permute-start(bf16[4,288,128]{2,1,0:T(8,128)(2,1)} %get-tuple-element.23), channel_id=1, source_target_pairs={{0,3},{1,2},{2,1},{3,0},{4,7},{5,6},{6,5},{7,4},{8,11},{9,10},{10,... | collective-permute-start | bytes 884744 | tf_op jit(solution)/shard_map/ppermute | solution.py:314
  138.4 18.0 %copy-start.7 = (bf16[4,288,128]{2,1,0:T(8,128)(2,1)}, bf16[4,288,128]{2,1,0:T(8,128)(2,1)S(1)}, u32[]{:S(2)}) copy-start(bf16[4,288,128]{2,1,0:T(8,128)(2,1)S(1)} %collective-permute-done.16.refs_0_) | copy-start | bytes 884740
  138.4 17.9 %collective-permute-start.18 = (bf16[4,288,128]{2,1,0:T(8,128)(2,1)S(1)}, bf16[4,288,128]{2,1,0:T(8,128)(2,1)S(1)}, u32[]{:S(2)}, u32[]{:S(2)}) collective-permute-start(bf16[4,288,128]{2,1,0:T(8,128)(2,1)S(1)} %copy-done.23), channel_id=1, source_target_pairs={{0,1},{1,0},{2,3},{3,2},{4,5},{5,4},{6,7},{7,6},{8,9},{9,8},{10,11... | collective-permute-start | bytes 884744 | tf_op jit(solution)/shard_map/ppermute | solution.py:314
  (14 other events, 25.1 us)

commit v3 on v2

--- a/solution.py
+++ b/solution.py
@@ -13,6 +13,8 @@
 SUB = 8
 PAIR = 16
 TURNS = 3
+GRANT = pltpu.CompilerParams(vmem_limit_bytes=28 << 20)
+MAP_SLOTS = 16
 CHUNKS = 2
 
 
@@ -30,6 +32,14 @@
         [cut(real, 0, full), cut(imag, 0, full), cut(real, full, ports), blank, cut(imag, full, ports), blank],
         axis=axis,
     )
+
+
+def lane_places(ports):
+    full = ports // LANES * LANES
+    part = jnp.arange(2)[:, None]
+    port = jnp.arange(ports)[None, :]
+    place = jnp.where(port < full, part * full + port, full + port + part * (LANES // 2))
+    return (place[:, :, None] == jnp.arange(2 * full + LANES)).astype(jnp.bfloat16)
 
 
 def split_lanes(block, full):
@@ -141,6 +151,10 @@
     lax.fori_loop(0, channels // group, group_body, 0)
     for i in range(pay_sc.shape[0]):
         pay_ref[:, i * LANES : (i + 1) * LANES] = pay_sc[i].astype(jnp.bfloat16)
+
+
+def here(value):
+    return pltpu.with_memory_space_constraint(value, pltpu.VMEM)
 
 
 def power_weights(arrived, on, count, steer, ports):
@@ -172,49 +186,75 @@
             pltpu.VMEM((channels, 4 * pad, width), jnp.bfloat16),
             pltpu.VMEM((wide // LANES, beams * channels, LANES), jnp.float32),
         ],
+        compiler_params=GRANT,
         name="power",
-    )(arrived, on, count, steer)
-
-
-def maps_kernel(ids_ref, taps_ref, *refs, shards, views, channels, first, per_dev, begun):
-    shard_refs = refs[:shards]
-    out_ref, *sent_refs = refs[shards + begun : shards + begun + views]
-    in_buf, out_buf, in_sem, out_sem = refs[-4:]
-    pixels = out_buf.shape[3]
-    each = shard_refs[0].shape[0]
-
-    def fetch(op, i, slot):
-        return pltpu.make_async_copy(shard_refs[op].at[i], in_buf.at[slot], in_sem.at[slot])
+    )(here(arrived), on, count, steer)
+
+
+def other_parts(ordered):
+    half = LANES // 2
+    full = (ordered.shape[0] - LANES) // 2
+    real, imag, tails = ordered[:full], ordered[full : 2 * full], ordered[2 * full :]
+    return jnp.concatenate([imag, -real, tails[half:], -tails[:half]], axis=0)
+
+
+def view(rows, ordered):
+    pixels = ordered.shape[1]
+    taps = jnp.concatenate([ordered, other_parts(ordered)], axis=1)
+    response = jnp.dot(rows, taps, preferred_element_type=jnp.float32)
+    real, imag = response[:, :pixels], response[:, pixels:]
+    return real * real + imag * imag
+
+
+def away_kernel(*refs, shards, views):
+    shard_refs, taps_refs, sent_refs = refs[:shards], refs[shards : shards + views], refs[shards + views :]
+    for taps, sent in zip(taps_refs, sent_refs):
+        for step, shard in enumerate(shard_refs):
+            sent[step] = view(shard[...], taps[...]).astype(jnp.bfloat16)
+
+
+def away_maps(taps, shards):
+    depth, _ = shards[0].shape
+    pixels = taps[0].shape[1]
+    views = len(taps)
+    sent = jax.ShapeDtypeStruct((len(shards), depth, pixels), jnp.bfloat16)
+    vmem = pl.BlockSpec(memory_space=pltpu.VMEM)
+    return pl.pallas_call(
+        functools.partial(away_kernel, shards=len(shards), views=views),
+        out_shape=(sent,) * views,
+        in_specs=[vmem] * (views + len(shards)),
+        out_specs=(vmem,) * views,
+        compiler_params=GRANT,
+        name="away",
+    )(*[here(shard) for shard in shards], *taps)
+
+
+def write_kernel(rows_ref, *refs, parts, channels, with_taps, begun):
+    taps_ref = refs[0] if with_taps else None
+    part_refs = refs[with_taps : with_taps + parts]
+    out_ref = refs[with_taps + parts + begun]
+    buf, sem = refs[-2:]
+    each = part_refs[0].shape[0]
+    slots = buf.shape[0]
 
     def emit(step, slot):
-        row = pl.multiple_of(ids_ref[step] * per_dev + first, channels)
-        return pltpu.make_async_copy(out_buf.at[slot], out_ref.at[:, pl.ds(row, channels)], out_sem.at[slot])
-
-    def view(rows, j):
-        taps = taps_ref[:, 2 * j * pixels : 2 * (j + 1) * pixels]
-        response = jnp.dot(rows, taps, preferred_element_type=jnp.float32)
-        real, imag = response[:, :pixels], response[:, pixels:]
-        return real * real + imag * imag
-
-    if each == 1:
-        for step in range(shards):
-            fetch(step, 0, step).start()
-        for step in range(shards):
-            fetch(step, 0, step).wait()
-            rows = in_buf[step]
-            out_buf[step] = view(rows, 0).reshape(out_buf.shape[1:])
+        row = pl.multiple_of(rows_ref[step], channels)
+        return pltpu.make_async_copy(buf.at[slot], out_ref.at[:, pl.ds(row, channels)], sem.at[slot])
+
+    def work(piece, slot):
+        piece = view(piece, taps_ref[...]) if with_taps else piece.astype(jnp.float32)
+        buf[slot] = piece.reshape(buf.shape[1:])
+
+    if slots == parts * each:
+        for step in range(slots):
+            work(part_refs[step // each][step % each], step)
             emit(step, step).start()
-            for j, sent in enumerate(sent_refs):
-                sent[step] = view(rows, j + 1).astype(jnp.bfloat16)
-        for step in range(shards):
+        for step in range(slots):
             emit(step, step).wait()
     else:
 
         def body(step, carry):
-            copy = fetch(0, step, 0)
-            copy.start()
-            copy.wait()
-            out_buf[0] = view(in_buf[0], 0).reshape(out_buf.shape[1:])
+            work(part_refs[0][step], 0)
             out = emit(step, 0)
             out.start()
             out.wait()
@@ -223,71 +263,36 @@
         lax.fori_loop(0, each, body, 0)
 
 
-def beam_power(ids, taps, shards, into, shape, channels, first, per_dev):
+def write_maps(rows, parts, into, shape, channels, taps=None):
     beams, _, pixels = shape
-    each, depth, wide = shards[0].shape
-    assert each == 1 or len(shards) == 1
-    views = taps.shape[1] // (2 * pixels)
-    begun = into is not None
+    slots = parts[0].shape[0] * len(parts)
+    if slots > MAP_SLOTS:
+        assert len(parts) == 1
+        slots = 1
     any_space = pl.BlockSpec(memory_space=pl.ANY)
-    vmem = pl.BlockSpec(memory_space=pltpu.VMEM)
-    operands = [ids, taps, *shards] + ([into] if begun else [])
-    sent = jax.ShapeDtypeStruct((len(shards), depth, pixels), jnp.bfloat16)
-    slots = len(shards)
+    near = ([] if taps is None else [taps]) + [here(part) if slots > 1 else part for part in parts]
+    tails = [] if into is None else [into]
     return pl.pallas_call(
         functools.partial(
-            maps_kernel, shards=slots, views=views, channels=channels, first=first, per_dev=per_dev, begun=begun
+            write_kernel,
+            parts=len(parts),
+            channels=channels,
+            with_taps=len(near) - len(parts),
+            begun=len(tails),
         ),
-        out_shape=(jax.ShapeDtypeStruct(shape, jnp.float32),) + (sent,) * (views - 1),
-        in_specs=[pl.BlockSpec(memory_space=pltpu.SMEM), vmem] + [any_space] * (len(operands) - 2),
-        out_specs=(any_space,) + (vmem,) * (views - 1),
-        scratch_shapes=[
-            pltpu.VMEM((slots, depth, wide), jnp.bfloat16),
-            pltpu.VMEM((slots, beams, channels, pixels), jnp.float32),
-            pltpu.SemaphoreType.DMA((slots,)),
-            pltpu.SemaphoreType.DMA((slots,)),
-        ],
-        input_output_aliases={2 + slots: 0} if begun else {},
-        name="maps",
-    )(*operands)
-
-
-def place_kernel(ids_ref, *refs, parts, channels, first, per_dev):
-    part_refs = refs[:parts]
-    out_ref, buf, sem = refs[parts + 1], refs[-2], refs[-1]
-    each = part_refs[0].shape[0]
-
-    def emit(slot):
-        row = pl.multiple_of(ids_ref[slot] * per_dev + first, channels)
-        return pltpu.make_async_copy(buf.at[slot], out_ref.at[:, pl.ds(row, channels)], sem.at[slot])
-
-    for op, part in enumerate(part_refs):
-        for i in range(each):
-            slot = op * each + i
-            buf[slot] = part[i].astype(jnp.float32).reshape(buf.shape[1:])
-            emit(slot).start()
-    for slot in range(parts * each):
-        emit(slot).wait()
-
-
-def place_maps(ids, parts, into, channels, first, per_dev):
-    beams, _, pixels = into.shape
-    slots = len(parts) * parts[0].shape[0]
-    any_space = pl.BlockSpec(memory_space=pl.ANY)
-    return pl.pallas_call(
-        functools.partial(place_kernel, parts=len(parts), channels=channels, first=first, per_dev=per_dev),
-        out_shape=jax.ShapeDtypeStruct(into.shape, jnp.float32),
+        out_shape=jax.ShapeDtypeStruct(shape, jnp.float32),
         in_specs=[pl.BlockSpec(memory_space=pltpu.SMEM)]
-        + [pl.BlockSpec(memory_space=pltpu.VMEM)] * len(parts)
-        + [any_space],
+        + [pl.BlockSpec(memory_space=pltpu.VMEM)] * len(near)
+        + [any_space] * len(tails),
         out_specs=any_space,
         scratch_shapes=[
             pltpu.VMEM((slots, beams, channels, pixels), jnp.float32),
             pltpu.SemaphoreType.DMA((slots,)),
         ],
-        input_output_aliases={1 + len(parts): 0},
-        name="place",
-    )(ids, *parts, into)
+        input_output_aliases={1 + len(near): 0} if tails else {},
+        compiler_params=GRANT,
+        name="write",
+    )(rows, *near, *tails)
 
 
 def off_flags(moments, starts, range_len):
@@ -295,14 +300,17 @@
     return jnp.any(inside, axis=0)
 
 
-def sum_over(value, axis, devices):
+def sum_over(value, devices, lines):
     if devices & (devices - 1):
-        return lax.psum(value, axis)
+        return lax.psum(value, "tm")
     step = 1
-    while step < devices:
-        moved = lax.ppermute(value, axis, [(i, i ^ step) for i in range(devices)])
+    while step < (4 if lines else devices):
+        moved = crossed(value, step, devices)
         value = value + moved
         step *= 2
+    if lines:
+        moved = [turned(value, shift, devices) for shift in (4, 12, 8)]
+        value = (value + moved[0]) + (moved[1] + moved[2])
     return value
 
 
@@ -312,12 +320,6 @@
 
 def crossed(value, bits, count):
     return lax.ppermute(value, "tm", [(i, i ^ bits) for i in range(count)])
-
-
-def other_parts(ordered, full):
-    half = LANES // 2
-    real, imag, tails = ordered[:full], ordered[full : 2 * full], ordered[2 * full :]
-    return jnp.concatenate([imag, -real, tails[half:], -tails[:half]], axis=0)
 
 
 def on_device(voltages, off_starts, pointing, patterns):
@@ -338,11 +340,12 @@
     pixel_ids = position * pixels + jnp.arange(pixels, dtype=jnp.int32)
     selector = (pointing[:, None] == pixel_ids[None, :]).astype(jnp.bfloat16)
     steer_local = jnp.einsum("bx,lx->bl", selector, ordered, preferred_element_type=jnp.float32)
-    steering = sum_over(steer_local.astype(jnp.bfloat16), "tm", devices)
-
-    packed = lane_order(voltages[:, :, 0], voltages[:, :, 1], 2)
-    blocks = packed.reshape(devices, per_dev, samples_dev, packed.shape[-1])
     lines = devices == 16 and per_dev % (8 * CHUNKS) == 0
+    steering = sum_over(steer_local.astype(jnp.bfloat16), devices, lines)
+
+    wide = 2 * full + LANES
+    packed = jnp.einsum("ctrp,rpl->ctl", voltages, lane_places(ports), preferred_element_type=jnp.float32)
+    blocks = packed.astype(jnp.bfloat16).reshape(devices, per_dev, samples_dev, wide)
     chunks = CHUNKS if lines else 1
     part = per_dev // chunks
     shape = (beams, channels, pixels)
@@ -351,10 +354,9 @@
     for i in range(chunks):
         block = blocks[:, i * part : (i + 1) * part]
         arrived.append(lax.all_to_all(block, "tm", split_axis=0, concat_axis=0, tiled=True))
-    taps = [ordered]
+    near = (2, 3, 1)
     if lines:
-        taps += [crossed(ordered, bits, devices) for bits in (1, 2, 3)]
-    taps = jnp.concatenate([t for o in taps for t in (o, other_parts(o, full))], axis=1)
+        others = [crossed(ordered, bits, devices) for bits in near]
 
     outs = []
     for block in arrived:
@@ -364,20 +366,22 @@
     if lines:
         shifts = (0, 4, 12, 8)
         sources = jnp.stack([(position - shift) % devices for shift in shifts]).astype(jnp.int32)
-        maps = None
+        near_sources = jnp.concatenate([sources ^ bits for bits in near])
+        held = []
         sent = []
-        for i, (payload, _) in enumerate(outs):
+        for payload, _ in outs:
             shards = [payload] + [turned(payload, shift, devices) for shift in shifts[1:]]
-            maps, *away = beam_power(
-                sources, taps, [shard[None] for shard in shards], maps, shape, part, i * part, per_dev
-            )
-            sent.append([crossed(away[bits - 1], bits, devices) for bits in (2, 3, 1)])
-        places = jnp.concatenate([sources ^ bits for bits in (2, 3, 1)])
+            gone = away_maps(others, shards)
+            sent.append([crossed(value, bits, devices) for value, bits in zip(gone, near)])
+            held += [shard[None] for shard in shards]
+        rows = jnp.concatenate([sources * per_dev + i * part for i in range(chunks)])
+        maps = write_maps(rows, held, None, shape, part, ordered)
         for i, parts in enumerate(sent):
-            maps = place_maps(places, parts, maps, part, i * part, per_dev)
+            maps = write_maps(near_sources * per_dev + i * part, parts, maps, shape, part)
     else:
         collected = lax.all_gather(outs[0][0], "tm", axis=0, tiled=False)
-        (maps,) = beam_power(jnp.arange(devices, dtype=jnp.int32), taps, [collected], None, shape, part, 0, per_dev)
+        rows = jnp.arange(devices, dtype=jnp.int32) * per_dev
+        maps = write_maps(rows, [collected], None, shape, part, ordered)
     return (flat_pair, maps.transpose(1, 0, 2))
 
 

time: 165 us -> 151 us (0.915)
  the two profiles are of different devices: /device:TPU:13 before, /device:TPU:0 now
where the time goes in v3:
time: 151 us; the launch traced here: 149 us
  waiting for transfers between devices  60.1 us (40%)
  Pallas kernels  37.3 us (25%)
  starting transfers between devices  36.9 us (24%)
  local copies, waits for them, and re-layouts  10.3 us (7%)
  other arithmetic  2.08 us (1%)
    ppermute x9, waiting for transfers between devices, turned(): lax.ppermute(value, 'tm', [(i, (i + shift) % count) for i in range(count)])  30.6 us
    pallas_call x2, Pallas kernels, power_weights(): pl.pallas_call(functools.partial(power_kernel, ports=ports, group=group),...  25.4 us
    all_to_all x2, waiting for transfers between devices, on_device(): lax.all_to_all(block, 'tm', split_axis=0, concat_axis=0, tiled=True)  18.5 us
    ppermute x9, starting transfers between devices, turned(): lax.ppermute(value, 'tm', [(i, (i + shift) % count) for i in range(count)])  15.2 us
    all_to_all x2, starting transfers between devices, on_device(): lax.all_to_all(block, 'tm', split_axis=0, concat_axis=0, tiled=True)  12.9 us
    ppermute x11, waiting for transfers between devices, crossed(): return lax.ppermute(value, 'tm', [(i, i ^ bits) for i in range(count)])  11 us
    ppermute x11, starting transfers between devices, crossed(): return lax.ppermute(value, 'tm', [(i, i ^ bits) for i in range(count)])  8.77 us
    pallas_call x3, Pallas kernels, write_maps(): pl.pallas_call(functools.partial(write_kernel, parts=len(parts), channels...  7.02 us
  transfers between devices with their start and end apart: 22, of which 11 were waited for; matrix products, arithmetic and copies ran while one was open for 4% of the time, Pallas kernels for 23%

profile of v3, /device:TPU:0, one launch (start us, length us, event | category | flops | bytes accessed | tf_op | source)
XLA Modules:
  0.0 149.1 jit_solution(6820314769146868717)
XLA Ops:
  0.8 1.3 copy-done
  2.0 1.2 fusion.1
  4.2 1.3 fusion.12
  5.5 7.5 %all-to-all-start = ((bf16[16,8,8,384]{3,2,1,0:T(8,128)(2,1)}), bf16[16,8,8,384]{3,2,1,0:T(8,128)(2,1)S(1)}, u32[]{:S(2)}, u32[]{:S(2)}) async-start(bf16[16,8,8,384]{3,2,1,0:T(8,128)(2,1)} %get-tuple-element.30), calls=%async_computation | async-start | bytes 1572864 | tf_op jit(solution)/shard_map/all_to_all | solution.py:356
  13.3 18.5 %all-to-all-done.arr_ref = bf16[16,8,8,384]{3,2,1,0:T(8,128)(2,1)S(1)} async-done(((bf16[16,8,8,384]{3,2,1,0:T(8,128)(2,1)}), bf16[16,8,8,384]{3,2,1,0:T(8,128)(2,1)S(1)}, u32[]{:S(2)}, u32[]{:S(2)}) %all-to-all-start) | async-done | bytes 786464 | tf_op jit(solution)/shard_map/all_to_all | solution.py:356
  31.7 5.4 %all-to-all-start.1 = ((bf16[16,8,8,384]{3,2,1,0:T(8,128)(2,1)}), bf16[16,8,8,384]{3,2,1,0:T(8,128)(2,1)S(1)}, u32[]{:S(2)}, u32[]{:S(2)}) async-start(bf16[16,8,8,384]{3,2,1,0:T(8,128)(2,1)} %get-tuple-element.31), calls=%async_computation.1 | async-start | bytes 1572864 | tf_op jit(solution)/shard_map/all_to_all | solution.py:356
  38.8 1.9 %collective-permute-start.1 = (bf16[36,384]{1,0:T(8,128)(2,1)S(1)}, bf16[36,384]{1,0:T(8,128)(2,1)S(1)}, u32[]{:S(2)}, u32[]{:S(2)}) collective-permute-start(bf16[36,384]{1,0:T(8,128)(2,1)S(1)} %add.103), channel_id=1, source_target_pairs={{0,2},{1,3},{2,0},{3,1},{4,6},{5,7},{6,4},{7,5},{8,10},{9,11},{10,... | collective-permute-start | bytes 82952 | tf_op jit(solution)/shard_map/ppermute | solution.py:322
  40.8 3.9 %collective-permute-done.1 = bf16[36,384]{1,0:T(8,128)(2,1)S(1)} collective-permute-done((bf16[36,384]{1,0:T(8,128)(2,1)S(1)}, bf16[36,384]{1,0:T(8,128)(2,1)S(1)}, u32[]{:S(2)}, u32[]{:S(2)}) %collective-permute-start.1) | collective-permute-done | bytes 27680 | tf_op jit(solution)/shard_map/ppermute | solution.py:322
  44.8 2.0 %collective-permute-start.4 = (bf16[36,384]{1,0:T(8,128)(2,1)S(1)}, bf16[36,384]{1,0:T(8,128)(2,1)S(1)}, u32[]{:S(2)}, u32[]{:S(2)}) collective-permute-start(bf16[36,384]{1,0:T(8,128)(2,1)S(1)} %add.104), channel_id=1, source_target_pairs={{0,8},{1,9},{2,10},{3,11},{4,12},{5,13},{6,14},{7,15},{8,0},{9,1},... | collective-permute-start | bytes 82952 | tf_op jit(solution)/shard_map/ppermute | solution.py:318
  46.7 2.6 %collective-permute-start.3 = (bf16[36,384]{1,0:T(8,128)(2,1)S(1)}, bf16[36,384]{1,0:T(8,128)(2,1)S(1)}, u32[]{:S(2)}, u32[]{:S(2)}) collective-permute-start(bf16[36,384]{1,0:T(8,128)(2,1)S(1)} %add.104), channel_id=1, source_target_pairs={{0,12},{1,13},{2,14},{3,15},{4,0},{5,1},{6,2},{7,3},{8,4},{9,5},{1... | collective-permute-start | bytes 82952 | tf_op jit(solution)/shard_map/ppermute | solution.py:318
  50.6 9.8 %collective-permute-done.4 = bf16[36,384]{1,0:T(8,128)(2,1)S(1)} collective-permute-done((bf16[36,384]{1,0:T(8,128)(2,1)S(1)}, bf16[36,384]{1,0:T(8,128)(2,1)S(1)}, u32[]{:S(2)}, u32[]{:S(2)}) %collective-permute-start.4) | collective-permute-done | bytes 27680 | tf_op jit(solution)/shard_map/ppermute | solution.py:318
  60.4 12.7 %power.2 = (bf16[288,384]{1,0:T(8,128)(2,1)S(1)}, bf16[8,2,36,188]{3,2,1,0:T(8,128)(2,1)S(1)}) custom-call(bf16[16,8,8,384]{3,2,1,0:T(8,128)(2,1)S(1)} %all-to-all-done.arr_ref, f32[128,1]{1,0:T(8,128)S(1)} %copy.32.on_ref, f32[1,1]{1,0:T(1,128)} %bitcast.6.count_ref, bf16[36,384]{1,0:T(8,128)(2,1)S(1)} %add_add_fusion.steer_ref), custom_call_target="tpu_custom_call" | custom-call | tf_op jit(solution)/shard_map/power/pallas_call | solution.py:169
  74.6 2.4 %collective-permute-start.15 = (bf16[288,384]{1,0:T(8,128)(2,1)S(1)}, bf16[288,384]{1,0:T(8,128)(2,1)S(1)}, u32[]{:S(2)}, u32[]{:S(2)}) collective-permute-start(bf16[288,384]{1,0:T(8,128)(2,1)S(1)} %get-tuple-element.18.refs_0_), channel_id=1, source_target_pairs={{0,12},{1,13},{2,14},{3,15},{4,0},{5,1},{6,2},{7,3},{8,4},{9,5},{1... | collective-permute-start | bytes 663560 | tf_op jit(solution)/shard_map/ppermute | solution.py:318
  77.0 1.6 %collective-permute-start.9 = (bf16[384,128]{1,0:T(8,128)(2,1)S(1)}, bf16[384,128]{1,0:T(8,128)(2,1)}, u32[]{:S(2)}, u32[]{:S(2)}) collective-permute-start(bf16[384,128]{1,0:T(8,128)(2,1)S(1)} %concatenate.12.refs_0_), channel_id=1, source_target_pairs={{0,3},{1,2},{2,1},{3,0},{4,7},{5,6},{6,5},{7,4},{8,11},{9,10},{10,... | collective-permute-start | bytes 294920 | tf_op jit(solution)/shard_map/ppermute | solution.py:322
  78.6 1.2 collective-permute-start.8
  79.8 2.0 %collective-permute-done.9.refs_5_ = bf16[384,128]{1,0:T(8,128)(2,1)} collective-permute-done((bf16[384,128]{1,0:T(8,128)(2,1)S(1)}, bf16[384,128]{1,0:T(8,128)(2,1)}, u32[]{:S(2)}, u32[]{:S(2)}) %collective-permute-start.9) | collective-permute-done | bytes 98336 | tf_op jit(solution)/shard_map/ppermute | solution.py:322
  81.8 2.5 %collective-permute-done.8.refs_4_ = bf16[384,128]{1,0:T(8,128)(2,1)} collective-permute-done((bf16[384,128]{1,0:T(8,128)(2,1)S(1)}, bf16[384,128]{1,0:T(8,128)(2,1)}, u32[]{:S(2)}, u32[]{:S(2)}) %collective-permute-start.8) | collective-permute-done | bytes 98336 | tf_op jit(solution)/shard_map/ppermute | solution.py:322
  84.3 3.8 %collective-permute-done.16.refs_3_ = bf16[288,384]{1,0:T(8,128)(2,1)S(1)} collective-permute-done((bf16[288,384]{1,0:T(8,128)(2,1)S(1)}, bf16[288,384]{1,0:T(8,128)(2,1)S(1)}, u32[]{:S(2)}, u32[]{:S(2)}) %collective-permute-start.16) | collective-permute-done | bytes 221216 | tf_op jit(solution)/shard_map/ppermute | solution.py:318
  88.1 3.1 %collective-permute-done.14.refs_1_ = bf16[288,384]{1,0:T(8,128)(2,1)S(1)} collective-permute-done((bf16[288,384]{1,0:T(8,128)(2,1)S(1)}, bf16[288,384]{1,0:T(8,128)(2,1)S(1)}, u32[]{:S(2)}, u32[]{:S(2)}) %collective-permute-start.14) | collective-permute-done | bytes 221216 | tf_op jit(solution)/shard_map/ppermute | solution.py:318
  91.2 2.1 %away.3 = (bf16[4,288,128]{2,1,0:T(8,128)(2,1)}, bf16[4,288,128]{2,1,0:T(8,128)(2,1)S(1)}, bf16[4,288,128]{2,1,0:T(8,128)(2,1)S(1)}) custom-call(bf16[288,384]{1,0:T(8,128)(2,1)S(1)} %get-tuple-element.18.refs_0_, bf16[288,384]{1,0:T(8,128)(2,1)S(1)} %collective-permute-done.14.refs_1_, bf16[288,384]{1,0:T(8,128)(2,1)S(1)} %collective-permute-done.15.refs_2_, ...), custom_call_target="tpu_custom_call" | custom-call | tf_op jit(solution)/shard_map/away/pallas_call | solution.py:222
  93.3 1.5 collective-permute-start.17
  96.5 12.7 %power.3 = (bf16[288,384]{1,0:T(8,128)(2,1)S(1)}, bf16[8,2,36,188]{3,2,1,0:T(8,128)(2,1)S(1)}) custom-call(bf16[16,8,8,384]{3,2,1,0:T(8,128)(2,1)S(1)} %all-to-all-done.1.arr_ref, f32[128,1]{1,0:T(8,128)S(1)} %copy-done.4, f32[1,1]{1,0:T(1,128)} %bitcast.6.count_ref, bf16[36,384]{1,0:T(8,128)(2,1)S(1)} %copy-done.10), custom_call_target="tpu_custom_call" | custom-call | tf_op jit(solution)/shard_map/power/pallas_call | solution.py:169
  109.2 4.7 %collective-permute-start.7 = (bf16[288,384]{1,0:T(8,128)(2,1)S(1)}, bf16[288,384]{1,0:T(8,128)(2,1)S(1)}, u32[]{:S(2)}, u32[]{:S(2)}) collective-permute-start(bf16[288,384]{1,0:T(8,128)(2,1)S(1)} %get-tuple-element.14.refs_0_), channel_id=1, source_target_pairs={{0,8},{1,9},{2,10},{3,11},{4,12},{5,13},{6,14},{7,15},{8,0},{9,1},... | collective-permute-start | bytes 663560 | tf_op jit(solution)/shard_map/ppermute | solution.py:318
  113.8 2.3 %collective-permute-start.6 = (bf16[288,384]{1,0:T(8,128)(2,1)S(1)}, bf16[288,384]{1,0:T(8,128)(2,1)S(1)}, u32[]{:S(2)}, u32[]{:S(2)}) collective-permute-start(bf16[288,384]{1,0:T(8,128)(2,1)S(1)} %get-tuple-element.14.refs_0_), channel_id=1, source_target_pairs={{0,12},{1,13},{2,14},{3,15},{4,0},{5,1},{6,2},{7,3},{8,4},{9,5},{1... | collective-permute-start | bytes 663560 | tf_op jit(solution)/shard_map/ppermute | solution.py:318
  116.1 10.1 %collective-permute-done.7.refs_3_ = bf16[288,384]{1,0:T(8,128)(2,1)S(1)} collective-permute-done((bf16[288,384]{1,0:T(8,128)(2,1)S(1)}, bf16[288,384]{1,0:T(8,128)(2,1)S(1)}, u32[]{:S(2)}, u32[]{:S(2)}) %collective-permute-start.7) | collective-permute-done | bytes 221216 | tf_op jit(solution)/shard_map/ppermute | solution.py:318
  126.3 3.9 %collective-permute-done.5.refs_1_ = bf16[288,384]{1,0:T(8,128)(2,1)S(1)} collective-permute-done((bf16[288,384]{1,0:T(8,128)(2,1)S(1)}, bf16[288,384]{1,0:T(8,128)(2,1)S(1)}, u32[]{:S(2)}, u32[]{:S(2)}) %collective-permute-start.5) | collective-permute-done | bytes 221216 | tf_op jit(solution)/shard_map/ppermute | solution.py:318
  131.0 2.8 %away.2 = (bf16[4,288,128]{2,1,0:T(8,128)(2,1)}, bf16[4,288,128]{2,1,0:T(8,128)(2,1)}, bf16[4,288,128]{2,1,0:T(8,128)(2,1)}) custom-call(bf16[288,384]{1,0:T(8,128)(2,1)S(1)} %get-tuple-element.14.refs_0_, bf16[288,384]{1,0:T(8,128)(2,1)S(1)} %collective-permute-done.5.refs_1_, bf16[288,384]{1,0:T(8,128)(2,1)S(1)} %collective-permute-done.6.refs_2_, ...), custom_call_target="tpu_custom_call" | custom-call | tf_op jit(solution)/shard_map/away/pallas_call | solution.py:222
  137.1 3.1 %reshape.124 = bf16[16,2,6768]{2,1,0:T(2,128)(2,1)} reshape(bf16[16,2,36,188]{3,2,1,0:T(8,128)(2,1)} %pad_maximum_fusion) | data formatting | bytes 866304 | tf_op jit(solution)/shard_map/reshape | solution.py:365
  140.2 2.1 %write.3.refs_3_ = f32[36,256,128]{2,1,0:T(8,128)} custom-call(s32[8]{0:T(128)S(1)} %pad_add_fusion.1.rows_ref, bf16[384,128]{1,0:T(8,128)(2,1)S(1)} %copy-done.2, bf16[1,288,384]{2,1,0:T(8,128)(2,1)S(1)} %bitcast.36, bf16[1,288,384]{2,1,0:T(8,128)(2,1)S(1)} %bitcast.39, bf16[1,288,384]{2,1,0:T(8,128)(2,1)S(1)} %bitcast.38, ...), custom_call_target="tpu_custom_call" | custom-call | tf_op jit(solution)/shard_map/write/pallas_call | solution.py:275
  142.3 2.5 %write.4.refs_3_ = f32[36,256,128]{2,1,0:T(8,128)} custom-call(s32[12]{0:T(128)S(1)} %get-tuple-element.29.rows_ref, bf16[4,288,128]{2,1,0:T(8,128)(2,1)} %collective-permute-done.17.refs_0_, bf16[4,288,128]{2,1,0:T(8,128)(2,1)} %collective-permute-done.18.refs_1_, ...), custom_call_target="tpu_custom_call", output_to_operand_aliasing={{}: (4, {})} | custom-call | tf_op jit(solution)/shard_map/write/pallas_call | solution.py:275
  144.8 1.7 %collective-permute-done.12.refs_1_ = bf16[4,288,128]{2,1,0:T(8,128)(2,1)} collective-permute-done((bf16[4,288,128]{2,1,0:T(8,128)(2,1)}, bf16[4,288,128]{2,1,0:T(8,128)(2,1)}, u32[]{:S(2)}, u32[]{:S(2)}) %collective-permute-start.12) | collective-permute-done | bytes 294944 | tf_op jit(solution)/shard_map/ppermute | solution.py:322
  146.5 2.5 %write.5 = f32[36,256,128]{2,1,0:T(8,128)} custom-call(s32[12]{0:T(128)S(1)} %get-tuple-element.28.rows_ref, bf16[4,288,128]{2,1,0:T(8,128)(2,1)} %collective-permute-done.11.refs_0_, bf16[4,288,128]{2,1,0:T(8,128)(2,1)} %collective-permute-done.12.refs_1_, bf16[4,288,128]{2,1,0:T(8,128)(2,1)} %collective-permute-done.13.refs_2_, ...), custom_call_target="tpu_custom_call", output_to_operand_aliasing={{}: (4, {})} | custom-call | tf_op jit(solution)/shard_map/write/pallas_call | solution.py:275
  (79 shorter events, 11.7 us)
Async XLA Ops:
  5.5 7.6 %copy-start.13 = (bf16[2,188,128]{2,0,1:T(2,128)(2,1)S(1)}, bf16[2,188,128]{2,0,1:T(2,128)(2,1)}, u32[]{:S(2)}) copy-start(bf16[2,188,128]{2,0,1:T(2,128)(2,1)} %param.7) | copy-start | bytes 288772
  5.5 26.2 %all-to-all-start = ((bf16[16,8,8,384]{3,2,1,0:T(8,128)(2,1)}), bf16[16,8,8,384]{3,2,1,0:T(8,128)(2,1)S(1)}, u32[]{:S(2)}, u32[]{:S(2)}) async-start(bf16[16,8,8,384]{3,2,1,0:T(8,128)(2,1)} %get-tuple-element.30), calls=%async_computation | async-start | bytes 1572864 | tf_op jit(solution)/shard_map/all_to_all | solution.py:356
  13.1 24.2 %copy-start.14 = (s32[36]{0:T(128)S(1)}, s32[36]{0:T(128)}, u32[]{:S(2)}) copy-start(s32[36]{0:T(128)} %param.6) | copy-start | bytes 436
  13.1 24.9 %copy-start.15 = (s32[8]{0:T(128)S(1)}, s32[8]{0:T(128)}, u32[]{:S(2)}) copy-start(s32[8]{0:T(128)} %param.5) | copy-start | bytes 100
  31.7 63.1 %all-to-all-start.1 = ((bf16[16,8,8,384]{3,2,1,0:T(8,128)(2,1)}), bf16[16,8,8,384]{3,2,1,0:T(8,128)(2,1)S(1)}, u32[]{:S(2)}, u32[]{:S(2)}) async-start(bf16[16,8,8,384]{3,2,1,0:T(8,128)(2,1)} %get-tuple-element.31), calls=%async_computation.1 | async-start | bytes 1572864 | tf_op jit(solution)/shard_map/all_to_all | solution.py:356
  37.3 57.6 %copy-start.1 = (bf16[384,128]{1,0:T(8,128)(2,1)}, bf16[384,128]{1,0:T(8,128)(2,1)S(1)}, u32[]{:S(2)}) copy-start(bf16[384,128]{1,0:T(8,128)(2,1)S(1)} %concatenate.12.refs_0_) | copy-start | bytes 294916
  37.5 1.3 collective-permute-start
  38.8 5.9 %collective-permute-start.1 = (bf16[36,384]{1,0:T(8,128)(2,1)S(1)}, bf16[36,384]{1,0:T(8,128)(2,1)S(1)}, u32[]{:S(2)}, u32[]{:S(2)}) collective-permute-start(bf16[36,384]{1,0:T(8,128)(2,1)S(1)} %add.103), channel_id=1, source_target_pairs={{0,2},{1,3},{2,0},{3,1},{4,6},{5,7},{6,4},{7,5},{8,10},{9,11},{10,... | collective-permute-start | bytes 82952 | tf_op jit(solution)/shard_map/ppermute | solution.py:322
  44.8 15.6 %collective-permute-start.4 = (bf16[36,384]{1,0:T(8,128)(2,1)S(1)}, bf16[36,384]{1,0:T(8,128)(2,1)S(1)}, u32[]{:S(2)}, u32[]{:S(2)}) collective-permute-start(bf16[36,384]{1,0:T(8,128)(2,1)S(1)} %add.104), channel_id=1, source_target_pairs={{0,8},{1,9},{2,10},{3,11},{4,12},{5,13},{6,14},{7,15},{8,0},{9,1},... | collective-permute-start | bytes 82952 | tf_op jit(solution)/shard_map/ppermute | solution.py:318
  46.7 13.6 %collective-permute-start.3 = (bf16[36,384]{1,0:T(8,128)(2,1)S(1)}, bf16[36,384]{1,0:T(8,128)(2,1)S(1)}, u32[]{:S(2)}, u32[]{:S(2)}) collective-permute-start(bf16[36,384]{1,0:T(8,128)(2,1)S(1)} %add.104), channel_id=1, source_target_pairs={{0,12},{1,13},{2,14},{3,15},{4,0},{5,1},{6,2},{7,3},{8,4},{9,5},{1... | collective-permute-start | bytes 82952 | tf_op jit(solution)/shard_map/ppermute | solution.py:318
  49.3 11.1 %collective-permute-start.2 = (bf16[36,384]{1,0:T(8,128)(2,1)S(1)}, bf16[36,384]{1,0:T(8,128)(2,1)S(1)}, u32[]{:S(2)}, u32[]{:S(2)}) collective-permute-start(bf16[36,384]{1,0:T(8,128)(2,1)S(1)} %add.104), channel_id=1, source_target_pairs={{0,4},{1,5},{2,6},{3,7},{4,8},{5,9},{6,10},{7,11},{8,12},{9,13},{1... | collective-permute-start | bytes 82952 | tf_op jit(solution)/shard_map/ppermute | solution.py:318
  50.6 44.3 %copy-start.3 = (f32[128,1]{1,0:T(8,128)}, f32[128,1]{1,0:T(8,128)S(1)}, u32[]{:S(2)}) copy-start(f32[128,1]{1,0:T(8,128)S(1)} %copy.32.on_ref) | copy-start | bytes 1540
  60.3 18.2 %copy-start.9 = (bf16[36,384]{1,0:T(8,128)(2,1)}, bf16[36,384]{1,0:T(8,128)(2,1)S(1)}, u32[]{:S(2)}) copy-start(bf16[36,384]{1,0:T(8,128)(2,1)S(1)} %add_add_fusion.steer_ref) | copy-start | bytes 82948
  73.7 14.3 %collective-permute-start.16 = (bf16[288,384]{1,0:T(8,128)(2,1)S(1)}, bf16[288,384]{1,0:T(8,128)(2,1)S(1)}, u32[]{:S(2)}, u32[]{:S(2)}) collective-permute-start(bf16[288,384]{1,0:T(8,128)(2,1)S(1)} %get-tuple-element.18.refs_0_), channel_id=1, source_target_pairs={{0,8},{1,9},{2,10},{3,11},{4,12},{5,13},{6,14},{7,15},{8,0},{9,1},... | collective-permute-start | bytes 663560 | tf_op jit(solution)/shard_map/ppermute | solution.py:318
  74.6 13.5 %collective-permute-start.15 = (bf16[288,384]{1,0:T(8,128)(2,1)S(1)}, bf16[288,384]{1,0:T(8,128)(2,1)S(1)}, u32[]{:S(2)}, u32[]{:S(2)}) collective-permute-start(bf16[288,384]{1,0:T(8,128)(2,1)S(1)} %get-tuple-element.18.refs_0_), channel_id=1, source_target_pairs={{0,12},{1,13},{2,14},{3,15},{4,0},{5,1},{6,2},{7,3},{8,4},{9,5},{1... | collective-permute-start | bytes 663560 | tf_op jit(solution)/shard_map/ppermute | solution.py:318
  77.0 14.2 %collective-permute-start.14 = (bf16[288,384]{1,0:T(8,128)(2,1)S(1)}, bf16[288,384]{1,0:T(8,128)(2,1)S(1)}, u32[]{:S(2)}, u32[]{:S(2)}) collective-permute-start(bf16[288,384]{1,0:T(8,128)(2,1)S(1)} %get-tuple-element.18.refs_0_), channel_id=1, source_target_pairs={{0,4},{1,5},{2,6},{3,7},{4,8},{5,9},{6,10},{7,11},{8,12},{9,13},{1... | collective-permute-start | bytes 663560 | tf_op jit(solution)/shard_map/ppermute | solution.py:318
  77.0 1.6 %collective-permute-start.10 = (bf16[384,128]{1,0:T(8,128)(2,1)S(1)}, bf16[384,128]{1,0:T(8,128)(2,1)S(1)}, u32[]{:S(2)}, u32[]{:S(2)}) collective-permute-start(bf16[384,128]{1,0:T(8,128)(2,1)S(1)} %concatenate.12.refs_0_), channel_id=1, source_target_pairs={{0,1},{1,0},{2,3},{3,2},{4,5},{5,4},{6,7},{7,6},{8,9},{9,8},{10,11... | collective-permute-start | bytes 294920 | tf_op jit(solution)/shard_map/ppermute | solution.py:322
  77.0 4.8 %collective-permute-start.9 = (bf16[384,128]{1,0:T(8,128)(2,1)S(1)}, bf16[384,128]{1,0:T(8,128)(2,1)}, u32[]{:S(2)}, u32[]{:S(2)}) collective-permute-start(bf16[384,128]{1,0:T(8,128)(2,1)S(1)} %concatenate.12.refs_0_), channel_id=1, source_target_pairs={{0,3},{1,2},{2,1},{3,0},{4,7},{5,6},{6,5},{7,4},{8,11},{9,10},{10,... | collective-permute-start | bytes 294920 | tf_op jit(solution)/shard_map/ppermute | solution.py:322
  78.6 16.3 %copy-start.5 = (bf16[384,128]{1,0:T(8,128)(2,1)}, bf16[384,128]{1,0:T(8,128)(2,1)S(1)}, u32[]{:S(2)}) copy-start(bf16[384,128]{1,0:T(8,128)(2,1)S(1)} %collective-permute-done.10.refs_6_) | copy-start | bytes 294916
  78.6 5.7 %collective-permute-start.8 = (bf16[384,128]{1,0:T(8,128)(2,1)S(1)}, bf16[384,128]{1,0:T(8,128)(2,1)}, u32[]{:S(2)}, u32[]{:S(2)}) collective-permute-start(bf16[384,128]{1,0:T(8,128)(2,1)S(1)} %concatenate.12.refs_0_), channel_id=1, source_target_pairs={{0,2},{1,3},{2,0},{3,1},{4,6},{5,7},{6,4},{7,5},{8,10},{9,11},{10,... | collective-permute-start | bytes 294920 | tf_op jit(solution)/shard_map/ppermute | solution.py:322
  93.3 1.5 copy-start.12
  93.3 41.6 %collective-permute-start.17 = (bf16[4,288,128]{2,1,0:T(8,128)(2,1)}, bf16[4,288,128]{2,1,0:T(8,128)(2,1)}, u32[]{:S(2)}, u32[]{:S(2)}) collective-permute-start(bf16[4,288,128]{2,1,0:T(8,128)(2,1)} %get-tuple-element.19), channel_id=1, source_target_pairs={{0,2},{1,3},{2,0},{3,1},{4,6},{5,7},{6,4},{7,5},{8,10},{9,11},{10,... | collective-permute-start | bytes 884744 | tf_op jit(solution)/shard_map/ppermute | solution.py:322
  96.5 39.6 %copy-start.8 = (bf16[8,2,36,188]{3,2,1,0:T(8,128)(2,1)S(1)}, bf16[8,2,36,188]{3,2,1,0:T(8,128)(2,1)}, u32[]{:S(2)}) copy-start(bf16[8,2,36,188]{3,2,1,0:T(8,128)(2,1)} %copy-done.7) | copy-start | bytes 649732
  109.2 17.1 %collective-permute-start.7 = (bf16[288,384]{1,0:T(8,128)(2,1)S(1)}, bf16[288,384]{1,0:T(8,128)(2,1)S(1)}, u32[]{:S(2)}, u32[]{:S(2)}) collective-permute-start(bf16[288,384]{1,0:T(8,128)(2,1)S(1)} %get-tuple-element.14.refs_0_), channel_id=1, source_target_pairs={{0,8},{1,9},{2,10},{3,11},{4,12},{5,13},{6,14},{7,15},{8,0},{9,1},... | collective-permute-start | bytes 663560 | tf_op jit(solution)/shard_map/ppermute | solution.py:318
  113.8 12.4 %collective-permute-start.6 = (bf16[288,384]{1,0:T(8,128)(2,1)S(1)}, bf16[288,384]{1,0:T(8,128)(2,1)S(1)}, u32[]{:S(2)}, u32[]{:S(2)}) collective-permute-start(bf16[288,384]{1,0:T(8,128)(2,1)S(1)} %get-tuple-element.14.refs_0_), channel_id=1, source_target_pairs={{0,12},{1,13},{2,14},{3,15},{4,0},{5,1},{6,2},{7,3},{8,4},{9,5},{1... | collective-permute-start | bytes 663560 | tf_op jit(solution)/shard_map/ppermute | solution.py:318
  116.1 14.0 %collective-permute-start.5 = (bf16[288,384]{1,0:T(8,128)(2,1)S(1)}, bf16[288,384]{1,0:T(8,128)(2,1)S(1)}, u32[]{:S(2)}, u32[]{:S(2)}) collective-permute-start(bf16[288,384]{1,0:T(8,128)(2,1)S(1)} %get-tuple-element.14.refs_0_), channel_id=1, source_target_pairs={{0,4},{1,5},{2,6},{3,7},{4,8},{5,9},{6,10},{7,11},{8,12},{9,13},{1... | collective-permute-start | bytes 663560 | tf_op jit(solution)/shard_map/ppermute | solution.py:318
  116.1 26.2 %collective-permute-start.18 = (bf16[4,288,128]{2,1,0:T(8,128)(2,1)}, bf16[4,288,128]{2,1,0:T(8,128)(2,1)}, u32[]{:S(2)}, u32[]{:S(2)}) collective-permute-start(bf16[4,288,128]{2,1,0:T(8,128)(2,1)} %copy-done.12), channel_id=1, source_target_pairs={{0,3},{1,2},{2,1},{3,0},{4,7},{5,6},{6,5},{7,4},{8,11},{9,10},{10,... | collective-permute-start | bytes 884744 | tf_op jit(solution)/shard_map/ppermute | solution.py:322
  126.3 13.9 %copy-start.2 = (bf16[384,128]{1,0:T(8,128)(2,1)S(1)}, bf16[384,128]{1,0:T(8,128)(2,1)}, u32[]{:S(2)}) copy-start(bf16[384,128]{1,0:T(8,128)(2,1)} %copy-done.1) | copy-start | bytes 294916
  126.3 16.0 %collective-permute-start.19 = (bf16[4,288,128]{2,1,0:T(8,128)(2,1)}, bf16[4,288,128]{2,1,0:T(8,128)(2,1)}, u32[]{:S(2)}, u32[]{:S(2)}) collective-permute-start(bf16[4,288,128]{2,1,0:T(8,128)(2,1)} %copy-done.11), channel_id=1, source_target_pairs={{0,1},{1,0},{2,3},{3,2},{4,5},{5,4},{6,7},{7,6},{8,9},{9,8},{10,11... | collective-permute-start | bytes 884744 | tf_op jit(solution)/shard_map/ppermute | solution.py:322
  133.8 11.0 %collective-permute-start.11 = (bf16[4,288,128]{2,1,0:T(8,128)(2,1)}, bf16[4,288,128]{2,1,0:T(8,128)(2,1)}, u32[]{:S(2)}, u32[]{:S(2)}) collective-permute-start(bf16[4,288,128]{2,1,0:T(8,128)(2,1)} %get-tuple-element.15), channel_id=1, source_target_pairs={{0,2},{1,3},{2,0},{3,1},{4,6},{5,7},{6,4},{7,5},{8,10},{9,11},{10,... | collective-permute-start | bytes 884744 | tf_op jit(solution)/shard_map/ppermute | solution.py:322
  134.9 11.6 %collective-permute-start.12 = (bf16[4,288,128]{2,1,0:T(8,128)(2,1)}, bf16[4,288,128]{2,1,0:T(8,128)(2,1)}, u32[]{:S(2)}, u32[]{:S(2)}) collective-permute-start(bf16[4,288,128]{2,1,0:T(8,128)(2,1)} %get-tuple-element.16), channel_id=1, source_target_pairs={{0,3},{1,2},{2,1},{3,0},{4,7},{5,6},{6,5},{7,4},{8,11},{9,10},{10,... | collective-permute-start | bytes 884744 | tf_op jit(solution)/shard_map/ppermute | solution.py:322
  134.9 11.6 %collective-permute-start.13 = (bf16[4,288,128]{2,1,0:T(8,128)(2,1)}, bf16[4,288,128]{2,1,0:T(8,128)(2,1)}, u32[]{:S(2)}, u32[]{:S(2)}) collective-permute-start(bf16[4,288,128]{2,1,0:T(8,128)(2,1)} %get-tuple-element.17), channel_id=1, source_target_pairs={{0,1},{1,0},{2,3},{3,2},{4,5},{5,4},{6,7},{7,6},{8,9},{9,8},{10,11... | collective-permute-start | bytes 884744 | tf_op jit(solution)/shard_map/ppermute | solution.py:322
  (6 other events, 6.1 us)

commit v4 on v3

--- a/solution.py
+++ b/solution.py
@@ -12,8 +12,8 @@
 LANES = 128
 SUB = 8
 PAIR = 16
-TURNS = 3
-GRANT = pltpu.CompilerParams(vmem_limit_bytes=28 << 20)
+TURNS = 9
+GRANT = pltpu.CompilerParams(vmem_limit_bytes=14 << 20)
 MAP_SLOTS = 16
 CHUNKS = 2
 
@@ -50,10 +50,11 @@
 
 
 def power_kernel(
-    arr_ref, on_ref, count_ref, steer_ref, pay_ref, flat_ref, volt_ref, voltt_ref, scale_ref, lhs_ref, pay_sc, *, ports, group
+    arr_ref, starts_ref, *refs, ports, group, span
 ):
+    steer_refs, (pay_ref, flat_ref, volt_ref, voltt_ref, scale_ref, lhs_ref, pay_sc) = refs[:-7], refs[-7:]
     _, channels, _, wide = arr_ref.shape
-    beams = steer_ref.shape[0]
+    beams = steer_refs[0].shape[0]
     rows = volt_ref.shape[1] // 2
     full = ports // LANES * LANES
     width = full + LANES
@@ -65,11 +66,17 @@
             return block
         return jnp.concatenate([block, jnp.zeros((pad - beams, width), jnp.float32)], axis=0)
 
-    steer_real, steer_imag = split_lanes(steer_ref[...].astype(jnp.float32), full)
+    steer_real, steer_imag = split_lanes(sum(ref[...].astype(jnp.float32) for ref in steer_refs), full)
     steer_real = padded(jnp.where(valid, steer_real, 0.0))
     steer_imag = padded(jnp.where(valid, steer_imag, 0.0))
     energy = steer_real * steer_real + steer_imag * steer_imag
-    on = on_ref[...]
+    moment = lax.broadcasted_iota(jnp.int32, (rows, LANES), 0)
+    off = jnp.zeros((rows, LANES), jnp.float32)
+    for i in range(starts_ref.shape[0]):
+        start = starts_ref[i]
+        off = jnp.where((moment >= start) & (moment < start + span), 1.0, off)
+    on = jnp.concatenate([1.0 - off] * (wide // LANES), axis=1)
+    count = jnp.concatenate([jnp.sum(off, axis=0, keepdims=True)] * (width // LANES), axis=1)
 
     def store_pair(k, both):
         high = both.astype(jnp.bfloat16)
@@ -87,7 +94,7 @@
         gone = block - kept
         power = jnp.sum(gone * gone, axis=0, keepdims=True)
         power_real, power_imag = split_lanes(power, full)
-        noise = (power_real + power_imag) / count_ref[0, 0] + 1e-06
+        noise = (power_real + power_imag) / count + 1e-06
         real, imag = split_lanes(kept, full)
         both = jnp.concatenate([real, imag], axis=0)
         volt_ref[k] = both.astype(jnp.bfloat16)
@@ -157,9 +164,9 @@
     return pltpu.with_memory_space_constraint(value, pltpu.VMEM)
 
 
-def power_weights(arrived, on, count, steer, ports):
+def power_weights(arrived, starts, span, steer, ports):
     sources, channels, samples, wide = arrived.shape
-    beams = steer.shape[0]
+    beams = steer[0].shape[0]
     rows = sources * samples
     width = ports // LANES * LANES + LANES
     pad = -(-beams // SUB) * SUB
@@ -167,17 +174,16 @@
     while channels % group:
         group //= 2
     return pl.pallas_call(
-        functools.partial(power_kernel, ports=ports, group=group),
+        functools.partial(power_kernel, ports=ports, group=group, span=span),
         out_shape=(
             jax.ShapeDtypeStruct((beams * channels, wide), jnp.bfloat16),
             jax.ShapeDtypeStruct((channels, 2, beams, ports), jnp.bfloat16),
         ),
         in_specs=[
             pl.BlockSpec(memory_space=pltpu.VMEM),
-            pl.BlockSpec(memory_space=pltpu.VMEM),
             pl.BlockSpec(memory_space=pltpu.SMEM),
-            pl.BlockSpec(memory_space=pltpu.VMEM),
-        ],
+        ]
+        + [pl.BlockSpec(memory_space=pltpu.VMEM)] * len(steer),
         out_specs=(pl.BlockSpec(memory_space=pltpu.VMEM), pl.BlockSpec(memory_space=pltpu.VMEM)),
         scratch_shapes=[
             pltpu.VMEM((channels, 2 * rows, width), jnp.bfloat16),
@@ -188,7 +194,7 @@
         ],
         compiler_params=GRANT,
         name="power",
-    )(here(arrived), on, count, steer)
+    )(here(arrived), starts, *steer)
 
 
 def other_parts(ordered):
@@ -234,7 +240,7 @@
     part_refs = refs[with_taps : with_taps + parts]
     out_ref = refs[with_taps + parts + begun]
     buf, sem = refs[-2:]
-    each = part_refs[0].shape[0]
+    pieces = [(part, i) for part in part_refs for i in range(part.shape[0])]
     slots = buf.shape[0]
 
     def emit(step, slot):
@@ -245,9 +251,9 @@
         piece = view(piece, taps_ref[...]) if with_taps else piece.astype(jnp.float32)
         buf[slot] = piece.reshape(buf.shape[1:])
 
-    if slots == parts * each:
-        for step in range(slots):
-            work(part_refs[step // each][step % each], step)
+    if slots == len(pieces):
+        for step, (part, i) in enumerate(pieces):
+            work(part[i], step)
             emit(step, step).start()
         for step in range(slots):
             emit(step, step).wait()
@@ -260,12 +266,12 @@
             out.wait()
             return carry
 
-        lax.fori_loop(0, each, body, 0)
+        lax.fori_loop(0, len(pieces), body, 0)
 
 
 def write_maps(rows, parts, into, shape, channels, taps=None):
     beams, _, pixels = shape
-    slots = parts[0].shape[0] * len(parts)
+    slots = sum(part.shape[0] for part in parts)
     if slots > MAP_SLOTS:
         assert len(parts) == 1
         slots = 1
@@ -295,14 +301,9 @@
     )(rows, *near, *tails)
 
 
-def off_flags(moments, starts, range_len):
-    inside = (moments[None, :] >= starts[:, None]) & (moments[None, :] < starts[:, None] + range_len)
-    return jnp.any(inside, axis=0)
-
-
 def sum_over(value, devices, lines):
     if devices & (devices - 1):
-        return lax.psum(value, "tm")
+        return [lax.psum(value, "tm")]
     step = 1
     while step < (4 if lines else devices):
         moved = crossed(value, step, devices)
@@ -310,8 +311,8 @@
         step *= 2
     if lines:
         moved = [turned(value, shift, devices) for shift in (4, 12, 8)]
-        value = (value + moved[0]) + (moved[1] + moved[2])
-    return value
+        return [value] + moved
+    return [value]
 
 
 def turned(value, shift, count):
@@ -331,10 +332,6 @@
     full = ports // LANES * LANES
     total_time = samples_dev * devices
     off_span = max(4, total_time // 32)
-    is_off = off_flags(jnp.arange(total_time, dtype=jnp.int32), off_starts, off_span)
-    off_count = jnp.sum(is_off.astype(jnp.float32)).reshape(1, 1)
-    on = 1.0 - is_off.astype(jnp.float32)[:, None]
-
     pixels = patterns.shape[2]
     ordered = lane_order(patterns[0], patterns[1], 0)
     pixel_ids = position * pixels + jnp.arange(pixels, dtype=jnp.int32)
@@ -360,24 +357,49 @@
 
     outs = []
     for block in arrived:
-        outs.append(power_weights(block, on, off_count, steering, ports))
+        outs.append(power_weights(block, off_starts, off_span, steering, ports))
     weights = jnp.concatenate([w for _, w in outs], axis=0)
     flat_pair = weights.reshape(per_dev, 2, beams * ports)
     if lines:
-        shifts = (0, 4, 12, 8)
-        sources = jnp.stack([(position - shift) % devices for shift in shifts]).astype(jnp.int32)
-        near_sources = jnp.concatenate([sources ^ bits for bits in near])
+        own_rows = []
         held = []
         sent = []
-        for payload, _ in outs:
-            shards = [payload] + [turned(payload, shift, devices) for shift in shifts[1:]]
-            gone = away_maps(others, shards)
-            sent.append([crossed(value, bits, devices) for value, bits in zip(gone, near)])
+
+        def send(pieces):
+            gone = away_maps(others, [shard for shard, _ in pieces])
+            gone = [crossed(value, bits, devices) for value, bits in zip(gone, near)]
+            sent.append((gone, [spot for _, spot in pieces]))
+
+        waiting = []
+        for i, (payload, _) in enumerate(outs):
+            if i + 1 < chunks:
+                one, two = crossed(payload, 4, devices), crossed(payload, 8, devices)
+                three = crossed(two, 4, devices)
+                shards = [payload, one, two, three]
+                spots = [(position ^ bits, i * part) for bits in (0, 4, 8, 12)]
+                waiting += zip(shards, spots)
+            else:
+                shards = [payload] + [turned(payload, shift, devices) for shift in (8, 12, 4)]
+                spots = [((position - shift) % devices, i * part) for shift in (0, 8, 12, 4)]
+                pieces = list(zip(shards, spots))
+                send(waiting[:-1] + pieces[:1])
+                send(waiting[-1:])
+                send(pieces[1:])
             held += [shard[None] for shard in shards]
-        rows = jnp.concatenate([sources * per_dev + i * part for i in range(chunks)])
-        maps = write_maps(rows, held, None, shape, part, ordered)
-        for i, parts in enumerate(sent):
-            maps = write_maps(near_sources * per_dev + i * part, parts, maps, shape, part)
+            own_rows += [source * per_dev + offset for source, offset in spots]
+
+        last = len(sent) - 1
+        groups = [[(n, j) for n in range(last) for j in range(3)], [(last, 2), (last, 0)], [(last, 1)]]
+        own_rows = jnp.stack(own_rows).astype(jnp.int32)
+        near_rows = [
+            jnp.stack(
+                [(source ^ near[j]) * per_dev + offset for n, j in group for source, offset in sent[n][1]]
+            ).astype(jnp.int32)
+            for group in groups
+        ]
+        maps = write_maps(own_rows, held, None, shape, part, ordered)
+        for i, group in enumerate(groups):
+            maps = write_maps(near_rows[i], [sent[n][0][j] for n, j in group], maps, shape, part)
     else:
         collected = lax.all_gather(outs[0][0], "tm", axis=0, tiled=False)
         rows = jnp.arange(devices, dtype=jnp.int32) * per_dev

time: 151 us -> 143 us (0.947)
  blocking collectives: 0 us -> 27.4 us
  waiting for transfers between devices: 60.1 us -> 32.9 us
  starting transfers between devices: 36.9 us -> 25.3 us
  local copies, waits for them, and re-layouts: 10.3 us -> 15.5 us
  Pallas kernels: 37.3 us -> 35.5 us
    all_to_all x0 -> x1, blocking collectives: none -> 27.4 us  [on_device(): lax.all_to_all(block, 'tm', split_axis=0, concat_axis=0, tiled=True)]
    all_to_all x2 -> x1, waiting for transfers between devices: 18.5 us -> 0.01 us  [on_device(): lax.all_to_all(block, 'tm', split_axis=0, concat_axis=0, tiled=True)]
    ppermute x9 -> x6, waiting for transfers between devices: 30.6 us -> 18.9 us  [turned(): lax.ppermute(value, 'tm', [(i, (i + shift) % count) for i in range(count)])]
    all_to_all x2 -> x1, starting transfers between devices: 12.9 us -> 4.07 us  [on_device(): lax.all_to_all(block, 'tm', split_axis=0, concat_axis=0, tiled=True)]
    ppermute x9 -> x6, starting transfers between devices: 15.2 us -> 8.87 us  [turned(): lax.ppermute(value, 'tm', [(i, (i + shift) % count) for i in range(count)])]
    concatenate x1, local copies, waits for them, and re-layouts: 0.11 us -> 5 us  [lane_order(): jnp.concatenate([cut(real, 0, full), cut(imag, 0, full), cut(real, full,...]
    pallas_call x2, Pallas kernels: 25.4 us -> 21.2 us  [power_weights(): pl.pallas_call(functools.partial(power_kernel, ports=ports, group=group,...]
    ppermute x11 -> x17, starting transfers between devices: 8.77 us -> 12.4 us  [crossed(): return lax.ppermute(value, 'tm', [(i, i ^ bits) for i in range(count)])]
  transfers between devices with their start and end apart: 22 -> 24, of which waited for: 11 -> 8; matrix products, arithmetic and copies ran while one was open for 4% -> 8% of each run, Pallas kernels for 23% -> 24%
where the time goes in v4:
time: 143 us; the launch traced here: 142 us
  Pallas kernels  35.5 us (25%)
  waiting for transfers between devices  32.9 us (23%)
  blocking collectives  27.4 us (19%)
  starting transfers between devices  25.3 us (18%)
  local copies, waits for them, and re-layouts  15.5 us (11%)
  matrix products  2.32 us (2%)
  other arithmetic  2.22 us (2%)
    all_to_all x1, blocking collectives, on_device(): lax.all_to_all(block, 'tm', split_axis=0, concat_axis=0, tiled=True)  27.4 us
    pallas_call x2, Pallas kernels, power_weights(): pl.pallas_call(functools.partial(power_kernel, ports=ports, group=group,...  21.2 us
    ppermute x6, waiting for transfers between devices, turned(): lax.ppermute(value, 'tm', [(i, (i + shift) % count) for i in range(count)])  18.9 us
    ppermute x17, waiting for transfers between devices, crossed(): return lax.ppermute(value, 'tm', [(i, i ^ bits) for i in range(count)])  14 us
    ppermute x17, starting transfers between devices, crossed(): return lax.ppermute(value, 'tm', [(i, i ^ bits) for i in range(count)])  12.4 us
    pallas_call x4, Pallas kernels, write_maps(): pl.pallas_call(functools.partial(write_kernel, parts=len(parts), channels...  8.93 us
    ppermute x6, starting transfers between devices, turned(): lax.ppermute(value, 'tm', [(i, (i + shift) % count) for i in range(count)])  8.87 us
    pallas_call x3, Pallas kernels, away_maps(): pl.pallas_call(functools.partial(away_kernel, shards=len(shards), views=v...  5.37 us
  transfers between devices with their start and end apart: 24, of which 8 were waited for; matrix products, arithmetic and copies ran while one was open for 8% of the time, Pallas kernels for 24%

profile of v4, /device:TPU:0, one launch (start us, length us, event | category | flops | bytes accessed | tf_op | source)
XLA Modules:
  0.0 142.4 jit_solution(11989840060011420359)
XLA Ops:
  0.8 1.3 copy-done
  2.0 1.2 fusion.1
  5.3 27.4 %all_to_all.10.arr_ref = bf16[16,8,8,384]{3,2,1,0:T(8,128)(2,1)S(1)} all-to-all(bf16[16,8,8,384]{3,2,1,0:T(8,128)(2,1)S(1)} %get-tuple-element.30), channel_id=1, replica_groups=mesh['groups'=2,'tm'=16] {'tm'}, dimensions={0} | all-to-all | bytes 1572864 | tf_op jit(solution)/shard_map/all_to_all | solution.py:353
  32.7 4.1 %all-to-all-start.1 = ((bf16[16,8,8,384]{3,2,1,0:T(8,128)(2,1)}), bf16[16,8,8,384]{3,2,1,0:T(8,128)(2,1)S(1)}, u32[]{:S(2)}, u32[]{:S(2)}) async-start(bf16[16,8,8,384]{3,2,1,0:T(8,128)(2,1)} %get-tuple-element.31), calls=%async_computation.1 | async-start | bytes 1572864 | tf_op jit(solution)/shard_map/all_to_all | solution.py:353
  37.0 5.0 %concatenate.6.refs_0_ = bf16[384,128]{1,0:T(8,128)(2,1)} concatenate(bf16[128,128]{1,0:T(8,128)(2,1)S(1)} %get-tuple-element.39, bf16[128,128]{1,0:T(8,128)(2,1)S(1)} %get-tuple-element.38, bf16[60,128]{1,0:T(8,128)(2,1)S(1)} %get-tuple-element.41, bf16[4,128]{1,0:T(4,128)(2,1)S(1)} %broadcast_in_dim.42, bf16[60,128]{1,0:T(8,128)(2,1)S(1)} %get-tuple-element.40, ...), dimensions={0} | concatenate | bytes 196608 | tf_op jit(solution)/shard_map/concatenate | solution.py:31
  42.0 1.1 convolution_convert_fusion
  44.5 1.8 %collective-permute-start.1 = (bf16[36,384]{1,0:T(8,128)(2,1)S(1)}, bf16[36,384]{1,0:T(8,128)(2,1)S(1)}, u32[]{:S(2)}, u32[]{:S(2)}) collective-permute-start(bf16[36,384]{1,0:T(8,128)(2,1)S(1)} %add.131), channel_id=1, source_target_pairs={{0,2},{1,3},{2,0},{3,1},{4,6},{5,7},{6,4},{7,5},{8,10},{9,11},{10,... | collective-permute-start | bytes 82952 | tf_op jit(solution)/shard_map/ppermute | solution.py:323
  46.3 2.5 %collective-permute-done.1 = bf16[36,384]{1,0:T(8,128)(2,1)S(1)} collective-permute-done((bf16[36,384]{1,0:T(8,128)(2,1)S(1)}, bf16[36,384]{1,0:T(8,128)(2,1)S(1)}, u32[]{:S(2)}, u32[]{:S(2)}) %collective-permute-start.1) | collective-permute-done | bytes 27680 | tf_op jit(solution)/shard_map/ppermute | solution.py:323
  48.8 2.7 %collective-permute-start.4 = (bf16[36,384]{1,0:T(8,128)(2,1)S(1)}, bf16[36,384]{1,0:T(8,128)(2,1)S(1)}, u32[]{:S(2)}, u32[]{:S(2)}) collective-permute-start(bf16[36,384]{1,0:T(8,128)(2,1)S(1)} %add.132.refs_0_), channel_id=1, source_target_pairs={{0,8},{1,9},{2,10},{3,11},{4,12},{5,13},{6,14},{7,15},{8,0},{9,1},... | collective-permute-start | bytes 82952 | tf_op jit(solution)/shard_map/ppermute | solution.py:319
  51.5 1.3 collective-permute-start.3
  53.5 6.4 %collective-permute-done.4.refs_3_ = bf16[36,384]{1,0:T(8,128)(2,1)S(1)} collective-permute-done((bf16[36,384]{1,0:T(8,128)(2,1)S(1)}, bf16[36,384]{1,0:T(8,128)(2,1)S(1)}, u32[]{:S(2)}, u32[]{:S(2)}) %collective-permute-start.4) | collective-permute-done | bytes 27680 | tf_op jit(solution)/shard_map/ppermute | solution.py:319
  60.0 10.6 %power.2 = (bf16[288,384]{1,0:T(8,128)(2,1)S(1)}, bf16[8,2,36,188]{3,2,1,0:T(8,128)(2,1)S(1)}) custom-call(bf16[16,8,8,384]{3,2,1,0:T(8,128)(2,1)S(1)} %all_to_all.10.arr_ref, s32[8]{0:T(128)S(1)} %copy-done.13, bf16[36,384]{1,0:T(8,128)(2,1)S(1)} %add.132.refs_0_, bf16[36,384]{1,0:T(8,128)(2,1)S(1)} %collective-permute-done.2.refs_1_, ...), custom_call_target="tpu_custom_call" | custom-call | tf_op jit(solution)/shard_map/power/pallas_call | solution.py:176
  71.5 1.2 collective-permute-start.14
  72.7 1.6 %collective-permute-start.9 = (bf16[384,128]{1,0:T(8,128)(2,1)}, bf16[384,128]{1,0:T(8,128)(2,1)S(1)}, u32[]{:S(2)}, u32[]{:S(2)}) collective-permute-start(bf16[384,128]{1,0:T(8,128)(2,1)} %concatenate.6.refs_0_), channel_id=1, source_target_pairs={{0,3},{1,2},{2,1},{3,0},{4,7},{5,6},{6,5},{7,4},{8,11},{9,10},{10,... | collective-permute-start | bytes 294920 | tf_op jit(solution)/shard_map/ppermute | solution.py:323
  74.8 7.7 %collective-permute-done.15.refs_2_ = bf16[288,384]{1,0:T(8,128)(2,1)S(1)} collective-permute-done((bf16[288,384]{1,0:T(8,128)(2,1)S(1)}, bf16[288,384]{1,0:T(8,128)(2,1)S(1)}, u32[]{:S(2)}, u32[]{:S(2)}) %collective-permute-start.15) | collective-permute-done | bytes 221216 | tf_op jit(solution)/shard_map/ppermute | solution.py:323
  86.4 10.6 %power.3 = (bf16[288,384]{1,0:T(8,128)(2,1)S(1)}, bf16[8,2,36,188]{3,2,1,0:T(8,128)(2,1)S(1)}) custom-call(bf16[16,8,8,384]{3,2,1,0:T(8,128)(2,1)S(1)} %all-to-all-done.1.arr_ref, s32[8]{0:T(128)S(1)} %copy-done.14, bf16[36,384]{1,0:T(8,128)(2,1)S(1)} %copy-done.4, bf16[36,384]{1,0:T(8,128)(2,1)S(1)} %copy-done.10, bf16[36,384]{1,0:T(8,128)(2,1)S(1)} %copy-done.8, ...), custom_call_target="tpu_custom_call" | custom-call | tf_op jit(solution)/shard_map/power/pallas_call | solution.py:176
  97.0 2.1 %collective-permute-start.7 = (bf16[288,384]{1,0:T(8,128)(2,1)S(1)}, bf16[288,384]{1,0:T(8,128)(2,1)S(1)}, u32[]{:S(2)}, u32[]{:S(2)}) collective-permute-start(bf16[288,384]{1,0:T(8,128)(2,1)S(1)} %get-tuple-element.17.refs_3_), channel_id=1, source_target_pairs={{0,4},{1,5},{2,6},{3,7},{4,8},{5,9},{6,10},{7,11},{8,12},{9,13},{1... | collective-permute-start | bytes 663560 | tf_op jit(solution)/shard_map/ppermute | solution.py:319
  99.1 1.8 %collective-permute-start.6 = (bf16[288,384]{1,0:T(8,128)(2,1)S(1)}, bf16[288,384]{1,0:T(8,128)(2,1)S(1)}, u32[]{:S(2)}, u32[]{:S(2)}) collective-permute-start(bf16[288,384]{1,0:T(8,128)(2,1)S(1)} %get-tuple-element.17.refs_3_), channel_id=1, source_target_pairs={{0,12},{1,13},{2,14},{3,15},{4,0},{5,1},{6,2},{7,3},{8,4},{9,5},{1... | collective-permute-start | bytes 663560 | tf_op jit(solution)/shard_map/ppermute | solution.py:319
  100.9 1.8 %away.4 = (bf16[4,288,128]{2,1,0:T(8,128)(2,1)}, bf16[4,288,128]{2,1,0:T(8,128)(2,1)}, bf16[4,288,128]{2,1,0:T(8,128)(2,1)}) custom-call(bf16[288,384]{1,0:T(8,128)(2,1)S(1)} %get-tuple-element.21.refs_0_, bf16[288,384]{1,0:T(8,128)(2,1)S(1)} %collective-permute-done.14.refs_1_, bf16[288,384]{1,0:T(8,128)(2,1)S(1)} %collective-permute-done.15.refs_2_, ...), custom_call_target="tpu_custom_call" | custom-call | tf_op jit(solution)/shard_map/away/pallas_call | solution.py:228
  102.7 1.5 %collective-permute-start.16 = (bf16[4,288,128]{2,1,0:T(8,128)(2,1)}, bf16[4,288,128]{2,1,0:T(8,128)(2,1)}, u32[]{:S(2)}, u32[]{:S(2)}) collective-permute-start(bf16[4,288,128]{2,1,0:T(8,128)(2,1)} %get-tuple-element.22), channel_id=1, source_target_pairs={{0,2},{1,3},{2,0},{3,1},{4,6},{5,7},{6,4},{7,5},{8,10},{9,11},{10,... | collective-permute-start | bytes 884744 | tf_op jit(solution)/shard_map/ppermute | solution.py:323
  104.5 2.0 %away.5 = (bf16[1,288,128]{2,1,0:T(8,128)(2,1)S(1)}, bf16[1,288,128]{2,1,0:T(8,128)(2,1)}, bf16[1,288,128]{2,1,0:T(8,128)(2,1)}) custom-call(bf16[288,384]{1,0:T(8,128)(2,1)} %collective-permute-done.19.refs_0_, bf16[384,128]{1,0:T(8,128)(2,1)S(1)} %collective-permute-done.8.refs_3_.refs_4_.refs_1_, ...), custom_call_target="tpu_custom_call" | custom-call | tf_op jit(solution)/shard_map/away/pallas_call | solution.py:228
  107.2 2.8 %collective-permute-done.6.refs_1_ = bf16[288,384]{1,0:T(8,128)(2,1)S(1)} collective-permute-done((bf16[288,384]{1,0:T(8,128)(2,1)S(1)}, bf16[288,384]{1,0:T(8,128)(2,1)S(1)}, u32[]{:S(2)}, u32[]{:S(2)}) %collective-permute-start.6) | collective-permute-done | bytes 221216 | tf_op jit(solution)/shard_map/ppermute | solution.py:319
  110.0 9.5 %collective-permute-done.5.refs_0_ = bf16[288,384]{1,0:T(8,128)(2,1)S(1)} collective-permute-done((bf16[288,384]{1,0:T(8,128)(2,1)S(1)}, bf16[288,384]{1,0:T(8,128)(2,1)S(1)}, u32[]{:S(2)}, u32[]{:S(2)}) %collective-permute-start.5) | collective-permute-done | bytes 221216 | tf_op jit(solution)/shard_map/ppermute | solution.py:319
  121.4 1.6 %away.3 = (bf16[3,288,128]{2,1,0:T(8,128)(2,1)}, bf16[3,288,128]{2,1,0:T(8,128)(2,1)}, bf16[3,288,128]{2,1,0:T(8,128)(2,1)}) custom-call(bf16[288,384]{1,0:T(8,128)(2,1)S(1)} %collective-permute-done.5.refs_0_, bf16[288,384]{1,0:T(8,128)(2,1)S(1)} %collective-permute-done.6.refs_1_, bf16[288,384]{1,0:T(8,128)(2,1)S(1)} %collective-permute-done.7.refs_2_, ...), custom_call_target="tpu_custom_call" | custom-call | tf_op jit(solution)/shard_map/away/pallas_call | solution.py:228
  123.5 1.5 %collective-permute-start.13 = (bf16[3,288,128]{2,1,0:T(8,128)(2,1)}, bf16[3,288,128]{2,1,0:T(8,128)(2,1)}, u32[]{:S(2)}, u32[]{:S(2)}) collective-permute-start(bf16[3,288,128]{2,1,0:T(8,128)(2,1)} %get-tuple-element.20), channel_id=1, source_target_pairs={{0,2},{1,3},{2,0},{3,1},{4,6},{5,7},{6,4},{7,5},{8,10},{9,11},{10,... | collective-permute-start | bytes 663560 | tf_op jit(solution)/shard_map/ppermute | solution.py:323
  125.1 2.0 %pad_maximum_fusion = bf16[16,2,36,188]{3,2,1,0:T(8,128)(2,1)} fusion(bf16[8,2,36,188]{3,2,1,0:T(8,128)(2,1)} %copy-done.2, bf16[8,2,36,188]{3,2,1,0:T(8,128)(2,1)} %copy-done.1), kind=kLoop, calls=%fused_computation.4 | loop fusion | flops 216576 | bytes 866304 | tf_op jit(solution)/shard_map/concatenate | solution.py:361
  127.2 3.1 %reshape.103 = bf16[16,2,6768]{2,1,0:T(2,128)(2,1)} reshape(bf16[16,2,36,188]{3,2,1,0:T(8,128)(2,1)} %pad_maximum_fusion) | data formatting | bytes 866304 | tf_op jit(solution)/shard_map/reshape | solution.py:362
  130.3 2.6 %write.4.refs_6_ = f32[36,256,128]{2,1,0:T(8,128)} custom-call(s32[8]{0:T(128)S(1)} %stack.143.rows_ref, bf16[384,128]{1,0:T(8,128)(2,1)} %concatenate.6.refs_0_, bf16[1,288,384]{2,1,0:T(8,128)(2,1)S(1)} %bitcast.61, bf16[1,288,384]{2,1,0:T(8,128)(2,1)S(1)} %bitcast.63, bf16[1,288,384]{2,1,0:T(8,128)(2,1)S(1)} %bitcast.62, ...), custom_call_target="tpu_custom_call" | custom-call | tf_op jit(solution)/shard_map/write/pallas_call | solution.py:281
  132.9 2.7 %write.5.refs_2_ = f32[36,256,128]{2,1,0:T(8,128)} custom-call(s32[15]{0:T(128)S(1)} %stack.134.rows_ref, bf16[4,288,128]{2,1,0:T(8,128)(2,1)} %collective-permute-done.16.refs_0_, bf16[4,288,128]{2,1,0:T(8,128)(2,1)} %collective-permute-done.17.refs_1_, bf16[4,288,128]{2,1,0:T(8,128)(2,1)} %collective-permute-done.18.refs_2_, ...), custom_call_target="tpu_custom_call", output_to_operand_aliasing={{}: (7, {})} | custom-call | tf_op jit(solution)/shard_map/write/pallas_call | solution.py:281
  135.6 2.9 %collective-permute-done.13.refs_1_ = bf16[3,288,128]{2,1,0:T(8,128)(2,1)} collective-permute-done((bf16[3,288,128]{2,1,0:T(8,128)(2,1)}, bf16[3,288,128]{2,1,0:T(8,128)(2,1)}, u32[]{:S(2)}, u32[]{:S(2)}) %collective-permute-start.13) | collective-permute-done | bytes 221216 | tf_op jit(solution)/shard_map/ppermute | solution.py:323
  138.5 1.9 %write.6.refs_1_ = f32[36,256,128]{2,1,0:T(8,128)} custom-call(s32[6]{0:T(128)S(1)} %stack.118.rows_ref, bf16[3,288,128]{2,1,0:T(8,128)(2,1)S(1)} %collective-permute-done.12.refs_0_, bf16[3,288,128]{2,1,0:T(8,128)(2,1)} %collective-permute-done.13.refs_1_, f32[36,256,128]{2,1,0:T(8,128)} %write.5.refs_2_), custom_call_target="tpu_custom_call", output_to_operand_aliasing={{}: (3, {})} | custom-call | tf_op jit(solution)/shard_map/write/pallas_call | solution.py:281
  140.5 1.7 %write.7 = f32[36,256,128]{2,1,0:T(8,128)} custom-call(s32[3]{0:T(128)S(1)} %pad_add_fusion.rows_ref, bf16[3,288,128]{2,1,0:T(8,128)(2,1)} %collective-permute-done.11.refs_0_, f32[36,256,128]{2,1,0:T(8,128)} %write.6.refs_1_), custom_call_target="tpu_custom_call", output_to_operand_aliasing={{}: (2, {})} | custom-call | tf_op jit(solution)/shard_map/write/pallas_call | solution.py:281
  (83 shorter events, 13.3 us)
Async XLA Ops:
  5.3 31.5 %copy-start.15 = (bf16[2,188,128]{2,0,1:T(2,128)(2,1)S(1)}, bf16[2,188,128]{2,0,1:T(2,128)(2,1)}, u32[]{:S(2)}) copy-start(bf16[2,188,128]{2,0,1:T(2,128)(2,1)} %param.7) | copy-start | bytes 288772
  32.7 9.3 %copy-start.16 = (s32[36]{0:T(128)S(1)}, s32[36]{0:T(128)}, u32[]{:S(2)}) copy-start(s32[36]{0:T(128)} %param.6) | copy-start | bytes 436
  32.7 27.3 %copy-start.13 = (s32[8]{0:T(128)S(1)}, s32[8]{0:T(128)}, u32[]{:S(2)}) copy-start(s32[8]{0:T(128)} %starts_ref.3) | copy-start | bytes 100
  32.7 50.0 %all-to-all-start.1 = ((bf16[16,8,8,384]{3,2,1,0:T(8,128)(2,1)}), bf16[16,8,8,384]{3,2,1,0:T(8,128)(2,1)S(1)}, u32[]{:S(2)}, u32[]{:S(2)}) async-start(bf16[16,8,8,384]{3,2,1,0:T(8,128)(2,1)} %get-tuple-element.31), calls=%async_computation.1 | async-start | bytes 1572864 | tf_op jit(solution)/shard_map/all_to_all | solution.py:353
  43.1 1.4 %collective-permute-start = (bf16[36,384]{1,0:T(8,128)(2,1)S(1)}, bf16[36,384]{1,0:T(8,128)(2,1)S(1)}, u32[]{:S(2)}, u32[]{:S(2)}) collective-permute-start(bf16[36,384]{1,0:T(8,128)(2,1)S(1)} %convolution_convert_fusion), channel_id=1, source_target_pairs={{0,1},{1,0},{2,3},{3,2},{4,5},{5,4},{6,7},{7,6},{8,9},{9,8},{10,11... | collective-permute-start | bytes 82952 | tf_op jit(solution)/shard_map/ppermute | solution.py:323
  44.5 4.3 %collective-permute-start.1 = (bf16[36,384]{1,0:T(8,128)(2,1)S(1)}, bf16[36,384]{1,0:T(8,128)(2,1)S(1)}, u32[]{:S(2)}, u32[]{:S(2)}) collective-permute-start(bf16[36,384]{1,0:T(8,128)(2,1)S(1)} %add.131), channel_id=1, source_target_pairs={{0,2},{1,3},{2,0},{3,1},{4,6},{5,7},{6,4},{7,5},{8,10},{9,11},{10,... | collective-permute-start | bytes 82952 | tf_op jit(solution)/shard_map/ppermute | solution.py:323
  48.8 33.8 %copy-start.3 = (bf16[36,384]{1,0:T(8,128)(2,1)}, bf16[36,384]{1,0:T(8,128)(2,1)S(1)}, u32[]{:S(2)}) copy-start(bf16[36,384]{1,0:T(8,128)(2,1)S(1)} %add.132.refs_0_) | copy-start | bytes 82948
  48.8 11.1 %collective-permute-start.4 = (bf16[36,384]{1,0:T(8,128)(2,1)S(1)}, bf16[36,384]{1,0:T(8,128)(2,1)S(1)}, u32[]{:S(2)}, u32[]{:S(2)}) collective-permute-start(bf16[36,384]{1,0:T(8,128)(2,1)S(1)} %add.132.refs_0_), channel_id=1, source_target_pairs={{0,8},{1,9},{2,10},{3,11},{4,12},{5,13},{6,14},{7,15},{8,0},{9,1},... | collective-permute-start | bytes 82952 | tf_op jit(solution)/shard_map/ppermute | solution.py:319
  51.5 8.5 %collective-permute-start.3 = (bf16[36,384]{1,0:T(8,128)(2,1)S(1)}, bf16[36,384]{1,0:T(8,128)(2,1)S(1)}, u32[]{:S(2)}, u32[]{:S(2)}) collective-permute-start(bf16[36,384]{1,0:T(8,128)(2,1)S(1)} %add.132.refs_0_), channel_id=1, source_target_pairs={{0,12},{1,13},{2,14},{3,15},{4,0},{5,1},{6,2},{7,3},{8,4},{9,5},{1... | collective-permute-start | bytes 82952 | tf_op jit(solution)/shard_map/ppermute | solution.py:319
  52.8 7.2 %collective-permute-start.2 = (bf16[36,384]{1,0:T(8,128)(2,1)S(1)}, bf16[36,384]{1,0:T(8,128)(2,1)S(1)}, u32[]{:S(2)}, u32[]{:S(2)}) collective-permute-start(bf16[36,384]{1,0:T(8,128)(2,1)S(1)} %add.132.refs_0_), channel_id=1, source_target_pairs={{0,4},{1,5},{2,6},{3,7},{4,8},{5,9},{6,10},{7,11},{8,12},{9,13},{1... | collective-permute-start | bytes 82952 | tf_op jit(solution)/shard_map/ppermute | solution.py:319
  60.0 22.6 %copy-start.5 = (bf16[36,384]{1,0:T(8,128)(2,1)}, bf16[36,384]{1,0:T(8,128)(2,1)S(1)}, u32[]{:S(2)}) copy-start(bf16[36,384]{1,0:T(8,128)(2,1)S(1)} %collective-permute-done.4.refs_3_) | copy-start | bytes 82948
  60.0 22.6 %copy-start.7 = (bf16[36,384]{1,0:T(8,128)(2,1)}, bf16[36,384]{1,0:T(8,128)(2,1)S(1)}, u32[]{:S(2)}) copy-start(bf16[36,384]{1,0:T(8,128)(2,1)S(1)} %collective-permute-done.3.refs_2_) | copy-start | bytes 82948
  60.0 22.6 %copy-start.9 = (bf16[36,384]{1,0:T(8,128)(2,1)}, bf16[36,384]{1,0:T(8,128)(2,1)S(1)}, u32[]{:S(2)}) copy-start(bf16[36,384]{1,0:T(8,128)(2,1)S(1)} %collective-permute-done.2.refs_1_) | copy-start | bytes 82948
  70.6 12.0 %copy-start.1 = (bf16[8,2,36,188]{3,2,1,0:T(8,128)(2,1)}, bf16[8,2,36,188]{3,2,1,0:T(8,128)(2,1)S(1)}, u32[]{:S(2)}) copy-start(bf16[8,2,36,188]{3,2,1,0:T(8,128)(2,1)S(1)} %get-tuple-element.15) | copy-start | bytes 649732
  70.6 12.0 %collective-permute-start.15 = (bf16[288,384]{1,0:T(8,128)(2,1)S(1)}, bf16[288,384]{1,0:T(8,128)(2,1)S(1)}, u32[]{:S(2)}, u32[]{:S(2)}) collective-permute-start(bf16[288,384]{1,0:T(8,128)(2,1)S(1)} %get-tuple-element.21.refs_0_), channel_id=1, source_target_pairs={{0,8},{1,9},{2,10},{3,11},{4,12},{5,13},{6,14},{7,15},{8,0},{9,1},... | collective-permute-start | bytes 663560 | tf_op jit(solution)/shard_map/ppermute | solution.py:323
  71.5 29.4 %collective-permute-start.14 = (bf16[288,384]{1,0:T(8,128)(2,1)S(1)}, bf16[288,384]{1,0:T(8,128)(2,1)S(1)}, u32[]{:S(2)}, u32[]{:S(2)}) collective-permute-start(bf16[288,384]{1,0:T(8,128)(2,1)S(1)} %get-tuple-element.21.refs_0_), channel_id=1, source_target_pairs={{0,4},{1,5},{2,6},{3,7},{4,0},{5,1},{6,2},{7,3},{8,12},{9,13},{10,... | collective-permute-start | bytes 663560 | tf_op jit(solution)/shard_map/ppermute | solution.py:323
  72.7 24.3 %collective-permute-start.10 = (bf16[384,128]{1,0:T(8,128)(2,1)}, bf16[384,128]{1,0:T(8,128)(2,1)S(1)}, u32[]{:S(2)}, u32[]{:S(2)}) collective-permute-start(bf16[384,128]{1,0:T(8,128)(2,1)} %concatenate.6.refs_0_), channel_id=1, source_target_pairs={{0,1},{1,0},{2,3},{3,2},{4,5},{5,4},{6,7},{7,6},{8,9},{9,8},{10,11... | collective-permute-start | bytes 294920 | tf_op jit(solution)/shard_map/ppermute | solution.py:323
  72.7 26.4 %collective-permute-start.9 = (bf16[384,128]{1,0:T(8,128)(2,1)}, bf16[384,128]{1,0:T(8,128)(2,1)S(1)}, u32[]{:S(2)}, u32[]{:S(2)}) collective-permute-start(bf16[384,128]{1,0:T(8,128)(2,1)} %concatenate.6.refs_0_), channel_id=1, source_target_pairs={{0,3},{1,2},{2,1},{3,0},{4,7},{5,6},{6,5},{7,4},{8,11},{9,10},{10,... | collective-permute-start | bytes 294920 | tf_op jit(solution)/shard_map/ppermute | solution.py:323
  74.3 26.6 %collective-permute-start.8 = (bf16[384,128]{1,0:T(8,128)(2,1)}, bf16[384,128]{1,0:T(8,128)(2,1)S(1)}, u32[]{:S(2)}, u32[]{:S(2)}) collective-permute-start(bf16[384,128]{1,0:T(8,128)(2,1)} %concatenate.6.refs_0_), channel_id=1, source_target_pairs={{0,2},{1,3},{2,0},{3,1},{4,6},{5,7},{6,4},{7,5},{8,10},{9,11},{10,... | collective-permute-start | bytes 294920 | tf_op jit(solution)/shard_map/ppermute | solution.py:323
  82.6 21.9 %collective-permute-start.19 = (bf16[288,384]{1,0:T(8,128)(2,1)S(1)}, bf16[288,384]{1,0:T(8,128)(2,1)}, u32[]{:S(2)}, u32[]{:S(2)}) collective-permute-start(bf16[288,384]{1,0:T(8,128)(2,1)S(1)} %collective-permute-done.15.refs_2_), channel_id=1, source_target_pairs={{0,4},{1,5},{2,6},{3,7},{4,0},{5,1},{6,2},{7,3},{8,12},{9,13},{10,... | collective-permute-start | bytes 663560 | tf_op jit(solution)/shard_map/ppermute | solution.py:323
  97.0 10.2 %collective-permute-start.7 = (bf16[288,384]{1,0:T(8,128)(2,1)S(1)}, bf16[288,384]{1,0:T(8,128)(2,1)S(1)}, u32[]{:S(2)}, u32[]{:S(2)}) collective-permute-start(bf16[288,384]{1,0:T(8,128)(2,1)S(1)} %get-tuple-element.17.refs_3_), channel_id=1, source_target_pairs={{0,4},{1,5},{2,6},{3,7},{4,8},{5,9},{6,10},{7,11},{8,12},{9,13},{1... | collective-permute-start | bytes 663560 | tf_op jit(solution)/shard_map/ppermute | solution.py:319
  99.1 10.9 %collective-permute-start.6 = (bf16[288,384]{1,0:T(8,128)(2,1)S(1)}, bf16[288,384]{1,0:T(8,128)(2,1)S(1)}, u32[]{:S(2)}, u32[]{:S(2)}) collective-permute-start(bf16[288,384]{1,0:T(8,128)(2,1)S(1)} %get-tuple-element.17.refs_3_), channel_id=1, source_target_pairs={{0,12},{1,13},{2,14},{3,15},{4,0},{5,1},{6,2},{7,3},{8,4},{9,5},{1... | collective-permute-start | bytes 663560 | tf_op jit(solution)/shard_map/ppermute | solution.py:319
  102.7 20.8 %collective-permute-start.16 = (bf16[4,288,128]{2,1,0:T(8,128)(2,1)}, bf16[4,288,128]{2,1,0:T(8,128)(2,1)}, u32[]{:S(2)}, u32[]{:S(2)}) collective-permute-start(bf16[4,288,128]{2,1,0:T(8,128)(2,1)} %get-tuple-element.22), channel_id=1, source_target_pairs={{0,2},{1,3},{2,0},{3,1},{4,6},{5,7},{6,4},{7,5},{8,10},{9,11},{10,... | collective-permute-start | bytes 884744 | tf_op jit(solution)/shard_map/ppermute | solution.py:323
  104.2 15.2 %collective-permute-start.5 = (bf16[288,384]{1,0:T(8,128)(2,1)S(1)}, bf16[288,384]{1,0:T(8,128)(2,1)S(1)}, u32[]{:S(2)}, u32[]{:S(2)}) collective-permute-start(bf16[288,384]{1,0:T(8,128)(2,1)S(1)} %get-tuple-element.17.refs_3_), channel_id=1, source_target_pairs={{0,8},{1,9},{2,10},{3,11},{4,12},{5,13},{6,14},{7,15},{8,0},{9,1},... | collective-permute-start | bytes 663560 | tf_op jit(solution)/shard_map/ppermute | solution.py:319
  106.5 13.8 %collective-permute-start.20 = (bf16[1,288,128]{2,1,0:T(8,128)(2,1)S(1)}, bf16[1,288,128]{2,1,0:T(8,128)(2,1)S(1)}, u32[]{:S(2)}, u32[]{:S(2)}) collective-permute-start(bf16[1,288,128]{2,1,0:T(8,128)(2,1)S(1)} %get-tuple-element.25), channel_id=1, source_target_pairs={{0,2},{1,3},{2,0},{3,1},{4,6},{5,7},{6,4},{7,5},{8,10},{9,11},{10,... | collective-permute-start | bytes 221192 | tf_op jit(solution)/shard_map/ppermute | solution.py:323
  107.2 15.8 %collective-permute-start.21 = (bf16[1,288,128]{2,1,0:T(8,128)(2,1)}, bf16[1,288,128]{2,1,0:T(8,128)(2,1)}, u32[]{:S(2)}, u32[]{:S(2)}) collective-permute-start(bf16[1,288,128]{2,1,0:T(8,128)(2,1)} %get-tuple-element.26), channel_id=1, source_target_pairs={{0,3},{1,2},{2,1},{3,0},{4,7},{5,6},{6,5},{7,4},{8,11},{9,10},{10,... | collective-permute-start | bytes 221192 | tf_op jit(solution)/shard_map/ppermute | solution.py:323
  109.9 13.2 %collective-permute-start.22 = (bf16[1,288,128]{2,1,0:T(8,128)(2,1)}, bf16[1,288,128]{2,1,0:T(8,128)(2,1)}, u32[]{:S(2)}, u32[]{:S(2)}) collective-permute-start(bf16[1,288,128]{2,1,0:T(8,128)(2,1)} %get-tuple-element.27), channel_id=1, source_target_pairs={{0,1},{1,0},{2,3},{3,2},{4,5},{5,4},{6,7},{7,6},{8,9},{9,8},{10,11... | collective-permute-start | bytes 221192 | tf_op jit(solution)/shard_map/ppermute | solution.py:323
  119.4 13.4 %collective-permute-start.17 = (bf16[4,288,128]{2,1,0:T(8,128)(2,1)}, bf16[4,288,128]{2,1,0:T(8,128)(2,1)}, u32[]{:S(2)}, u32[]{:S(2)}) collective-permute-start(bf16[4,288,128]{2,1,0:T(8,128)(2,1)} %get-tuple-element.23), channel_id=1, source_target_pairs={{0,3},{1,2},{2,1},{3,0},{4,7},{5,6},{6,5},{7,4},{8,11},{9,10},{10,... | collective-permute-start | bytes 884744 | tf_op jit(solution)/shard_map/ppermute | solution.py:323
  120.3 12.6 %collective-permute-start.18 = (bf16[4,288,128]{2,1,0:T(8,128)(2,1)}, bf16[4,288,128]{2,1,0:T(8,128)(2,1)}, u32[]{:S(2)}, u32[]{:S(2)}) collective-permute-start(bf16[4,288,128]{2,1,0:T(8,128)(2,1)} %get-tuple-element.24), channel_id=1, source_target_pairs={{0,1},{1,0},{2,3},{3,2},{4,5},{5,4},{6,7},{7,6},{8,9},{9,8},{10,11... | collective-permute-start | bytes 884744 | tf_op jit(solution)/shard_map/ppermute | solution.py:323
  122.9 17.5 %collective-permute-start.11 = (bf16[3,288,128]{2,1,0:T(8,128)(2,1)}, bf16[3,288,128]{2,1,0:T(8,128)(2,1)}, u32[]{:S(2)}, u32[]{:S(2)}) collective-permute-start(bf16[3,288,128]{2,1,0:T(8,128)(2,1)} %get-tuple-element.18), channel_id=1, source_target_pairs={{0,3},{1,2},{2,1},{3,0},{4,7},{5,6},{6,5},{7,4},{8,11},{9,10},{10,... | collective-permute-start | bytes 663560 | tf_op jit(solution)/shard_map/ppermute | solution.py:323
  123.1 12.5 %collective-permute-start.12 = (bf16[3,288,128]{2,1,0:T(8,128)(2,1)}, bf16[3,288,128]{2,1,0:T(8,128)(2,1)S(1)}, u32[]{:S(2)}, u32[]{:S(2)}) collective-permute-start(bf16[3,288,128]{2,1,0:T(8,128)(2,1)} %get-tuple-element.19), channel_id=1, source_target_pairs={{0,1},{1,0},{2,3},{3,2},{4,5},{5,4},{6,7},{7,6},{8,9},{9,8},{10,11... | collective-permute-start | bytes 663560 | tf_op jit(solution)/shard_map/ppermute | solution.py:323
  123.5 15.0 %collective-permute-start.13 = (bf16[3,288,128]{2,1,0:T(8,128)(2,1)}, bf16[3,288,128]{2,1,0:T(8,128)(2,1)}, u32[]{:S(2)}, u32[]{:S(2)}) collective-permute-start(bf16[3,288,128]{2,1,0:T(8,128)(2,1)} %get-tuple-element.20), channel_id=1, source_target_pairs={{0,2},{1,3},{2,0},{3,1},{4,6},{5,7},{6,4},{7,5},{8,10},{9,11},{10,... | collective-permute-start | bytes 663560 | tf_op jit(solution)/shard_map/ppermute | solution.py:323
  (9 other events, 16.3 us)

commit v5 on v4

--- a/solution.py
+++ b/solution.py
@@ -144,20 +144,20 @@
             k = g * group + j
             real, imag, _, _, factor = apply_corr(k)
             gain = scale_ref[k] * factor
-            weight_real = ((steer_real * real - steer_imag * imag) * gain)[:beams]
-            weight_imag = ((steer_real * imag + steer_imag * real) * gain)[:beams]
-            flat_ref[k, 0] = weight_real[:, :ports].astype(jnp.bfloat16)
-            flat_ref[k, 1] = weight_imag[:, :ports].astype(jnp.bfloat16)
+            weight_real = (steer_real * real - steer_imag * imag) * gain
+            weight_imag = (steer_real * imag + steer_imag * real) * gain
+            flat_ref[k, 0] = weight_real[:beams, :ports].astype(jnp.bfloat16)
+            flat_ref[k, 1] = weight_imag[:beams, :ports].astype(jnp.bfloat16)
             tails = weight_real[:, full:] + pltpu.roll(weight_imag[:, full:], LANES // 2, 1)
             tiles = [weight_real[:, i : i + LANES] for i in range(0, full, LANES)]
             tiles += [weight_imag[:, i : i + LANES] for i in range(0, full, LANES)]
             for i, tile in enumerate(tiles + [tails]):
-                pay_sc[i, pl.ds(k, beams, stride=channels)] = tile
+                pay_sc[i, pl.ds(k, pad, stride=channels)] = tile
         return carry
 
     lax.fori_loop(0, channels // group, group_body, 0)
     for i in range(pay_sc.shape[0]):
-        pay_ref[:, i * LANES : (i + 1) * LANES] = pay_sc[i].astype(jnp.bfloat16)
+        pay_ref[:, i * LANES : (i + 1) * LANES] = pay_sc[i, : beams * channels].astype(jnp.bfloat16)
 
 
 def here(value):
@@ -190,7 +190,7 @@
             pltpu.VMEM((channels, width, 2 * rows), jnp.bfloat16),
             pltpu.VMEM((channels, 1, width), jnp.float32),
             pltpu.VMEM((channels, 4 * pad, width), jnp.bfloat16),
-            pltpu.VMEM((wide // LANES, beams * channels, LANES), jnp.float32),
+            pltpu.VMEM((wide // LANES, pad * channels, LANES), jnp.float32),
         ],
         compiler_params=GRANT,
         name="power",
@@ -349,6 +349,8 @@
 
     arrived = []
     for i in range(chunks):
+        if i:
+            blocks, steering[0] = lax.optimization_barrier((blocks, steering[0]))
         block = blocks[:, i * part : (i + 1) * part]
         arrived.append(lax.all_to_all(block, "tm", split_axis=0, concat_axis=0, tiled=True))
     near = (2, 3, 1)

time: 143 us -> 146 us (1.021)
  blocking collectives: 27.4 us -> 0 us
  waiting for transfers between devices: 32.9 us -> 49.5 us
  starting transfers between devices: 25.3 us -> 34.3 us
  local copies, waits for them, and re-layouts: 15.5 us -> 19.8 us
    all_to_all x1 -> x0, blocking collectives: 27.4 us -> none  [on_device(): lax.all_to_all(block, 'tm', split_axis=0, concat_axis=0, tiled=True)]
    ppermute x6, waiting for transfers between devices: 18.9 us -> 30.9 us  [turned(): lax.ppermute(value, 'tm', [(i, (i + shift) % count) for i in range(count)])]
    all_to_all x1 -> x2, starting transfers between devices: 4.07 us -> 12.9 us  [on_device(): lax.all_to_all(block, 'tm', split_axis=0, concat_axis=0, tiled=True)]
    all_to_all x1 -> x2, waiting for transfers between devices: 0.01 us -> 4.59 us  [on_device(): lax.all_to_all(block, 'tm', split_axis=0, concat_axis=0, tiled=True)]
    slice x1 -> x2, local copies, waits for them, and re-layouts: 1.05 us -> 4.27 us  [on_device(): block = blocks[:, i * part:(i + 1) * part]]
    unnamed x34 -> x30, local copies, waits for them, and re-layouts: 4.99 us -> 4.99 us
  transfers between devices with their start and end apart: 24 -> 25, of which waited for: 8 -> 9; matrix products, arithmetic and copies ran while one was open for 8% -> 10% of each run, Pallas kernels for 24% -> 23%
where the time goes in v5:
time: 146 us; the launch traced here: 145 us
  waiting for transfers between devices  49.5 us (34%)
  Pallas kernels  35.4 us (24%)
  starting transfers between devices  34.3 us (23%)
  local copies, waits for them, and re-layouts  19.8 us (14%)
  matrix products  2.32 us (2%)
  other arithmetic  2.22 us (2%)
    ppermute x6, waiting for transfers between devices, turned(): lax.ppermute(value, 'tm', [(i, (i + shift) % count) for i in range(count)])  30.9 us
    pallas_call x2, Pallas kernels, power_weights(): pl.pallas_call(functools.partial(power_kernel, ports=ports, group=group,...  21.2 us
    ppermute x17, waiting for transfers between devices, crossed(): return lax.ppermute(value, 'tm', [(i, i ^ bits) for i in range(count)])  14 us
    all_to_all x2, starting transfers between devices, on_device(): lax.all_to_all(block, 'tm', split_axis=0, concat_axis=0, tiled=True)  12.9 us
    ppermute x17, starting transfers between devices, crossed(): return lax.ppermute(value, 'tm', [(i, i ^ bits) for i in range(count)])  12.4 us
    ppermute x6, starting transfers between devices, turned(): lax.ppermute(value, 'tm', [(i, (i + shift) % count) for i in range(count)])  9.04 us
    pallas_call x4, Pallas kernels, write_maps(): pl.pallas_call(functools.partial(write_kernel, parts=len(parts), channels...  8.86 us
    pallas_call x3, Pallas kernels, away_maps(): pl.pallas_call(functools.partial(away_kernel, shards=len(shards), views=v...  5.33 us
  transfers between devices with their start and end apart: 25, of which 9 were waited for; matrix products, arithmetic and copies ran while one was open for 10% of the time, Pallas kernels for 23%

profile of v5, /device:TPU:0, one launch (start us, length us, event | category | flops | bytes accessed | tf_op | source)
XLA Modules:
  0.0 144.7 jit_solution(14842847881156178469)
XLA Ops:
  3.3 2.1 %copy.16 = bf16[256,8,384]{2,1,0:T(8,128)(2,1)} copy(bf16[256,8,384]{2,0,1:T(8,128)(2,1)S(1)} %fusion.1) | data formatting | bytes 3145728 | tf_op jit(solution)/shard_map/convert_element_type | solution.py:345
  5.3 2.2 %slice.46 = bf16[16,8,8,384]{3,2,1,0:T(8,128)(2,1)} slice(bf16[16,16,8,384]{3,2,1,0:T(8,128)(2,1)} %bitcast.4), slice={[0:16], [0:8], [0:8], [0:384]} | slice | bytes 1572864 | tf_op jit(solution)/shard_map/slice | solution.py:354
  7.5 7.5 %all-to-all-start = ((bf16[16,8,8,384]{3,2,1,0:T(8,128)(2,1)}), bf16[16,8,8,384]{3,2,1,0:T(8,128)(2,1)S(1)}, u32[]{:S(2)}, u32[]{:S(2)}) async-start(bf16[16,8,8,384]{3,2,1,0:T(8,128)(2,1)} %slice.46), calls=%async_computation | async-start | bytes 1572864 | tf_op jit(solution)/shard_map/all_to_all | solution.py:355
  15.2 5.0 %concatenate.6.refs_0_ = bf16[384,128]{1,0:T(8,128)(2,1)} concatenate(bf16[128,128]{1,0:T(8,128)(2,1)S(1)} %get-tuple-element.41, bf16[128,128]{1,0:T(8,128)(2,1)S(1)} %get-tuple-element.40, bf16[60,128]{1,0:T(8,128)(2,1)S(1)} %get-tuple-element.43, bf16[4,128]{1,0:T(4,128)(2,1)S(1)} %broadcast_in_dim.42, bf16[60,128]{1,0:T(8,128)(2,1)S(1)} %get-tuple-element.42, ...), dimensions={0} | concatenate | bytes 196608 | tf_op jit(solution)/shard_map/concatenate | solution.py:31
  22.6 1.9 %collective-permute-start.1 = (bf16[36,384]{1,0:T(8,128)(2,1)S(1)}, bf16[36,384]{1,0:T(8,128)(2,1)S(1)}, u32[]{:S(2)}, u32[]{:S(2)}) collective-permute-start(bf16[36,384]{1,0:T(8,128)(2,1)S(1)} %add.131), channel_id=1, source_target_pairs={{0,2},{1,3},{2,0},{3,1},{4,6},{5,7},{6,4},{7,5},{8,10},{9,11},{10,... | collective-permute-start | bytes 82952 | tf_op jit(solution)/shard_map/ppermute | solution.py:323
  24.6 2.4 %collective-permute-done.1 = bf16[36,384]{1,0:T(8,128)(2,1)S(1)} collective-permute-done((bf16[36,384]{1,0:T(8,128)(2,1)S(1)}, bf16[36,384]{1,0:T(8,128)(2,1)S(1)}, u32[]{:S(2)}, u32[]{:S(2)}) %collective-permute-start.1) | collective-permute-done | bytes 27680 | tf_op jit(solution)/shard_map/ppermute | solution.py:323
  27.0 2.1 %slice.45 = bf16[16,8,8,384]{3,2,1,0:T(8,128)(2,1)} slice(bf16[16,16,8,384]{3,2,1,0:T(8,128)(2,1)} %bitcast.4), slice={[0:16], [8:16], [0:8], [0:384]} | slice | bytes 1572864 | tf_op jit(solution)/shard_map/slice | solution.py:354
  29.1 4.6 %all-to-all-done.arr_ref = bf16[16,8,8,384]{3,2,1,0:T(8,128)(2,1)S(1)} async-done(((bf16[16,8,8,384]{3,2,1,0:T(8,128)(2,1)}), bf16[16,8,8,384]{3,2,1,0:T(8,128)(2,1)S(1)}, u32[]{:S(2)}, u32[]{:S(2)}) %all-to-all-start) | async-done | bytes 786464 | tf_op jit(solution)/shard_map/all_to_all | solution.py:355
  33.7 5.4 %all-to-all-start.1 = ((bf16[16,8,8,384]{3,2,1,0:T(8,128)(2,1)}), bf16[16,8,8,384]{3,2,1,0:T(8,128)(2,1)S(1)}, u32[]{:S(2)}, u32[]{:S(2)}) async-start(bf16[16,8,8,384]{3,2,1,0:T(8,128)(2,1)} %slice.45), calls=%async_computation.1 | async-start | bytes 1572864 | tf_op jit(solution)/shard_map/all_to_all | solution.py:355
  39.1 2.8 %collective-permute-start.4 = (bf16[36,384]{1,0:T(8,128)(2,1)S(1)}, bf16[36,384]{1,0:T(8,128)(2,1)S(1)}, u32[]{:S(2)}, u32[]{:S(2)}) collective-permute-start(bf16[36,384]{1,0:T(8,128)(2,1)S(1)} %add.132.refs_0_), channel_id=1, source_target_pairs={{0,8},{1,9},{2,10},{3,11},{4,12},{5,13},{6,14},{7,15},{8,0},{9,1},... | collective-permute-start | bytes 82952 | tf_op jit(solution)/shard_map/ppermute | solution.py:319
  41.9 1.5 %collective-permute-start.3 = (bf16[36,384]{1,0:T(8,128)(2,1)S(1)}, bf16[36,384]{1,0:T(8,128)(2,1)S(1)}, u32[]{:S(2)}, u32[]{:S(2)}) collective-permute-start(bf16[36,384]{1,0:T(8,128)(2,1)S(1)} %add.132.refs_0_), channel_id=1, source_target_pairs={{0,12},{1,13},{2,14},{3,15},{4,0},{5,1},{6,2},{7,3},{8,4},{9,5},{1... | collective-permute-start | bytes 82952 | tf_op jit(solution)/shard_map/ppermute | solution.py:319
  43.9 18.3 %collective-permute-done.4.refs_3_ = bf16[36,384]{1,0:T(8,128)(2,1)S(1)} collective-permute-done((bf16[36,384]{1,0:T(8,128)(2,1)S(1)}, bf16[36,384]{1,0:T(8,128)(2,1)S(1)}, u32[]{:S(2)}, u32[]{:S(2)}) %collective-permute-start.4) | collective-permute-done | bytes 27680 | tf_op jit(solution)/shard_map/ppermute | solution.py:319
  62.3 10.6 %power.2 = (bf16[288,384]{1,0:T(8,128)(2,1)S(1)}, bf16[8,2,36,188]{3,2,1,0:T(8,128)(2,1)S(1)}) custom-call(bf16[16,8,8,384]{3,2,1,0:T(8,128)(2,1)S(1)} %all-to-all-done.arr_ref, s32[8]{0:T(128)S(1)} %copy-done.11, bf16[36,384]{1,0:T(8,128)(2,1)S(1)} %add.132.refs_0_, bf16[36,384]{1,0:T(8,128)(2,1)S(1)} %collective-permute-done.2.refs_1_, ...), custom_call_target="tpu_custom_call" | custom-call | tf_op jit(solution)/shard_map/power/pallas_call | solution.py:176
  75.1 1.6 %collective-permute-start.9 = (bf16[384,128]{1,0:T(8,128)(2,1)}, bf16[384,128]{1,0:T(8,128)(2,1)S(1)}, u32[]{:S(2)}, u32[]{:S(2)}) collective-permute-start(bf16[384,128]{1,0:T(8,128)(2,1)} %concatenate.6.refs_0_), channel_id=1, source_target_pairs={{0,3},{1,2},{2,1},{3,0},{4,7},{5,6},{6,5},{7,4},{8,11},{9,10},{10,... | collective-permute-start | bytes 294920 | tf_op jit(solution)/shard_map/ppermute | solution.py:323
  77.2 7.7 %collective-permute-done.15.refs_2_ = bf16[288,384]{1,0:T(8,128)(2,1)S(1)} collective-permute-done((bf16[288,384]{1,0:T(8,128)(2,1)S(1)}, bf16[288,384]{1,0:T(8,128)(2,1)S(1)}, u32[]{:S(2)}, u32[]{:S(2)}) %collective-permute-start.15) | collective-permute-done | bytes 221216 | tf_op jit(solution)/shard_map/ppermute | solution.py:323
  88.7 10.6 %power.3 = (bf16[288,384]{1,0:T(8,128)(2,1)S(1)}, bf16[8,2,36,188]{3,2,1,0:T(8,128)(2,1)S(1)}) custom-call(bf16[16,8,8,384]{3,2,1,0:T(8,128)(2,1)S(1)} %all-to-all-done.1.arr_ref, s32[8]{0:T(128)S(1)} %copy-done.12, bf16[36,384]{1,0:T(8,128)(2,1)S(1)} %copy-done.4, bf16[36,384]{1,0:T(8,128)(2,1)S(1)} %copy-done.10, bf16[36,384]{1,0:T(8,128)(2,1)S(1)} %copy-done.8, ...), custom_call_target="tpu_custom_call" | custom-call | tf_op jit(solution)/shard_map/power/pallas_call | solution.py:176
  99.3 2.1 %collective-permute-start.7 = (bf16[288,384]{1,0:T(8,128)(2,1)S(1)}, bf16[288,384]{1,0:T(8,128)(2,1)S(1)}, u32[]{:S(2)}, u32[]{:S(2)}) collective-permute-start(bf16[288,384]{1,0:T(8,128)(2,1)S(1)} %get-tuple-element.21.refs_3_), channel_id=1, source_target_pairs={{0,4},{1,5},{2,6},{3,7},{4,8},{5,9},{6,10},{7,11},{8,12},{9,13},{1... | collective-permute-start | bytes 663560 | tf_op jit(solution)/shard_map/ppermute | solution.py:319
  101.4 1.8 %collective-permute-start.6 = (bf16[288,384]{1,0:T(8,128)(2,1)S(1)}, bf16[288,384]{1,0:T(8,128)(2,1)S(1)}, u32[]{:S(2)}, u32[]{:S(2)}) collective-permute-start(bf16[288,384]{1,0:T(8,128)(2,1)S(1)} %get-tuple-element.21.refs_3_), channel_id=1, source_target_pairs={{0,12},{1,13},{2,14},{3,15},{4,0},{5,1},{6,2},{7,3},{8,4},{9,5},{1... | collective-permute-start | bytes 663560 | tf_op jit(solution)/shard_map/ppermute | solution.py:319
  103.2 1.8 %away.4 = (bf16[4,288,128]{2,1,0:T(8,128)(2,1)}, bf16[4,288,128]{2,1,0:T(8,128)(2,1)}, bf16[4,288,128]{2,1,0:T(8,128)(2,1)}) custom-call(bf16[288,384]{1,0:T(8,128)(2,1)S(1)} %get-tuple-element.25.refs_0_, bf16[288,384]{1,0:T(8,128)(2,1)S(1)} %collective-permute-done.14.refs_1_, bf16[288,384]{1,0:T(8,128)(2,1)S(1)} %collective-permute-done.15.refs_2_, ...), custom_call_target="tpu_custom_call" | custom-call | tf_op jit(solution)/shard_map/away/pallas_call | solution.py:228
  105.0 1.5 %collective-permute-start.16 = (bf16[4,288,128]{2,1,0:T(8,128)(2,1)}, bf16[4,288,128]{2,1,0:T(8,128)(2,1)}, u32[]{:S(2)}, u32[]{:S(2)}) collective-permute-start(bf16[4,288,128]{2,1,0:T(8,128)(2,1)} %get-tuple-element.26), channel_id=1, source_target_pairs={{0,2},{1,3},{2,0},{3,1},{4,6},{5,7},{6,4},{7,5},{8,10},{9,11},{10,... | collective-permute-start | bytes 884744 | tf_op jit(solution)/shard_map/ppermute | solution.py:323
  106.8 2.0 %away.5 = (bf16[1,288,128]{2,1,0:T(8,128)(2,1)S(1)}, bf16[1,288,128]{2,1,0:T(8,128)(2,1)}, bf16[1,288,128]{2,1,0:T(8,128)(2,1)}) custom-call(bf16[288,384]{1,0:T(8,128)(2,1)} %collective-permute-done.19.refs_0_, bf16[384,128]{1,0:T(8,128)(2,1)S(1)} %collective-permute-done.8.refs_3_.refs_4_.refs_1_, ...), custom_call_target="tpu_custom_call" | custom-call | tf_op jit(solution)/shard_map/away/pallas_call | solution.py:228
  109.5 2.8 %collective-permute-done.6.refs_1_ = bf16[288,384]{1,0:T(8,128)(2,1)S(1)} collective-permute-done((bf16[288,384]{1,0:T(8,128)(2,1)S(1)}, bf16[288,384]{1,0:T(8,128)(2,1)S(1)}, u32[]{:S(2)}, u32[]{:S(2)}) %collective-permute-start.6) | collective-permute-done | bytes 221216 | tf_op jit(solution)/shard_map/ppermute | solution.py:319
  112.3 9.5 %collective-permute-done.5.refs_0_ = bf16[288,384]{1,0:T(8,128)(2,1)S(1)} collective-permute-done((bf16[288,384]{1,0:T(8,128)(2,1)S(1)}, bf16[288,384]{1,0:T(8,128)(2,1)S(1)}, u32[]{:S(2)}, u32[]{:S(2)}) %collective-permute-start.5) | collective-permute-done | bytes 221216 | tf_op jit(solution)/shard_map/ppermute | solution.py:319
  123.7 1.5 %away.3 = (bf16[3,288,128]{2,1,0:T(8,128)(2,1)}, bf16[3,288,128]{2,1,0:T(8,128)(2,1)}, bf16[3,288,128]{2,1,0:T(8,128)(2,1)}) custom-call(bf16[288,384]{1,0:T(8,128)(2,1)S(1)} %collective-permute-done.5.refs_0_, bf16[288,384]{1,0:T(8,128)(2,1)S(1)} %collective-permute-done.6.refs_1_, bf16[288,384]{1,0:T(8,128)(2,1)S(1)} %collective-permute-done.7.refs_2_, ...), custom_call_target="tpu_custom_call" | custom-call | tf_op jit(solution)/shard_map/away/pallas_call | solution.py:228
  125.9 1.5 %collective-permute-start.13 = (bf16[3,288,128]{2,1,0:T(8,128)(2,1)}, bf16[3,288,128]{2,1,0:T(8,128)(2,1)}, u32[]{:S(2)}, u32[]{:S(2)}) collective-permute-start(bf16[3,288,128]{2,1,0:T(8,128)(2,1)} %get-tuple-element.24), channel_id=1, source_target_pairs={{0,2},{1,3},{2,0},{3,1},{4,6},{5,7},{6,4},{7,5},{8,10},{9,11},{10,... | collective-permute-start | bytes 663560 | tf_op jit(solution)/shard_map/ppermute | solution.py:323
  127.5 2.0 %pad_maximum_fusion = bf16[16,2,36,188]{3,2,1,0:T(8,128)(2,1)} fusion(bf16[8,2,36,188]{3,2,1,0:T(8,128)(2,1)} %copy-done.2, bf16[8,2,36,188]{3,2,1,0:T(8,128)(2,1)} %copy-done.1), kind=kLoop, calls=%fused_computation.4 | loop fusion | flops 216576 | bytes 866304 | tf_op jit(solution)/shard_map/concatenate | solution.py:363
  129.5 3.1 %reshape.103 = bf16[16,2,6768]{2,1,0:T(2,128)(2,1)} reshape(bf16[16,2,36,188]{3,2,1,0:T(8,128)(2,1)} %pad_maximum_fusion) | data formatting | bytes 866304 | tf_op jit(solution)/shard_map/reshape | solution.py:364
  132.6 2.6 %write.4.refs_6_ = f32[36,256,128]{2,1,0:T(8,128)} custom-call(s32[8]{0:T(128)S(1)} %stack.143.rows_ref, bf16[384,128]{1,0:T(8,128)(2,1)} %concatenate.6.refs_0_, bf16[1,288,384]{2,1,0:T(8,128)(2,1)S(1)} %bitcast.61, bf16[1,288,384]{2,1,0:T(8,128)(2,1)S(1)} %bitcast.63, bf16[1,288,384]{2,1,0:T(8,128)(2,1)S(1)} %bitcast.62, ...), custom_call_target="tpu_custom_call" | custom-call | tf_op jit(solution)/shard_map/write/pallas_call | solution.py:281
  135.2 2.6 %write.5.refs_2_ = f32[36,256,128]{2,1,0:T(8,128)} custom-call(s32[15]{0:T(128)S(1)} %stack.134.rows_ref, bf16[4,288,128]{2,1,0:T(8,128)(2,1)} %collective-permute-done.16.refs_0_, bf16[4,288,128]{2,1,0:T(8,128)(2,1)} %collective-permute-done.17.refs_1_, bf16[4,288,128]{2,1,0:T(8,128)(2,1)} %collective-permute-done.18.refs_2_, ...), custom_call_target="tpu_custom_call", output_to_operand_aliasing={{}: (7, {})} | custom-call | tf_op jit(solution)/shard_map/write/pallas_call | solution.py:281
  137.9 3.0 %collective-permute-done.13.refs_1_ = bf16[3,288,128]{2,1,0:T(8,128)(2,1)} collective-permute-done((bf16[3,288,128]{2,1,0:T(8,128)(2,1)}, bf16[3,288,128]{2,1,0:T(8,128)(2,1)}, u32[]{:S(2)}, u32[]{:S(2)}) %collective-permute-start.13) | collective-permute-done | bytes 221216 | tf_op jit(solution)/shard_map/ppermute | solution.py:323
  140.9 1.9 %write.6.refs_1_ = f32[36,256,128]{2,1,0:T(8,128)} custom-call(s32[6]{0:T(128)S(1)} %stack.118.rows_ref, bf16[3,288,128]{2,1,0:T(8,128)(2,1)S(1)} %collective-permute-done.12.refs_0_, bf16[3,288,128]{2,1,0:T(8,128)(2,1)} %collective-permute-done.13.refs_1_, f32[36,256,128]{2,1,0:T(8,128)} %write.5.refs_2_), custom_call_target="tpu_custom_call", output_to_operand_aliasing={{}: (3, {})} | custom-call | tf_op jit(solution)/shard_map/write/pallas_call | solution.py:281
  142.8 1.7 %write.7 = f32[36,256,128]{2,1,0:T(8,128)} custom-call(s32[3]{0:T(128)S(1)} %pad_add_fusion.rows_ref, bf16[3,288,128]{2,1,0:T(8,128)(2,1)} %collective-permute-done.11.refs_0_, f32[36,256,128]{2,1,0:T(8,128)} %write.6.refs_1_), custom_call_target="tpu_custom_call", output_to_operand_aliasing={{}: (2, {})} | custom-call | tf_op jit(solution)/shard_map/write/pallas_call | solution.py:281
  (81 shorter events, 15.8 us)
Async XLA Ops:
  7.5 12.7 %copy-start.14 = (s32[36]{0:T(128)S(1)}, s32[36]{0:T(128)}, u32[]{:S(2)}) copy-start(s32[36]{0:T(128)} %param.6) | copy-start | bytes 436
  7.5 26.2 %all-to-all-start = ((bf16[16,8,8,384]{3,2,1,0:T(8,128)(2,1)}), bf16[16,8,8,384]{3,2,1,0:T(8,128)(2,1)S(1)}, u32[]{:S(2)}, u32[]{:S(2)}) async-start(bf16[16,8,8,384]{3,2,1,0:T(8,128)(2,1)} %slice.46), calls=%async_computation | async-start | bytes 1572864 | tf_op jit(solution)/shard_map/all_to_all | solution.py:355
  21.3 1.3 collective-permute-start
  22.6 4.3 %collective-permute-start.1 = (bf16[36,384]{1,0:T(8,128)(2,1)S(1)}, bf16[36,384]{1,0:T(8,128)(2,1)S(1)}, u32[]{:S(2)}, u32[]{:S(2)}) collective-permute-start(bf16[36,384]{1,0:T(8,128)(2,1)S(1)} %add.131), channel_id=1, source_target_pairs={{0,2},{1,3},{2,0},{3,1},{4,6},{5,7},{6,4},{7,5},{8,10},{9,11},{10,... | collective-permute-start | bytes 82952 | tf_op jit(solution)/shard_map/ppermute | solution.py:323
  27.0 35.3 %copy-start.3 = (bf16[36,384]{1,0:T(8,128)(2,1)}, bf16[36,384]{1,0:T(8,128)(2,1)S(1)}, u32[]{:S(2)}) copy-start(bf16[36,384]{1,0:T(8,128)(2,1)S(1)} %add.132.refs_0_) | copy-start | bytes 82948
  27.0 35.3 %copy-start.11 = (s32[8]{0:T(128)S(1)}, s32[8]{0:T(128)}, u32[]{:S(2)}) copy-start(s32[8]{0:T(128)} %starts_ref.3) | copy-start | bytes 100
  33.7 51.3 %all-to-all-start.1 = ((bf16[16,8,8,384]{3,2,1,0:T(8,128)(2,1)}), bf16[16,8,8,384]{3,2,1,0:T(8,128)(2,1)S(1)}, u32[]{:S(2)}, u32[]{:S(2)}) async-start(bf16[16,8,8,384]{3,2,1,0:T(8,128)(2,1)} %slice.45), calls=%async_computation.1 | async-start | bytes 1572864 | tf_op jit(solution)/shard_map/all_to_all | solution.py:355
  39.1 23.2 %collective-permute-start.4 = (bf16[36,384]{1,0:T(8,128)(2,1)S(1)}, bf16[36,384]{1,0:T(8,128)(2,1)S(1)}, u32[]{:S(2)}, u32[]{:S(2)}) collective-permute-start(bf16[36,384]{1,0:T(8,128)(2,1)S(1)} %add.132.refs_0_), channel_id=1, source_target_pairs={{0,8},{1,9},{2,10},{3,11},{4,12},{5,13},{6,14},{7,15},{8,0},{9,1},... | collective-permute-start | bytes 82952 | tf_op jit(solution)/shard_map/ppermute | solution.py:319
  41.9 20.4 %collective-permute-start.3 = (bf16[36,384]{1,0:T(8,128)(2,1)S(1)}, bf16[36,384]{1,0:T(8,128)(2,1)S(1)}, u32[]{:S(2)}, u32[]{:S(2)}) collective-permute-start(bf16[36,384]{1,0:T(8,128)(2,1)S(1)} %add.132.refs_0_), channel_id=1, source_target_pairs={{0,12},{1,13},{2,14},{3,15},{4,0},{5,1},{6,2},{7,3},{8,4},{9,5},{1... | collective-permute-start | bytes 82952 | tf_op jit(solution)/shard_map/ppermute | solution.py:319
  43.4 18.9 %collective-permute-start.2 = (bf16[36,384]{1,0:T(8,128)(2,1)S(1)}, bf16[36,384]{1,0:T(8,128)(2,1)S(1)}, u32[]{:S(2)}, u32[]{:S(2)}) collective-permute-start(bf16[36,384]{1,0:T(8,128)(2,1)S(1)} %add.132.refs_0_), channel_id=1, source_target_pairs={{0,4},{1,5},{2,6},{3,7},{4,8},{5,9},{6,10},{7,11},{8,12},{9,13},{1... | collective-permute-start | bytes 82952 | tf_op jit(solution)/shard_map/ppermute | solution.py:319
  62.3 22.6 %copy-start.5 = (bf16[36,384]{1,0:T(8,128)(2,1)}, bf16[36,384]{1,0:T(8,128)(2,1)S(1)}, u32[]{:S(2)}) copy-start(bf16[36,384]{1,0:T(8,128)(2,1)S(1)} %collective-permute-done.4.refs_3_) | copy-start | bytes 82948
  62.3 22.6 %copy-start.7 = (bf16[36,384]{1,0:T(8,128)(2,1)}, bf16[36,384]{1,0:T(8,128)(2,1)S(1)}, u32[]{:S(2)}) copy-start(bf16[36,384]{1,0:T(8,128)(2,1)S(1)} %collective-permute-done.3.refs_2_) | copy-start | bytes 82948
  62.3 22.6 %copy-start.9 = (bf16[36,384]{1,0:T(8,128)(2,1)}, bf16[36,384]{1,0:T(8,128)(2,1)S(1)}, u32[]{:S(2)}) copy-start(bf16[36,384]{1,0:T(8,128)(2,1)S(1)} %collective-permute-done.2.refs_1_) | copy-start | bytes 82948
  73.0 12.0 %copy-start.1 = (bf16[8,2,36,188]{3,2,1,0:T(8,128)(2,1)}, bf16[8,2,36,188]{3,2,1,0:T(8,128)(2,1)S(1)}, u32[]{:S(2)}) copy-start(bf16[8,2,36,188]{3,2,1,0:T(8,128)(2,1)S(1)} %get-tuple-element.18) | copy-start | bytes 649732
  73.0 12.0 %collective-permute-start.15 = (bf16[288,384]{1,0:T(8,128)(2,1)S(1)}, bf16[288,384]{1,0:T(8,128)(2,1)S(1)}, u32[]{:S(2)}, u32[]{:S(2)}) collective-permute-start(bf16[288,384]{1,0:T(8,128)(2,1)S(1)} %get-tuple-element.25.refs_0_), channel_id=1, source_target_pairs={{0,8},{1,9},{2,10},{3,11},{4,12},{5,13},{6,14},{7,15},{8,0},{9,1},... | collective-permute-start | bytes 663560 | tf_op jit(solution)/shard_map/ppermute | solution.py:323
  73.9 29.4 %collective-permute-start.14 = (bf16[288,384]{1,0:T(8,128)(2,1)S(1)}, bf16[288,384]{1,0:T(8,128)(2,1)S(1)}, u32[]{:S(2)}, u32[]{:S(2)}) collective-permute-start(bf16[288,384]{1,0:T(8,128)(2,1)S(1)} %get-tuple-element.25.refs_0_), channel_id=1, source_target_pairs={{0,4},{1,5},{2,6},{3,7},{4,0},{5,1},{6,2},{7,3},{8,12},{9,13},{10,... | collective-permute-start | bytes 663560 | tf_op jit(solution)/shard_map/ppermute | solution.py:323
  75.0 24.3 %collective-permute-start.10 = (bf16[384,128]{1,0:T(8,128)(2,1)}, bf16[384,128]{1,0:T(8,128)(2,1)S(1)}, u32[]{:S(2)}, u32[]{:S(2)}) collective-permute-start(bf16[384,128]{1,0:T(8,128)(2,1)} %concatenate.6.refs_0_), channel_id=1, source_target_pairs={{0,1},{1,0},{2,3},{3,2},{4,5},{5,4},{6,7},{7,6},{8,9},{9,8},{10,11... | collective-permute-start | bytes 294920 | tf_op jit(solution)/shard_map/ppermute | solution.py:323
  75.1 26.4 %collective-permute-start.9 = (bf16[384,128]{1,0:T(8,128)(2,1)}, bf16[384,128]{1,0:T(8,128)(2,1)S(1)}, u32[]{:S(2)}, u32[]{:S(2)}) collective-permute-start(bf16[384,128]{1,0:T(8,128)(2,1)} %concatenate.6.refs_0_), channel_id=1, source_target_pairs={{0,3},{1,2},{2,1},{3,0},{4,7},{5,6},{6,5},{7,4},{8,11},{9,10},{10,... | collective-permute-start | bytes 294920 | tf_op jit(solution)/shard_map/ppermute | solution.py:323
  76.6 26.6 %collective-permute-start.8 = (bf16[384,128]{1,0:T(8,128)(2,1)}, bf16[384,128]{1,0:T(8,128)(2,1)S(1)}, u32[]{:S(2)}, u32[]{:S(2)}) collective-permute-start(bf16[384,128]{1,0:T(8,128)(2,1)} %concatenate.6.refs_0_), channel_id=1, source_target_pairs={{0,2},{1,3},{2,0},{3,1},{4,6},{5,7},{6,4},{7,5},{8,10},{9,11},{10,... | collective-permute-start | bytes 294920 | tf_op jit(solution)/shard_map/ppermute | solution.py:323
  84.9 21.9 %collective-permute-start.19 = (bf16[288,384]{1,0:T(8,128)(2,1)S(1)}, bf16[288,384]{1,0:T(8,128)(2,1)}, u32[]{:S(2)}, u32[]{:S(2)}) collective-permute-start(bf16[288,384]{1,0:T(8,128)(2,1)S(1)} %collective-permute-done.15.refs_2_), channel_id=1, source_target_pairs={{0,4},{1,5},{2,6},{3,7},{4,0},{5,1},{6,2},{7,3},{8,12},{9,13},{10,... | collective-permute-start | bytes 663560 | tf_op jit(solution)/shard_map/ppermute | solution.py:323
  99.3 10.2 %collective-permute-start.7 = (bf16[288,384]{1,0:T(8,128)(2,1)S(1)}, bf16[288,384]{1,0:T(8,128)(2,1)S(1)}, u32[]{:S(2)}, u32[]{:S(2)}) collective-permute-start(bf16[288,384]{1,0:T(8,128)(2,1)S(1)} %get-tuple-element.21.refs_3_), channel_id=1, source_target_pairs={{0,4},{1,5},{2,6},{3,7},{4,8},{5,9},{6,10},{7,11},{8,12},{9,13},{1... | collective-permute-start | bytes 663560 | tf_op jit(solution)/shard_map/ppermute | solution.py:319
  101.4 10.9 %collective-permute-start.6 = (bf16[288,384]{1,0:T(8,128)(2,1)S(1)}, bf16[288,384]{1,0:T(8,128)(2,1)S(1)}, u32[]{:S(2)}, u32[]{:S(2)}) collective-permute-start(bf16[288,384]{1,0:T(8,128)(2,1)S(1)} %get-tuple-element.21.refs_3_), channel_id=1, source_target_pairs={{0,12},{1,13},{2,14},{3,15},{4,0},{5,1},{6,2},{7,3},{8,4},{9,5},{1... | collective-permute-start | bytes 663560 | tf_op jit(solution)/shard_map/ppermute | solution.py:319
  105.0 20.8 %collective-permute-start.16 = (bf16[4,288,128]{2,1,0:T(8,128)(2,1)}, bf16[4,288,128]{2,1,0:T(8,128)(2,1)}, u32[]{:S(2)}, u32[]{:S(2)}) collective-permute-start(bf16[4,288,128]{2,1,0:T(8,128)(2,1)} %get-tuple-element.26), channel_id=1, source_target_pairs={{0,2},{1,3},{2,0},{3,1},{4,6},{5,7},{6,4},{7,5},{8,10},{9,11},{10,... | collective-permute-start | bytes 884744 | tf_op jit(solution)/shard_map/ppermute | solution.py:323
  106.5 15.3 %collective-permute-start.5 = (bf16[288,384]{1,0:T(8,128)(2,1)S(1)}, bf16[288,384]{1,0:T(8,128)(2,1)S(1)}, u32[]{:S(2)}, u32[]{:S(2)}) collective-permute-start(bf16[288,384]{1,0:T(8,128)(2,1)S(1)} %get-tuple-element.21.refs_3_), channel_id=1, source_target_pairs={{0,8},{1,9},{2,10},{3,11},{4,12},{5,13},{6,14},{7,15},{8,0},{9,1},... | collective-permute-start | bytes 663560 | tf_op jit(solution)/shard_map/ppermute | solution.py:319
  108.8 13.9 %collective-permute-start.20 = (bf16[1,288,128]{2,1,0:T(8,128)(2,1)S(1)}, bf16[1,288,128]{2,1,0:T(8,128)(2,1)S(1)}, u32[]{:S(2)}, u32[]{:S(2)}) collective-permute-start(bf16[1,288,128]{2,1,0:T(8,128)(2,1)S(1)} %get-tuple-element.29), channel_id=1, source_target_pairs={{0,2},{1,3},{2,0},{3,1},{4,6},{5,7},{6,4},{7,5},{8,10},{9,11},{10,... | collective-permute-start | bytes 221192 | tf_op jit(solution)/shard_map/ppermute | solution.py:323
  109.5 15.7 %collective-permute-start.21 = (bf16[1,288,128]{2,1,0:T(8,128)(2,1)}, bf16[1,288,128]{2,1,0:T(8,128)(2,1)S(1)}, u32[]{:S(2)}, u32[]{:S(2)}) collective-permute-start(bf16[1,288,128]{2,1,0:T(8,128)(2,1)} %get-tuple-element.30), channel_id=1, source_target_pairs={{0,3},{1,2},{2,1},{3,0},{4,7},{5,6},{6,5},{7,4},{8,11},{9,10},{10,... | collective-permute-start | bytes 221192 | tf_op jit(solution)/shard_map/ppermute | solution.py:323
  112.3 13.1 %collective-permute-start.22 = (bf16[1,288,128]{2,1,0:T(8,128)(2,1)}, bf16[1,288,128]{2,1,0:T(8,128)(2,1)}, u32[]{:S(2)}, u32[]{:S(2)}) collective-permute-start(bf16[1,288,128]{2,1,0:T(8,128)(2,1)} %get-tuple-element.31), channel_id=1, source_target_pairs={{0,1},{1,0},{2,3},{3,2},{4,5},{5,4},{6,7},{7,6},{8,9},{9,8},{10,11... | collective-permute-start | bytes 221192 | tf_op jit(solution)/shard_map/ppermute | solution.py:323
  121.8 13.4 %collective-permute-start.17 = (bf16[4,288,128]{2,1,0:T(8,128)(2,1)}, bf16[4,288,128]{2,1,0:T(8,128)(2,1)}, u32[]{:S(2)}, u32[]{:S(2)}) collective-permute-start(bf16[4,288,128]{2,1,0:T(8,128)(2,1)} %get-tuple-element.27), channel_id=1, source_target_pairs={{0,3},{1,2},{2,1},{3,0},{4,7},{5,6},{6,5},{7,4},{8,11},{9,10},{10,... | collective-permute-start | bytes 884744 | tf_op jit(solution)/shard_map/ppermute | solution.py:323
  122.7 12.5 %collective-permute-start.18 = (bf16[4,288,128]{2,1,0:T(8,128)(2,1)}, bf16[4,288,128]{2,1,0:T(8,128)(2,1)}, u32[]{:S(2)}, u32[]{:S(2)}) collective-permute-start(bf16[4,288,128]{2,1,0:T(8,128)(2,1)} %get-tuple-element.28), channel_id=1, source_target_pairs={{0,1},{1,0},{2,3},{3,2},{4,5},{5,4},{6,7},{7,6},{8,9},{9,8},{10,11... | collective-permute-start | bytes 884744 | tf_op jit(solution)/shard_map/ppermute | solution.py:323
  125.2 17.6 %collective-permute-start.11 = (bf16[3,288,128]{2,1,0:T(8,128)(2,1)}, bf16[3,288,128]{2,1,0:T(8,128)(2,1)}, u32[]{:S(2)}, u32[]{:S(2)}) collective-permute-start(bf16[3,288,128]{2,1,0:T(8,128)(2,1)} %get-tuple-element.22), channel_id=1, source_target_pairs={{0,3},{1,2},{2,1},{3,0},{4,7},{5,6},{6,5},{7,4},{8,11},{9,10},{10,... | collective-permute-start | bytes 663560 | tf_op jit(solution)/shard_map/ppermute | solution.py:323
  125.4 12.5 %collective-permute-start.12 = (bf16[3,288,128]{2,1,0:T(8,128)(2,1)}, bf16[3,288,128]{2,1,0:T(8,128)(2,1)S(1)}, u32[]{:S(2)}, u32[]{:S(2)}) collective-permute-start(bf16[3,288,128]{2,1,0:T(8,128)(2,1)} %get-tuple-element.23), channel_id=1, source_target_pairs={{0,1},{1,0},{2,3},{3,2},{4,5},{5,4},{6,7},{7,6},{8,9},{9,8},{10,11... | collective-permute-start | bytes 663560 | tf_op jit(solution)/shard_map/ppermute | solution.py:323
  125.9 15.0 %collective-permute-start.13 = (bf16[3,288,128]{2,1,0:T(8,128)(2,1)}, bf16[3,288,128]{2,1,0:T(8,128)(2,1)}, u32[]{:S(2)}, u32[]{:S(2)}) collective-permute-start(bf16[3,288,128]{2,1,0:T(8,128)(2,1)} %get-tuple-element.24), channel_id=1, source_target_pairs={{0,2},{1,3},{2,0},{3,1},{4,6},{5,7},{6,4},{7,5},{8,10},{9,11},{10,... | collective-permute-start | bytes 663560 | tf_op jit(solution)/shard_map/ppermute | solution.py:323
  (8 other events, 20.5 us)
